TPU v7x, 128 devices: a whole 4x4x4 slice. The times are simulated.
128 devices in a mesh: rep: 32 (over z, y, core), tensor: 4 (over x).
Axes of the slice: x: 4, y: 4, z: 4, core: 2. Of those that a mesh axis runs over, the one named last changes fastest.
Arguments:
- hidden_in: bfloat16 [2048, 4096], P('rep', 'tensor'), may hold values from -25 to 25
- query: bfloat16 [2048, 4096], P('rep', 'tensor'), may hold values from -6 to 6
- new_kv: bfloat16 [2048, 2, 512], P('rep', None, 'tensor'), may hold values from -8 to 8
- pool: bfloat16 [4096, 128, 2, 512], P('rep', None, None, 'tensor'), may hold values from -8 to 8
- page_table: int32 [2048, 2], P('rep'), may hold values from 0 to 127, as said below
- lengths: int32 [2048], replicated, may hold values from 1 to 256, 262144 in all
- dest: int32 [32], replicated, may hold values from 0 to 31, each once
- out_weight: bfloat16 [4096, 4096], P('tensor'), may hold values from -0.1875 to 0.1875
- norm_gain: float32 [4096], P('tensor'), may hold values from 0.1 to 1.9
- gate_up: bfloat16 [4096, 2, 11008], P('tensor', None, 'rep'), may hold values from -0.09375 to 0.09375
- down_weight: bfloat16 [11008, 4096], P('rep', 'tensor'), may hold values from -0.109375 to 0.109375
Outputs:
- layer_out: bfloat16 [2048, 4096], P('rep', 'tensor')
Inputs may be any that keep to these rules, and one draw needn't show every extreme that they name: `page_table`: within a group no two requests share a page.
All inputs are finite; a program needn't handle non-finite values.
Results may differ from a plain program's by a relative error of at most 0.03.
Values may be sent and summed in bfloat16 or wider, within the bound.
No kernel may reach another device: no remote copies, remote signals or barrier semaphores. Data moves between devices by JAX's collectives and lax.ppermute only.
A program may use at most 128 MiB of HBM per device.

v0:
```python
import jax
import jax.numpy as jnp
from jax import lax
from jax.sharding import PartitionSpec as P

D = 4096
HD = 128


EPSILON = 1e-05


def attend(queries, cache_block, new_pair, counts):
    row_count = cache_block.shape[0]
    cache_len = cache_block.shape[1]
    kv_width = cache_block.shape[3]
    kv_heads = kv_width // HD
    group_size = queries.shape[1] // kv_width
    query_heads = queries.reshape(row_count, kv_heads, group_size, HD)
    key_heads = cache_block[:, :, 0].reshape(row_count, cache_len, kv_heads, HD)
    value_heads = cache_block[:, :, 1].reshape(row_count, cache_len, kv_heads, HD)
    new_key = new_pair[:, 0].reshape(row_count, kv_heads, HD)
    new_value = new_pair[:, 1].reshape(row_count, kv_heads, HD)
    score_scale = HD ** (-0.5)
    scores = (
        jnp.einsum("nkgd,nlkd->nkgl", query_heads, key_heads, preferred_element_type=jnp.float32)
        * score_scale
    )
    own_score = (
        jnp.einsum("nkgd,nkd->nkg", query_heads, new_key, preferred_element_type=jnp.float32)
        * score_scale
    )
    in_range = (jnp.arange(cache_len, dtype=jnp.int32)[None, :] < counts[:, None])[:, None, None, :]
    masked = jnp.where(in_range, scores, -jnp.inf)
    peak_score = jnp.maximum(jnp.max(masked, axis=-1), own_score)
    weights = jnp.where(in_range, jnp.exp(scores - peak_score[..., None]), 0.0)
    own_weight = jnp.exp(own_score - peak_score)
    denominator = jnp.sum(weights, axis=-1) + own_weight
    weighted = jnp.einsum(
        "nkgl,nlkd->nkgd",
        weights.astype(jnp.bfloat16),
        value_heads,
        preferred_element_type=jnp.float32,
    )
    weighted = weighted + jnp.einsum(
        "nkg,nkd->nkgd",
        own_weight.astype(jnp.bfloat16),
        new_value,
        preferred_element_type=jnp.float32,
    )
    return (weighted / denominator[..., None]).astype(jnp.bfloat16).reshape(row_count, -1)


def local(
    hidden_in,
    query,
    new_kv,
    pool,
    page_table,
    lengths,
    dest,
    out_weight,
    norm_gain,
    gate_up,
    down_weight,
):
    rows_here = hidden_in.shape[0]
    group_count = lax.axis_size("rep")
    my_group = lax.axis_index("rep")
    group_ids = jnp.arange(group_count, dtype=jnp.int32)
    source = jnp.sum(jnp.where(dest == my_group, group_ids, 0))
    page_count = page_table.shape[1]
    page_len = pool.shape[1]
    kv_width = pool.shape[3]
    cache_rows = pool[page_table].reshape(rows_here, page_count * page_len, 2, kv_width)
    my_lengths = lax.dynamic_slice_in_dim(lengths, my_group * rows_here, rows_here)
    home_attn = attend(query, cache_rows, new_kv, my_lengths)
    every_attn, every_hidden = (
        lax.all_gather(home_attn[-1:], "rep", axis=0, tiled=True),
        lax.all_gather(hidden_in[-1:], "rep", axis=0, tiled=True),
    )
    attention = jnp.concatenate(
        [home_attn[:-1], lax.dynamic_slice_in_dim(every_attn, source, 1)], axis=0
    )
    served = jnp.concatenate(
        [hidden_in[:-1], lax.dynamic_slice_in_dim(every_hidden, source, 1)], axis=0
    )
    projected = jnp.dot(attention, out_weight, preferred_element_type=jnp.float32)
    head_total = lax.psum_scatter(
        projected.astype(jnp.bfloat16), "tensor", scatter_dimension=1, tiled=True
    ).astype(jnp.float32)
    residual = served.astype(jnp.float32) + head_total
    square_sum = lax.psum(jnp.sum(residual * residual, axis=1), "tensor")
    normed = (residual * lax.rsqrt(square_sum / D + EPSILON)[:, None] * norm_gain[None, :]).astype(
        jnp.bfloat16
    )
    unit_count = gate_up.shape[2]
    flat_weight = gate_up.reshape(gate_up.shape[0], 2 * unit_count)
    partial_units = jnp.dot(
        lax.all_gather(normed, "rep", axis=0, tiled=True),
        flat_weight,
        preferred_element_type=jnp.float32,
    )
    partial_units = partial_units.reshape(partial_units.shape[0], 2, unit_count)
    unit_total = lax.psum(partial_units.astype(jnp.bfloat16), "tensor").astype(jnp.float32)
    activated = (jax.nn.silu(unit_total[:, 0]) * unit_total[:, 1]).astype(jnp.bfloat16)
    mixed = lax.psum_scatter(
        jnp.dot(activated, down_weight, preferred_element_type=jnp.float32).astype(jnp.bfloat16),
        "rep",
        scatter_dimension=0,
        tiled=True,
    ).astype(jnp.float32)
    return (residual + mixed).astype(jnp.bfloat16)


def solution(mesh):
    return jax.shard_map(
        local,
        mesh=mesh,
        in_specs=(
            P("rep", "tensor"),
            P("rep", "tensor"),
            P("rep", None, "tensor"),
            P("rep", None, None, "tensor"),
            P("rep", None),
            P(),
            P(),
            P("tensor", None),
            P("tensor"),
            P("tensor", None, "rep"),
            P("rep", "tensor"),
        ),
        out_specs=P("rep", "tensor"),
        check_vma=False,
    )
```

profile of v0, /device:TPU:0, one launch (start us, length us, event | category | flops | bytes accessed | tf_op | source)
XLA Modules:
  0.0 336.0 jit_solution(7279921076718886438)
XLA Ops:
  6.5 0.0 copy-start
  6.5 0.0 reduce-scatter.3.cloned.1.call-start
  6.5 0.8 compare_select_fusion
  7.3 0.1 copy.17
  7.4 0.1 reshape.104
  7.6 23.2 %gather_fusion = bf16[128,128,2,128]{3,2,1,0:T(2,128)(2,1)} fusion(bf16[128,128,2,128]{3,2,1,0:T(2,128)(2,1)} %param.14, s32[1024]{0:T(1024)S(1)} %pad_clamp_fusion), kind=kCustom, calls=%fused_computation | custom fusion | bytes 16777728 | tf_op jit(solution)/shard_map/gather | solution.py:75
  30.8 0.0 copy-start.3
  30.8 0.0 copy-start.4
  30.8 8.9 %copy.18 = bf16[128,128,2,128]{3,1,0,2:T(8,128)(2,1)} copy(bf16[128,128,2,128]{3,2,1,0:T(2,128)(2,1)} %gather_fusion) | data formatting | bytes 16777216 | tf_op jit(solution)/shard_map/gather | solution.py:75
  39.7 0.8 dynamic_slice.10
  40.4 0.1 iota_compare_fusion
  40.5 0.0 copy-done.3
  40.5 0.0 copy-done.4
  40.6 0.2 fusion.22
  40.8 3.5 %select_reduce_fusion = (f32[64,8]{1,0:T(8,128)S(1)}, f32[64,256,8]{1,2,0:T(8,128)S(1)}) fusion(pred[64,256]{1,0:T(8,128)(4,1)S(1)} %iota_compare_fusion, bf16[64,8,128]{2,1,0:T(8,128)(2,1)S(1)} %bitcast.79, bf16[64,256,2,128]{3,1,0,2:T(8,128)(2,1)} %bitcast.68), kind=kOutput, calls=%fused_computation.23 | convolution fusion | flops 33947136 | bytes 4868096 | tf_op jit(solution)/shard_map/nkgd,nlkd->nkgl/dot_general | solution.py:26
  44.3 0.0 copy-start.7
  44.3 0.3 bitcast_reduce_fusion
  44.6 2.9 fusion.15
  47.5 26.2 %all-gather.1 = bf16[32,1,1024]{2,1,0:T(2,128)(2,1)S(1)} all-gather(bf16[1,1,1024]{2,1,0:T(2,128)(2,1)S(1)} %reshape.115), channel_id=1, replica_groups=mesh['rep'=32,'tensor'=4] {'rep'}, dimensions={0}, use_global_device_ids=true | all-gather | bytes 67584 | tf_op jit(solution)/shard_map/all_gather | solution.py:79
  73.7 0.0 copy-done.7
  73.7 0.6 fusion.25
  76.4 0.0 copy-start.1
  76.4 0.0 copy-start.5
  76.4 5.8 %convolution_convert_fusion = bf16[64,4096]{1,0:T(8,128)(2,1)} fusion(bf16[1024,4096]{1,0:T(8,128)(2,1)} %param.18, bf16[1,1024]{1,0:T(2,128)(2,1)S(1)} %dynamic-slice_bitcast_fusion, bf16[63,1024]{1,0:T(8,128)(2,1)S(1)} %bitcast.73), kind=kOutput, calls=%fused_computation.1 | convolution fusion | flops 537395200 | bytes 9043968 | tf_op jit(solution)/shard_map/dot_general | solution.py:88
  82.2 0.0 reduce-scatter.3.cloned.1.call-update
  82.2 0.0 all-gather.4.cloned.1.call-start
  82.2 0.0 copy-done.1
  82.3 24.0 %all-gather = bf16[32,1,1024]{2,1,0:T(2,128)(2,1)S(1)} all-gather(bf16[1,1,1024]{2,1,0:T(2,128)(2,1)S(1)} %slice_bitcast_fusion.14), channel_id=1, replica_groups=mesh['rep'=32,'tensor'=4] {'rep'}, dimensions={0}, use_global_device_ids=true | all-gather | bytes 67584 | tf_op jit(solution)/shard_map/all_gather | solution.py:80
  106.3 1.1 multiply_reduce_fusion
  107.4 10.5 %psum.14 = f32[64]{0:T(128)S(1)} all-reduce(f32[64]{0:T(128)S(1)} %multiply_reduce_fusion), channel_id=1, replica_groups=mesh['rep'=32,'tensor'=4] {'tensor'}, use_global_device_ids=true, to_apply=%region_5.6 | all-reduce | flops 64 | bytes 512 | tf_op jit(solution)/shard_map/psum | solution.py:93
  117.9 0.0 copy-done.5
  117.9 1.7 multiply_convert_fusion
  119.6 0.0 all-gather.4.cloned.1.call-update
  119.6 0.0 all-reduce.2.cloned.1.call-start
  119.6 42.7 %all-gather.4.cloned.1.call-done = bf16[2048,1024]{1,0:T(8,128)(2,1)} async-done(((bf16[64,1024]{1,0:T(8,128)(2,1)}), bf16[2048,1024]{1,0:T(8,128)(2,1)}) %all-gather.4.cloned.1.call-update) | async-done | bytes 4194320 | tf_op jit(solution)/shard_map/all_gather | solution.py:100
  162.3 0.0 copy-done
  162.3 6.7 %fusion.4 = bf16[2048,2,344]{0,2,1:T(8,128)(2,1)} fusion(bf16[2048,1024]{1,0:T(8,128)(2,1)} %all-gather.4.cloned.1.call-done, bf16[1024,2,344]{0,2,1:T(8,128)(2,1)S(1)} %copy-done), kind=kOutput, calls=%fused_computation.9 | convolution fusion | flops 2887090176 | bytes 8421376 | tf_op jit(solution)/shard_map/dot_general | solution.py:99
  169.0 0.0 all-reduce.2.cloned.1.call-update
  169.0 0.0 copy-start.6
  169.0 0.2 reduce-scatter.5.cloned.1.call-start
  169.3 69.5 %all-reduce.2.cloned.1.call-done = bf16[2048,2,344]{0,2,1:T(8,128)(2,1)} async-done(((bf16[2048,2,344]{0,2,1:T(8,128)(2,1)}), bf16[2048,2,344]{0,2,1:T(8,128)(2,1)}) %all-reduce.2.cloned.1.call-update) | async-done | bytes 2818064 | tf_op jit(solution)/shard_map/psum | solution.py:105
  238.8 2.5 convert_element_type.50
  241.3 0.0 copy-done.6
  241.3 4.4 %convolution_convert_fusion.1 = bf16[2048,1024]{1,0:T(8,128)(2,1)} fusion(bf16[344,1024]{1,0:T(8,128)(2,1)S(1)} %copy-done.6, f32[2048,2,344]{0,2,1:T(8,128)S(1)} %convert_element_type.50), kind=kOutput, calls=%fused_computation.8 | convolution fusion | flops 1449164800 | bytes 10534912 | tf_op jit(solution)/shard_map/dot_general | solution.py:108
  245.8 0.0 reduce-scatter.5.cloned.1.call-update
  245.8 82.1 %reduce-scatter.5.cloned.1.call-done = bf16[64,1024]{1,0:T(8,128)(2,1)} async-done(((bf16[2048,1024]{1,0:T(8,128)(2,1)}), bf16[64,1024]{1,0:T(8,128)(2,1)}) %reduce-scatter.5.cloned.1.call-update) | async-done | bytes 131088 | tf_op jit(solution)/shard_map/reduce_scatter | solution.py:107
  327.9 0.0 copy-done.2
  327.9 1.6 add_convert_fusion
  (17 shorter events, 0.2 us)
Async XLA Ops:
  6.5 155.8 %copy-start = (bf16[1024,2,344]{0,2,1:T(8,128)(2,1)S(1)}, bf16[1024,2,344]{0,2,1:T(8,128)(2,1)}, u32[]{:S(2)}) copy-start(bf16[1024,2,344]{0,2,1:T(8,128)(2,1)} %param.20) | copy-start | bytes 4227076
  6.5 99.8 %reduce-scatter.3.cloned.1.call-start = ((), (), s32[]{:S(2)}) async-start(), calls=%async_computation.2 | async-start | bytes 655360 | tf_op jit(solution)/shard_map/reduce_scatter | solution.py:89
  30.8 9.7 %copy-start.3 = (bf16[64,1024]{1,0:T(8,128)(2,1)S(1)}, bf16[64,1024]{1,0:T(8,128)(2,1)}, u32[]{:S(2)}) copy-start(bf16[64,1024]{1,0:T(8,128)(2,1)} %param.12) | copy-start | bytes 393220
  30.8 9.8 %copy-start.4 = (bf16[64,2,128]{2,1,0:T(2,128)(2,1)S(1)}, bf16[64,2,128]{2,1,0:T(2,128)(2,1)}, u32[]{:S(2)}) copy-start(bf16[64,2,128]{2,1,0:T(2,128)(2,1)} %param.13) | copy-start | bytes 98308
  44.3 29.4 %copy-start.7 = (s32[32]{0:T(128)S(1)}, s32[32]{0:T(128)}, u32[]{:S(2)}) copy-start(s32[32]{0:T(128)} %param.17) | copy-start | bytes 388
  76.4 5.9 %copy-start.1 = (bf16[64,1024]{1,0:T(8,128)(2,1)S(1)}, bf16[64,1024]{1,0:T(8,128)(2,1)}, u32[]{:S(2)}) copy-start(bf16[64,1024]{1,0:T(8,128)(2,1)} %param.11) | copy-start | bytes 393220
  76.4 41.5 %copy-start.5 = (f32[1024]{0:T(1024)S(1)}, f32[1024]{0:T(1024)}, u32[]{:S(2)}) copy-start(f32[1024]{0:T(1024)} %param.19) | copy-start | bytes 12292
  82.2 80.1 %all-gather.4.cloned.1.call-start = ((), (), s32[]{:S(2)}) async-start(), calls=%async_computation.3 | async-start | bytes 4325376 | tf_op jit(solution)/shard_map/all_gather | solution.py:100
  119.6 119.2 %all-reduce.2.cloned.1.call-start = ((), (), s32[]{:S(2)}) async-start(), calls=%async_computation.4 | async-start | bytes 5636096 | tf_op jit(solution)/shard_map/psum | solution.py:105
  169.0 72.3 %copy-start.6 = (bf16[344,1024]{1,0:T(8,128)(2,1)S(1)}, bf16[344,1024]{1,0:T(8,128)(2,1)}, u32[]{:S(2)}) copy-start(bf16[344,1024]{1,0:T(8,128)(2,1)} %param.21) | copy-start | bytes 2113540
  169.0 158.8 %reduce-scatter.5.cloned.1.call-start = ((), (), s32[]{:S(2)}) async-start(), calls=%async_computation.5 | async-start | bytes 4325376 | tf_op jit(solution)/shard_map/reduce_scatter | solution.py:107
  245.8 82.1 %copy-start.2 = (bf16[64,1024]{1,0:T(8,128)(2,1)S(1)}, bf16[64,1024]{1,0:T(8,128)(2,1)}, u32[]{:S(2)}) copy-start(bf16[64,1024]{1,0:T(8,128)(2,1)} %reduce-scatter.3.cloned.1.call-done) | copy-start | bytes 393220
Sparse Core Ops, SparseCore 0:
  82.3 20.4 reduce-scatter.2
  119.7 42.5 all-gather.3
  169.1 69.5 all-reduce.1
  245.9 81.9 reduce-scatter.4
where the time goes:
time: 336 us
  waiting for transfers between devices  194 us (58%)
  blocking collectives  60.7 us (18%)
  local copies, waits for them, and re-layouts  33.2 us (10%)
  matrix products  23.4 us (7%)
  between operations  15.3 us (5%)
  other arithmetic  8.71 us (3%)
    reduce_scatter x1, waiting for transfers between devices, local(): lax.psum_scatter(jnp.dot(activated, down_weight, preferred_element_type=j...  82.1 us
    psum x1, waiting for transfers between devices, local(): lax.psum(partial_units.astype(jnp.bfloat16), 'tensor').astype(jnp.float32)  69.5 us
    all_gather x1, waiting for transfers between devices, local(): lax.all_gather(normed, 'rep', axis=0, tiled=True)  42.7 us
    gather x2, local copies, waits for them, and re-layouts, local(): pool[page_table].reshape(rows_here, page_count * page_len, 2, kv_width)  32.1 us
    all_gather x1, blocking collectives, local(): lax.all_gather(home_attn[-1:], 'rep', axis=0, tiled=True)  26.2 us
    all_gather x1, blocking collectives, local(): lax.all_gather(hidden_in[-1:], 'rep', axis=0, tiled=True)  24 us
    psum x1, blocking collectives, local(): square_sum = lax.psum(jnp.sum(residual * residual, axis=1), 'tensor')  10.5 us
  transfers between devices with their start and end apart: 4, of which 3 were waited for; matrix products, arithmetic and copies ran while one was open for 0% of the time, Pallas kernels for 0%

commit v1 on v0

v1 whole, which is shorter than its diff:
```python
import jax
import jax.numpy as jnp
from jax import lax
from jax.sharding import Mesh, PartitionSpec as P

D = 4096
HD = 128
EPSILON = 1e-05
REP = ("z", "y", "c")
SIDE = 4


def x_ring(shift):
    return [(i, (i + shift) % SIDE) for i in range(SIDE)]


def chip_ring(shift, first):
    pairs = []
    for z in range(SIDE):
        for y in range(SIDE):
            for c in range(2):
                if (c == 0) == first:
                    to = (((z + shift) % SIDE) * SIDE + y) * 2 + c
                else:
                    to = (z * SIDE + (y + shift) % SIDE) * 2 + c
                pairs.append(((z * SIDE + y) * 2 + c, to))
    return pairs


def along_x(value, shift):
    return lax.ppermute(value, "x", x_ring(shift))


def along_chips(value, shift, first):
    return lax.ppermute(value, REP, chip_ring(shift, first))


def other_core(value):
    return lax.ppermute(value, "c", [(0, 1), (1, 0)])


def attend(queries, cache_block, new_pair, counts):
    row_count = cache_block.shape[0]
    cache_len = cache_block.shape[1]
    kv_width = cache_block.shape[3]
    kv_heads = kv_width // HD
    group_size = queries.shape[1] // kv_width
    query_heads = queries.reshape(row_count, kv_heads, group_size, HD)
    key_heads = cache_block[:, :, 0].reshape(row_count, cache_len, kv_heads, HD)
    value_heads = cache_block[:, :, 1].reshape(row_count, cache_len, kv_heads, HD)
    new_key = new_pair[:, 0].reshape(row_count, kv_heads, HD)
    new_value = new_pair[:, 1].reshape(row_count, kv_heads, HD)
    score_scale = HD ** (-0.5)
    scores = (
        jnp.einsum("nkgd,nlkd->nkgl", query_heads, key_heads, preferred_element_type=jnp.float32)
        * score_scale
    )
    own_score = (
        jnp.einsum("nkgd,nkd->nkg", query_heads, new_key, preferred_element_type=jnp.float32)
        * score_scale
    )
    in_range = (jnp.arange(cache_len, dtype=jnp.int32)[None, :] < counts[:, None])[:, None, None, :]
    masked = jnp.where(in_range, scores, -jnp.inf)
    peak_score = jnp.maximum(jnp.max(masked, axis=-1), own_score)
    weights = jnp.where(in_range, jnp.exp(scores - peak_score[..., None]), 0.0)
    own_weight = jnp.exp(own_score - peak_score)
    denominator = jnp.sum(weights, axis=-1) + own_weight
    weighted = jnp.einsum(
        "nkgl,nlkd->nkgd",
        weights.astype(jnp.bfloat16),
        value_heads,
        preferred_element_type=jnp.float32,
    )
    weighted = weighted + jnp.einsum(
        "nkg,nkd->nkgd",
        own_weight.astype(jnp.bfloat16),
        new_value,
        preferred_element_type=jnp.float32,
    )
    return (weighted / denominator[..., None]).astype(jnp.bfloat16).reshape(row_count, -1)


def slot_sources(dest):
    z, y, c = (lax.axis_index(a) for a in REP)
    other, second, first = jnp.meshgrid(
        jnp.arange(2), jnp.arange(SIDE), jnp.arange(SIDE), indexing="ij"
    )
    core = (c + other) % 2
    slot_z = (z - jnp.where(core == 0, first, second)) % SIDE
    slot_y = (y - jnp.where(core == 0, second, first)) % SIDE
    group = ((slot_z * SIDE + slot_y) * 2 + core).reshape(-1)
    target = jnp.sum(
        jnp.where(group[:, None] == jnp.arange(dest.shape[0])[None, :], dest[None, :], 0), axis=1
    )
    hit = group[:, None] == target[None, :]
    return jnp.sum(jnp.where(hit, jnp.arange(group.shape[0])[None, :], 0), axis=1)


def local(
    hidden_in,
    query,
    new_kv,
    pool,
    page_table,
    lengths,
    dest,
    out_weight,
    norm_gain,
    gate_up,
    down_weight,
):
    rows_here = hidden_in.shape[0]
    block = rows_here // SIDE
    x = lax.axis_index("x")
    my_group = lax.axis_index(REP)
    units = gate_up.shape[2]
    width = gate_up.shape[0]

    gate_up_t = jnp.transpose(gate_up, (1, 2, 0)).reshape(2 * units, width)
    weights = lax.all_gather(gate_up_t, "x", axis=0, tiled=False)
    gains = jnp.stack([norm_gain] + [along_x(norm_gain, s) for s in range(1, SIDE)])
    gain = gains[(x - jnp.arange(SIDE)) % SIDE].reshape(-1)

    cache_rows = pool[page_table].reshape(rows_here, -1, 2, pool.shape[3])
    my_lengths = lax.dynamic_slice_in_dim(lengths, my_group * rows_here, rows_here)
    attention = attend(query, cache_rows, new_kv, my_lengths)
    projected = jnp.dot(attention, out_weight, preferred_element_type=jnp.float32)
    mine = (jnp.arange(SIDE) == x)[None, :, None]
    projected = projected.reshape(rows_here, SIDE, width) + jnp.where(
        mine, hidden_in.astype(jnp.float32)[:, None, :], 0.0
    )
    projected = projected.astype(jnp.bfloat16).reshape(SIDE, block, SIDE * width)

    def for_shift(s):
        return lax.dynamic_index_in_dim(projected, (x + s) % SIDE, 0, keepdims=False)

    parts = [for_shift(0)] + [along_x(for_shift(s), s) for s in (1, 3, 2)]
    residual = sum(p.astype(jnp.float32) for p in parts)
    square = jnp.mean(residual * residual, axis=1, keepdims=True)
    normed = (residual * lax.rsqrt(square + EPSILON) * gain[None, :]).astype(jnp.bfloat16)

    residual_b = residual.astype(jnp.bfloat16).reshape(block, SIDE, width)

    def piece(s):
        return lax.dynamic_index_in_dim(residual_b, (x + s) % SIDE, 1, keepdims=False)

    pieces = jnp.stack([piece(0)] + [along_x(piece(s), s) for s in range(1, SIDE)])
    home = pieces[(x - jnp.arange(SIDE)) % SIDE].reshape(rows_here, width)

    first = jnp.concatenate([normed] + [along_chips(normed, s, True) for s in (1, 2, 3)])
    second = [first] + [along_chips(first, s, False) for s in (1, 2, 3)]
    every = jnp.concatenate(second + [other_core(v) for v in second])

    both = sum(
        lax.dot_general(
            every[:, t * width : (t + 1) * width],
            weights[t],
            (((1,), (1,)), ((), ())),
            preferred_element_type=jnp.float32,
        )
        for t in range(SIDE)
    )
    activated = jax.nn.silu(both[:, :units]) * both[:, units:]
    source = slot_sources(dest)
    slots = source.shape[0]
    source = jnp.where(x == SIDE - 1, source, jnp.arange(slots))
    activated = activated.astype(jnp.bfloat16).reshape(slots, block, units)
    last = activated[source, block - 1]
    activated = jnp.concatenate([activated[:, : block - 1], last[:, None]], axis=1)

    gathered = jnp.stack([activated] + [along_x(activated, s) for s in range(1, SIDE)])
    gathered = gathered[(x - jnp.arange(SIDE)) % SIDE]
    gathered = jnp.transpose(gathered, (1, 0, 2, 3)).reshape(slots * rows_here, units)
    down = jnp.dot(gathered, down_weight, preferred_element_type=jnp.float32)
    down = down.reshape(slots, rows_here, width)
    moved_to = slot_sources_inverse(dest)
    row = jnp.arange(rows_here)[None, :]
    target = jnp.where(row == rows_here - 1, moved_to, 0)
    mine = (jnp.arange(slots)[:, None] == target)[..., None]
    down = down + jnp.where(mine, home.astype(jnp.float32)[None], 0.0)
    down = down.astype(jnp.bfloat16).reshape(2, SIDE, SIDE * rows_here, width)

    summed = [
        (down[0, s].astype(jnp.float32) + other_core(down[1, s]).astype(jnp.float32)).astype(
            jnp.bfloat16
        )
        for s in range(SIDE)
    ]
    back = [summed[0]] + [along_chips(summed[s], -s, False) for s in (1, 2, 3)]
    total = sum(v.astype(jnp.float32) for v in back).astype(jnp.bfloat16)
    total = total.reshape(SIDE, rows_here, width)
    back = [total[0]] + [along_chips(total[s], -s, True) for s in (1, 2, 3)]
    return sum(v.astype(jnp.float32) for v in back).astype(jnp.bfloat16)


def slot_sources_inverse(dest):
    source = slot_sources(dest)
    return jnp.sum(jnp.where(source == 0, jnp.arange(source.shape[0]), 0))


def solution(mesh):
    chips = Mesh(mesh.devices.reshape(SIDE, SIDE, 2, SIDE), ("z", "y", "c", "x"))
    return jax.shard_map(
        local,
        mesh=chips,
        in_specs=(
            P(REP, "x"),
            P(REP, "x"),
            P(REP, None, "x"),
            P(REP, None, None, "x"),
            P(REP, None),
            P(),
            P(),
            P("x", None),
            P("x"),
            P("x", None, REP),
            P(REP, "x"),
        ),
        out_specs=P(REP, "x"),
        check_vma=False,
    )
```

time: 336 us -> 202 us (0.60)
  waiting for transfers between devices: 194 us -> 57.5 us
  blocking collectives: 60.7 us -> 0 us
  starting transfers between devices: 0.31 us -> 37.5 us
  local copies, waits for them, and re-layouts: 33.2 us -> 60.8 us
    reduce_scatter x2 -> x0, waiting for transfers between devices: 82.1 us -> none  [the longest x1 82.1 us: local(): lax.psum_scatter(jnp.dot(activated, down_weight, preferred_element_type=j...]
    psum x1 -> x0, waiting for transfers between devices: 69.5 us -> none  [local(): lax.psum(partial_units.astype(jnp.bfloat16), 'tensor').astype(jnp.float32)]
    ppermute x0 -> x32, waiting for transfers between devices: none -> 57.4 us  [the longest x12 29.6 us: along_x(): return lax.ppermute(value, 'x', x_ring(shift))]
    all_gather x2 -> x0, blocking collectives: 50.2 us -> none  [the longest x1 26.2 us: local(): lax.all_gather(home_attn[-1:], 'rep', axis=0, tiled=True)]
    all_gather x1, waiting for transfers between devices: 42.7 us -> 0.01 us  [local(): weights = lax.all_gather(gate_up_t, 'x', axis=0, tiled=False)]
    ppermute x0 -> x32, starting transfers between devices: none -> 37.5 us  [the longest x12 21 us: along_chips(): return lax.ppermute(value, REP, chip_ring(shift, first))]
    dot_general x0 -> x1, local copies, waits for them, and re-layouts: none -> 12.1 us  [local(): jnp.dot(attention, out_weight, preferred_element_type=jnp.float32)]
    psum x1 -> x0, blocking collectives: 10.5 us -> none  [local(): square_sum = lax.psum(jnp.sum(residual * residual, axis=1), 'tensor')]
  transfers between devices with their start and end apart: 4 -> 33, of which waited for: 3 -> 16; matrix products, arithmetic and copies ran while one was open for 0% -> 36% of each run, Pallas kernels for 0% -> 0%
where the time goes in v1:
time: 202 us; the launch traced here: 201 us
  local copies, waits for them, and re-layouts  60.8 us (30%)
  waiting for transfers between devices  57.5 us (28%)
  starting transfers between devices  37.5 us (19%)
  matrix products  24.9 us (12%)
  between operations  14 us (7%)
  other arithmetic  6.64 us (3%)
    gather x2, local copies, waits for them, and re-layouts, local(): cache_rows = pool[page_table].reshape(rows_here, -1, 2, pool.shape[3])  32.3 us
    ppermute x12, waiting for transfers between devices, along_x(): return lax.ppermute(value, 'x', x_ring(shift))  29.6 us
    ppermute x12, waiting for transfers between devices, along_chips(): return lax.ppermute(value, REP, chip_ring(shift, first))  25.5 us
    ppermute x12, starting transfers between devices, along_chips(): return lax.ppermute(value, REP, chip_ring(shift, first))  21 us
    ppermute x12, starting transfers between devices, along_x(): return lax.ppermute(value, 'x', x_ring(shift))  14.7 us
    dot_general x1, local copies, waits for them, and re-layouts, local(): jnp.dot(attention, out_weight, preferred_element_type=jnp.float32)  12.1 us
    dot_general x4, matrix products, local(): lax.dot_general(every[:, t * width:(t + 1) * width], weights[t], (((1,),...  9.68 us
    unnamed x30, local copies, waits for them, and re-layouts  7.09 us
  transfers between devices with their start and end apart: 33, of which 16 were waited for; matrix products, arithmetic and copies ran while one was open for 36% of the time, Pallas kernels for 0%

profile of v1, /device:TPU:0, one launch (start us, length us, event | category | flops | bytes accessed | tf_op | source)
XLA Modules:
  0.0 201.3 jit_solution(5285808861563448678)
XLA Ops:
  6.5 2.8 %collective-permute-start.5 = (f32[1024]{0:T(1024)}, f32[1024]{0:T(1024)S(1)}, u32[]{:S(2)}, u32[]{:S(2)}) collective-permute-start(f32[1024]{0:T(1024)} %param.19), channel_id=1, source_target_pairs={{0,3},{1,0},{2,1},{3,2},{4,7},{5,4},{6,5},{7,6},{8,11},{9,8},{10,9... | collective-permute-start | bytes 12296 | tf_op jit(solution)/shard_map/ppermute | solution.py:31
  10.2 0.9 collective-permute-start.3
  12.1 23.3 %gather_fusion = bf16[128,128,2,128]{3,2,1,0:T(2,128)(2,1)} fusion(bf16[128,128,2,128]{3,2,1,0:T(2,128)(2,1)} %param.14, s32[1024]{0:T(1024)S(1)} %pad_clamp_fusion.1), kind=kCustom, calls=%fused_computation | custom fusion | bytes 16777728 | tf_op jit(solution)/shard_map/gather | solution.py:124
  35.4 9.1 %copy.54 = bf16[128,128,2,128]{3,1,0,2:T(8,128)(2,1)} copy(bf16[128,128,2,128]{3,2,1,0:T(2,128)(2,1)} %gather_fusion) | data formatting | bytes 16777216 | tf_op jit(solution)/shard_map/gather | solution.py:124
  45.6 3.5 %select_reduce_fusion = (f32[64,8]{1,0:T(8,128)S(1)}, f32[64,256,8]{1,2,0:T(8,128)S(1)}) fusion(pred[64,256]{1,0:T(8,128)(4,1)S(1)} %iota_compare_fusion, bf16[64,8,128]{2,1,0:T(8,128)(2,1)S(1)} %bitcast.160, bf16[64,256,2,128]{3,1,0,2:T(8,128)(2,1)} %bitcast.142), kind=kOutput, calls=%fused_computation.55 | convolution fusion | flops 33947136 | bytes 4868096 | tf_op jit(solution)/shard_map/nkgd,nlkd->nkgl/dot_general | solution.py:55
  49.4 2.9 %fusion.11 = bf16[64,8,128]{2,1,0:T(8,128)(2,1)S(1)} fusion(bf16[64,256,2,128]{3,1,0,2:T(8,128)(2,1)} %bitcast.143, f32[64,256,8]{1,2,0:T(8,128)S(1)} %get-tuple-element.31, f32[64,8]{1,0:T(8,128)S(1)} %multiply_maximum_fusion, pred[64,256]{1,0:T(8,128)(4,1)S(1)} %iota_compare_fusion, f32[64,8]{1,0:T(8,128)S(1)} %get-tuple-element.27, ...), kind=kOutput, calls=%fused_computation.26 | convolution fusion | flops 34209792 | bytes 4904960 | tf_op jit(solution)/shard_map/nkgl,nlkd->nkgd/dot_general | solution.py:68
  52.3 12.1 %copy.67 = bf16[4096,1024]{1,0:T(8,128)(2,1)} copy(bf16[4096,1024]{0,1:T(8,128)(2,1)} %bitcast.141) | data formatting | bytes 16777216 | tf_op jit(solution)/shard_map/dot_general | solution.py:127
  64.5 6.1 %fusion.7 = bf16[64,4,1024]{2,0,1:T(8,128)(2,1)S(1)} fusion(bf16[64,1024,1]{1,0,2:T(8,128)(2,1)S(1)} %reshape.380, bf16[4,1024,1024]{2,1,0:T(8,128)(2,1)} %bitcast.140, f32[64,1024]{1,0:T(8,128)S(1)} %convert_element_type.136, pred[4]{0:T(512)(128)(4,1)S(1)} %iota_compare_fusion.3), kind=kOutput, calls=%fused_computation.22 | convolution fusion | flops 537657344 | bytes 9306116 | tf_op jit(solution)/shard_map/dot_general | solution.py:127
  71.4 1.9 collective-permute-start.2
  73.3 2.7 %collective-permute-start.1 = (bf16[16,4096]{1,0:T(8,128)(2,1)S(1)}, bf16[16,4096]{1,0:T(8,128)(2,1)S(1)}, u32[]{:S(2)}, u32[]{:S(2)}) collective-permute-start(bf16[16,4096]{1,0:T(8,128)(2,1)S(1)} %get-tuple-element.21), channel_id=1, source_target_pairs={{0,3},{1,0},{2,1},{3,2},{4,7},{5,4},{6,5},{7,6},{8,11},{9,8},{10,9... | collective-permute-start | bytes 393224 | tf_op jit(solution)/shard_map/ppermute | solution.py:31
  78.9 1.1 collective-permute-done.1
  79.9 4.4 %collective-permute-done = bf16[16,4096]{1,0:T(8,128)(2,1)S(1)} collective-permute-done((bf16[16,4096]{1,0:T(8,128)(2,1)S(1)}, bf16[16,4096]{1,0:T(8,128)(2,1)S(1)}, u32[]{:S(2)}, u32[]{:S(2)}) %collective-permute-start) | collective-permute-done | bytes 131104 | tf_op jit(solution)/shard_map/ppermute | solution.py:31
  86.0 1.9 collective-permute-start.6
  87.9 3.6 %collective-permute-start.7 = (bf16[16,4096]{1,0:T(8,128)(2,1)S(1)}, bf16[16,4096]{1,0:T(8,128)(2,1)S(1)}, u32[]{:S(2)}, u32[]{:S(2)}) collective-permute-start(bf16[16,4096]{1,0:T(8,128)(2,1)S(1)} %get-tuple-element.6), channel_id=1, source_target_pairs={{0,64},{4,20},{8,72},{12,28},{16,80},{20,4},{24,88},{28,12},{32,96... | collective-permute-start | bytes 393224 | tf_op jit(solution)/shard_map/ppermute | solution.py:35
  91.5 1.0 collective-permute-start.8
  92.5 0.9 collective-permute-start.20
  93.5 1.3 collective-permute-start.19
  94.7 3.3 %collective-permute-done.20 = bf16[16,1024]{1,0:T(8,128)(2,1)S(1)} collective-permute-done((bf16[16,1024]{1,0:T(8,128)(2,1)S(1)}, bf16[16,1024]{1,0:T(8,128)(2,1)S(1)}, u32[]{:S(2)}, u32[]{:S(2)}) %collective-permute-start.20) | collective-permute-done | bytes 32800 | tf_op jit(solution)/shard_map/ppermute | solution.py:31
  98.0 1.3 collective-permute-done.19
  99.9 1.6 collective-permute-start.9
  101.5 2.9 %collective-permute-start.10 = (bf16[64,4096]{1,0:T(8,128)(2,1)S(1)}, bf16[64,4096]{1,0:T(8,128)(2,1)S(1)}, u32[]{:S(2)}, u32[]{:S(2)}) collective-permute-start(bf16[64,4096]{1,0:T(8,128)(2,1)S(1)} %pad_maximum_fusion.1), channel_id=1, source_target_pairs={{0,16},{4,68},{8,24},{12,76},{16,0},{20,84},{24,8},{28,92},{32,48}... | collective-permute-start | bytes 1572872 | tf_op jit(solution)/shard_map/ppermute | solution.py:35
  104.5 1.3 collective-permute-start.11
  107.8 2.6 %collective-permute-done.9 = bf16[64,4096]{1,0:T(8,128)(2,1)S(1)} collective-permute-done((bf16[64,4096]{1,0:T(8,128)(2,1)S(1)}, bf16[64,4096]{1,0:T(8,128)(2,1)S(1)}, u32[]{:S(2)}, u32[]{:S(2)}) %collective-permute-start.9) | collective-permute-done | bytes 524320 | tf_op jit(solution)/shard_map/ppermute | solution.py:35
  110.4 0.8 constant_dynamic-update-slice_fusion.6
  111.2 6.0 %collective-permute-done.10 = bf16[64,4096]{1,0:T(8,128)(2,1)S(1)} collective-permute-done((bf16[64,4096]{1,0:T(8,128)(2,1)S(1)}, bf16[64,4096]{1,0:T(8,128)(2,1)S(1)}, u32[]{:S(2)}, u32[]{:S(2)}) %collective-permute-start.10) | collective-permute-done | bytes 524320 | tf_op jit(solution)/shard_map/ppermute | solution.py:35
  117.2 0.8 constant_dynamic-update-slice_fusion.5
  119.4 0.8 constant_dynamic-update-slice_fusion.3
  122.7 2.7 %fusion.3 = f32[512,688]{0,1:T(8,128)S(1)} fusion(bf16[4,688,1024]{2,1,0:T(8,128)(2,1)} %all-gather.2.cloned.1.call-done, bf16[512,4096]{1,0:T(8,128)(2,1)} %constant_dynamic-update-slice_fusion), kind=kOutput, calls=%fused_computation.14 | convolution fusion | flops 721420288 | bytes 3866624 | tf_op jit(solution)/shard_map/dot_general | solution.py:155
  125.5 2.6 %fusion.4 = f32[512,688]{0,1:T(8,128)S(1)} fusion(bf16[4,688,1024]{2,1,0:T(8,128)(2,1)} %all-gather.2.cloned.1.call-done, bf16[512,4096]{1,0:T(8,128)(2,1)} %constant_dynamic-update-slice_fusion), kind=kOutput, calls=%fused_computation.16 | convolution fusion | flops 721420288 | bytes 3866624 | tf_op jit(solution)/shard_map/dot_general | solution.py:155
  128.1 2.2 %fusion.5 = f32[512,688]{0,1:T(8,128)S(1)} fusion(bf16[4,688,1024]{2,1,0:T(8,128)(2,1)S(1)} %copy-done.1, bf16[512,4096]{1,0:T(8,128)(2,1)} %constant_dynamic-update-slice_fusion), kind=kOutput, calls=%fused_computation.18 | convolution fusion | flops 721420288 | bytes 3866624 | tf_op jit(solution)/shard_map/dot_general | solution.py:155
  130.3 2.2 %fusion.6 = f32[512,688]{0,1:T(8,128)S(1)} fusion(f32[512,688]{0,1:T(8,128)S(1)} %fusion.3, f32[512,688]{0,1:T(8,128)S(1)} %fusion.4, f32[512,688]{0,1:T(8,128)S(1)} %fusion.5, bf16[4,688,1024]{2,1,0:T(8,128)(2,1)S(1)} %copy-done.1, bf16[512,4096]{1,0:T(8,128)(2,1)} %constant_dynamic-update-slice_fusion), kind=kOutput, calls=%fused_computation.20 | convolution fusion | flops 722477056 | bytes 8093696 | tf_op jit(solution)/shard_map/dot_general | solution.py:155
  133.8 2.1 %collective-permute-start.18 = (bf16[32,16,344]{2,1,0:T(8,128)(2,1)S(1)}, bf16[32,16,344]{2,1,0:T(8,128)(2,1)S(1)}, u32[]{:S(2)}, u32[]{:S(2)}) collective-permute-start(bf16[32,16,344]{2,1,0:T(8,128)(2,1)S(1)} %pad_maximum_fusion.2), channel_id=1, source_target_pairs={{0,3},{1,0},{2,1},{3,2},{4,7},{5,4},{6,5},{7,6},{8,11},{9,8},{10,9... | collective-permute-start | bytes 1056776 | tf_op jit(solution)/shard_map/ppermute | solution.py:31
  137.0 15.9 %collective-permute-done.18 = bf16[32,16,344]{2,1,0:T(8,128)(2,1)S(1)} collective-permute-done((bf16[32,16,344]{2,1,0:T(8,128)(2,1)S(1)}, bf16[32,16,344]{2,1,0:T(8,128)(2,1)S(1)}, u32[]{:S(2)}, u32[]{:S(2)}) %collective-permute-start.18) | collective-permute-done | bytes 352288 | tf_op jit(solution)/shard_map/ppermute | solution.py:31
  152.9 3.7 %collective-permute-done.16 = bf16[32,16,344]{2,1,0:T(8,128)(2,1)S(1)} collective-permute-done((bf16[32,16,344]{2,1,0:T(8,128)(2,1)S(1)}, bf16[32,16,344]{2,1,0:T(8,128)(2,1)S(1)}, u32[]{:S(2)}, u32[]{:S(2)}) %collective-permute-start.16) | collective-permute-done | bytes 352288 | tf_op jit(solution)/shard_map/ppermute | solution.py:31
  156.9 1.9 gather_fusion.3
  158.9 1.7 copy.60
  160.6 2.6 %add_convert_fusion = bf16[32,64,1024]{2,1,0:T(8,128)(2,1)S(1)} fusion(f32[64,1024]{1,0:T(8,128)S(1)} %bitcast_convert_fusion.2, pred[32,64]{1,0:T(8,128)(4,1)S(1)} %iota_compare_fusion.1, bf16[32,64,344]{2,1,0:T(8,128)(2,1)S(1)} %bitcast.151, bf16[344,1024]{1,0:T(8,128)(2,1)S(1)} %copy-done), kind=kOutput, calls=%fused_computation.5 | convolution fusion | flops 1449132032 | bytes 6572032 | tf_op jit(solution)/shard_map/dot_general | solution.py:174
  164.7 0.9 collective-permute-done.23
  167.7 0.9 collective-permute-start.28
  168.6 2.1 %collective-permute-start.26 = (bf16[256,1024]{1,0:T(8,128)(2,1)S(1)}, bf16[256,1024]{1,0:T(8,128)(2,1)S(1)}, u32[]{:S(2)}, u32[]{:S(2)}) collective-permute-start(bf16[256,1024]{1,0:T(8,128)(2,1)S(1)} %get-tuple-element.15), channel_id=1, source_target_pairs={{0,16},{4,68},{8,24},{12,76},{16,0},{20,84},{24,8},{28,92},{32,48}... | collective-permute-start | bytes 1572872 | tf_op jit(solution)/shard_map/ppermute | solution.py:35
  170.7 1.8 collective-permute-start.24
  172.5 11.3 %collective-permute-done.28 = bf16[256,1024]{1,0:T(8,128)(2,1)S(1)} collective-permute-done((bf16[256,1024]{1,0:T(8,128)(2,1)S(1)}, bf16[256,1024]{1,0:T(8,128)(2,1)S(1)}, u32[]{:S(2)}, u32[]{:S(2)}) %collective-permute-start.28) | collective-permute-done | bytes 524320 | tf_op jit(solution)/shard_map/ppermute | solution.py:35
  183.8 0.9 collective-permute-done.24
  185.2 1.1 collective-permute-start.31
  186.8 2.3 %collective-permute-start.29 = (bf16[64,1024]{1,0:T(8,128)(2,1)S(1)}, bf16[64,1024]{1,0:T(8,128)(2,1)S(1)}, u32[]{:S(2)}, u32[]{:S(2)}) collective-permute-start(bf16[64,1024]{1,0:T(8,128)(2,1)S(1)} %get-tuple-element.16), channel_id=1, source_target_pairs={{0,96},{4,28},{8,104},{12,4},{16,112},{20,12},{24,120},{28,20},{32... | collective-permute-start | bytes 393224 | tf_op jit(solution)/shard_map/ppermute | solution.py:35
  189.1 2.4 %collective-permute-done.31 = bf16[64,1024]{1,0:T(8,128)(2,1)S(1)} collective-permute-done((bf16[64,1024]{1,0:T(8,128)(2,1)S(1)}, bf16[64,1024]{1,0:T(8,128)(2,1)S(1)}, u32[]{:S(2)}, u32[]{:S(2)}) %collective-permute-start.31) | collective-permute-done | bytes 131104 | tf_op jit(solution)/shard_map/ppermute | solution.py:35
  191.5 1.4 collective-permute-done.30
  192.9 0.9 collective-permute-done.29
  (120 shorter events, 23.0 us)
Async XLA Ops:
  6.5 154.0 %copy-start = (bf16[344,1024]{1,0:T(8,128)(2,1)S(1)}, bf16[344,1024]{1,0:T(8,128)(2,1)}, u32[]{:S(2)}) copy-start(bf16[344,1024]{1,0:T(8,128)(2,1)} %param.21) | copy-start | bytes 2113540
  6.5 116.2 %all-gather.2.cloned.1.call-start = ((), (), s32[]{:S(2)}) async-start(), calls=%async_computation | async-start | bytes 7045120 | tf_op jit(solution)/shard_map/all_gather | solution.py:120
  6.5 71.6 %collective-permute-start.5 = (f32[1024]{0:T(1024)}, f32[1024]{0:T(1024)S(1)}, u32[]{:S(2)}, u32[]{:S(2)}) collective-permute-start(f32[1024]{0:T(1024)} %param.19), channel_id=1, source_target_pairs={{0,3},{1,0},{2,1},{3,2},{4,7},{5,4},{6,5},{7,6},{8,11},{9,8},{10,9... | collective-permute-start | bytes 12296 | tf_op jit(solution)/shard_map/ppermute | solution.py:31
  9.4 68.8 %collective-permute-start.4 = (f32[1024]{0:T(1024)}, f32[1024]{0:T(1024)S(1)}, u32[]{:S(2)}, u32[]{:S(2)}) collective-permute-start(f32[1024]{0:T(1024)} %param.19), channel_id=1, source_target_pairs={{0,2},{1,3},{2,0},{3,1},{4,6},{5,7},{6,4},{7,5},{8,10},{9,11},{10,... | collective-permute-start | bytes 12296 | tf_op jit(solution)/shard_map/ppermute | solution.py:31
  10.2 68.0 %collective-permute-start.3 = (f32[1024]{0:T(1024)}, f32[1024]{0:T(1024)S(1)}, u32[]{:S(2)}, u32[]{:S(2)}) collective-permute-start(f32[1024]{0:T(1024)} %param.19), channel_id=1, source_target_pairs={{0,1},{1,2},{2,3},{3,0},{4,5},{5,6},{6,7},{7,4},{8,9},{9,10},{10,1... | collective-permute-start | bytes 12296 | tf_op jit(solution)/shard_map/ppermute | solution.py:31
  35.4 9.9 %copy-start.3 = (bf16[64,1024]{1,0:T(8,128)(2,1)S(1)}, bf16[64,1024]{1,0:T(8,128)(2,1)}, u32[]{:S(2)}) copy-start(bf16[64,1024]{1,0:T(8,128)(2,1)} %param.12) | copy-start | bytes 393220
  35.4 9.9 %copy-start.4 = (bf16[64,2,128]{2,1,0:T(2,128)(2,1)S(1)}, bf16[64,2,128]{2,1,0:T(2,128)(2,1)}, u32[]{:S(2)}) copy-start(bf16[64,2,128]{2,1,0:T(2,128)(2,1)} %param.13) | copy-start | bytes 98308
  52.3 12.1 %copy-start.2 = (bf16[64,1024]{1,0:T(8,128)(2,1)S(1)}, bf16[64,1024]{1,0:T(8,128)(2,1)}, u32[]{:S(2)}) copy-start(bf16[64,1024]{1,0:T(8,128)(2,1)} %param.11) | copy-start | bytes 393220
  64.5 11.9 %copy-start.6 = (s32[32]{0:T(128)S(1)}, s32[32]{0:T(128)}, u32[]{:S(2)}) copy-start(s32[32]{0:T(128)} %param.17) | copy-start | bytes 388
  64.5 13.8 %copy-start.5 = (f32[1024]{0:T(1024)S(1)}, f32[1024]{0:T(1024)}, u32[]{:S(2)}) copy-start(f32[1024]{0:T(1024)} %param.19) | copy-start | bytes 12292
  71.4 7.5 %collective-permute-start.2 = (bf16[16,4096]{1,0:T(8,128)(2,1)S(1)}, bf16[16,4096]{1,0:T(8,128)(2,1)S(1)}, u32[]{:S(2)}, u32[]{:S(2)}) collective-permute-start(bf16[16,4096]{1,0:T(8,128)(2,1)S(1)} %get-tuple-element.20), channel_id=1, source_target_pairs={{0,2},{1,3},{2,0},{3,1},{4,6},{5,7},{6,4},{7,5},{8,10},{9,11},{10,... | collective-permute-start | bytes 393224 | tf_op jit(solution)/shard_map/ppermute | solution.py:31
  73.3 6.6 %collective-permute-start.1 = (bf16[16,4096]{1,0:T(8,128)(2,1)S(1)}, bf16[16,4096]{1,0:T(8,128)(2,1)S(1)}, u32[]{:S(2)}, u32[]{:S(2)}) collective-permute-start(bf16[16,4096]{1,0:T(8,128)(2,1)S(1)} %get-tuple-element.21), channel_id=1, source_target_pairs={{0,3},{1,0},{2,1},{3,2},{4,7},{5,4},{6,5},{7,6},{8,11},{9,8},{10,9... | collective-permute-start | bytes 393224 | tf_op jit(solution)/shard_map/ppermute | solution.py:31
  78.1 6.2 %collective-permute-start = (bf16[16,4096]{1,0:T(8,128)(2,1)S(1)}, bf16[16,4096]{1,0:T(8,128)(2,1)S(1)}, u32[]{:S(2)}, u32[]{:S(2)}) collective-permute-start(bf16[16,4096]{1,0:T(8,128)(2,1)S(1)} %get-tuple-element.19), channel_id=1, source_target_pairs={{0,1},{1,2},{2,3},{3,0},{4,5},{5,6},{6,7},{7,4},{8,9},{9,10},{10,1... | collective-permute-start | bytes 393224 | tf_op jit(solution)/shard_map/ppermute | solution.py:31
  85.0 8.5 %collective-permute-start.21 = (bf16[16,1024]{1,0:T(8,128)(2,1)S(1)}, bf16[16,1024]{1,0:T(8,128)(2,1)S(1)}, u32[]{:S(2)}, u32[]{:S(2)}) collective-permute-start(bf16[16,1024]{1,0:T(8,128)(2,1)S(1)} %bitcast.165), channel_id=1, source_target_pairs={{0,3},{1,0},{2,1},{3,2},{4,7},{5,4},{6,5},{7,6},{8,11},{9,8},{10,9... | collective-permute-start | bytes 98312 | tf_op jit(solution)/shard_map/ppermute | solution.py:31
  86.0 13.9 %collective-permute-start.6 = (bf16[16,4096]{1,0:T(8,128)(2,1)S(1)}, bf16[16,4096]{1,0:T(8,128)(2,1)S(1)}, u32[]{:S(2)}, u32[]{:S(2)}) collective-permute-start(bf16[16,4096]{1,0:T(8,128)(2,1)S(1)} %get-tuple-element.6), channel_id=1, source_target_pairs={{0,32},{4,12},{8,40},{12,20},{16,48},{20,28},{24,56},{28,4},{32,64... | collective-permute-start | bytes 393224 | tf_op jit(solution)/shard_map/ppermute | solution.py:35
  87.9 12.0 %collective-permute-start.7 = (bf16[16,4096]{1,0:T(8,128)(2,1)S(1)}, bf16[16,4096]{1,0:T(8,128)(2,1)S(1)}, u32[]{:S(2)}, u32[]{:S(2)}) collective-permute-start(bf16[16,4096]{1,0:T(8,128)(2,1)S(1)} %get-tuple-element.6), channel_id=1, source_target_pairs={{0,64},{4,20},{8,72},{12,28},{16,80},{20,4},{24,88},{28,12},{32,96... | collective-permute-start | bytes 393224 | tf_op jit(solution)/shard_map/ppermute | solution.py:35
  91.5 8.4 %collective-permute-start.8 = (bf16[16,4096]{1,0:T(8,128)(2,1)S(1)}, bf16[16,4096]{1,0:T(8,128)(2,1)S(1)}, u32[]{:S(2)}, u32[]{:S(2)}) collective-permute-start(bf16[16,4096]{1,0:T(8,128)(2,1)S(1)} %get-tuple-element.6), channel_id=1, source_target_pairs={{0,96},{4,28},{8,104},{12,4},{16,112},{20,12},{24,120},{28,20},{32... | collective-permute-start | bytes 393224 | tf_op jit(solution)/shard_map/ppermute | solution.py:35
  92.5 5.5 %collective-permute-start.20 = (bf16[16,1024]{1,0:T(8,128)(2,1)S(1)}, bf16[16,1024]{1,0:T(8,128)(2,1)S(1)}, u32[]{:S(2)}, u32[]{:S(2)}) collective-permute-start(bf16[16,1024]{1,0:T(8,128)(2,1)S(1)} %bitcast.166), channel_id=1, source_target_pairs={{0,2},{1,3},{2,0},{3,1},{4,6},{5,7},{6,4},{7,5},{8,10},{9,11},{10,... | collective-permute-start | bytes 98312 | tf_op jit(solution)/shard_map/ppermute | solution.py:31
  93.5 5.8 %collective-permute-start.19 = (bf16[16,1024]{1,0:T(8,128)(2,1)S(1)}, bf16[16,1024]{1,0:T(8,128)(2,1)S(1)}, u32[]{:S(2)}, u32[]{:S(2)}) collective-permute-start(bf16[16,1024]{1,0:T(8,128)(2,1)S(1)} %bitcast.167), channel_id=1, source_target_pairs={{0,1},{1,2},{2,3},{3,0},{4,5},{5,6},{6,7},{7,4},{8,9},{9,10},{10,1... | collective-permute-start | bytes 98312 | tf_op jit(solution)/shard_map/ppermute | solution.py:31
  99.9 10.5 %collective-permute-start.9 = (bf16[64,4096]{1,0:T(8,128)(2,1)S(1)}, bf16[64,4096]{1,0:T(8,128)(2,1)S(1)}, u32[]{:S(2)}, u32[]{:S(2)}) collective-permute-start(bf16[64,4096]{1,0:T(8,128)(2,1)S(1)} %pad_maximum_fusion.1), channel_id=1, source_target_pairs={{0,8},{4,36},{8,16},{12,44},{16,24},{20,52},{24,0},{28,60},{32,40}... | collective-permute-start | bytes 1572872 | tf_op jit(solution)/shard_map/ppermute | solution.py:35
  101.5 15.7 %collective-permute-start.10 = (bf16[64,4096]{1,0:T(8,128)(2,1)S(1)}, bf16[64,4096]{1,0:T(8,128)(2,1)S(1)}, u32[]{:S(2)}, u32[]{:S(2)}) collective-permute-start(bf16[64,4096]{1,0:T(8,128)(2,1)S(1)} %pad_maximum_fusion.1), channel_id=1, source_target_pairs={{0,16},{4,68},{8,24},{12,76},{16,0},{20,84},{24,8},{28,92},{32,48}... | collective-permute-start | bytes 1572872 | tf_op jit(solution)/shard_map/ppermute | solution.py:35
  104.5 13.6 %collective-permute-start.11 = (bf16[64,4096]{1,0:T(8,128)(2,1)S(1)}, bf16[64,4096]{1,0:T(8,128)(2,1)S(1)}, u32[]{:S(2)}, u32[]{:S(2)}) collective-permute-start(bf16[64,4096]{1,0:T(8,128)(2,1)S(1)} %pad_maximum_fusion.1), channel_id=1, source_target_pairs={{0,24},{4,100},{8,0},{12,108},{16,8},{20,116},{24,16},{28,124},{32... | collective-permute-start | bytes 1572872 | tf_op jit(solution)/shard_map/ppermute | solution.py:35
  105.8 13.6 %collective-permute-start.12 = (bf16[64,4096]{1,0:T(8,128)(2,1)S(1)}, bf16[64,4096]{1,0:T(8,128)(2,1)S(1)}, u32[]{:S(2)}, u32[]{:S(2)}) collective-permute-start(bf16[64,4096]{1,0:T(8,128)(2,1)S(1)} %pad_maximum_fusion.1), channel_id=1, source_target_pairs={{0,4},{4,0},{1,5},{5,1},{2,6},{6,2},{3,7},{7,3},{8,12},{12,8},{9,1... | collective-permute-start | bytes 1572872 | tf_op jit(solution)/shard_map/ppermute | solution.py:39
  110.4 9.9 %collective-permute-start.13 = (bf16[64,4096]{1,0:T(8,128)(2,1)S(1)}, bf16[64,4096]{1,0:T(8,128)(2,1)S(1)}, u32[]{:S(2)}, u32[]{:S(2)}) collective-permute-start(bf16[64,4096]{1,0:T(8,128)(2,1)S(1)} %collective-permute-done.9), channel_id=1, source_target_pairs={{0,4},{4,0},{1,5},{5,1},{2,6},{6,2},{3,7},{7,3},{8,12},{12,8},{9,1... | collective-permute-start | bytes 1572872 | tf_op jit(solution)/shard_map/ppermute | solution.py:39
  117.2 3.8 %collective-permute-start.14 = (bf16[64,4096]{1,0:T(8,128)(2,1)S(1)}, bf16[64,4096]{1,0:T(8,128)(2,1)S(1)}, u32[]{:S(2)}, u32[]{:S(2)}) collective-permute-start(bf16[64,4096]{1,0:T(8,128)(2,1)S(1)} %collective-permute-done.10), channel_id=1, source_target_pairs={{0,4},{4,0},{1,5},{5,1},{2,6},{6,2},{3,7},{7,3},{8,12},{12,8},{9,1... | collective-permute-start | bytes 1572872 | tf_op jit(solution)/shard_map/ppermute | solution.py:39
  118.1 3.8 %collective-permute-start.15 = (bf16[64,4096]{1,0:T(8,128)(2,1)S(1)}, bf16[64,4096]{1,0:T(8,128)(2,1)S(1)}, u32[]{:S(2)}, u32[]{:S(2)}) collective-permute-start(bf16[64,4096]{1,0:T(8,128)(2,1)S(1)} %collective-permute-done.11), channel_id=1, source_target_pairs={{0,4},{4,0},{1,5},{5,1},{2,6},{6,2},{3,7},{7,3},{8,12},{12,8},{9,1... | collective-permute-start | bytes 1572872 | tf_op jit(solution)/shard_map/ppermute | solution.py:39
  122.7 5.4 %copy-start.1 = (bf16[4,688,1024]{2,1,0:T(8,128)(2,1)S(1)}, bf16[4,688,1024]{2,1,0:T(8,128)(2,1)}, u32[]{:S(2)}) copy-start(bf16[4,688,1024]{2,1,0:T(8,128)(2,1)} %all-gather.2.cloned.1.call-done) | copy-start | bytes 16908292
  133.8 19.1 %collective-permute-start.18 = (bf16[32,16,344]{2,1,0:T(8,128)(2,1)S(1)}, bf16[32,16,344]{2,1,0:T(8,128)(2,1)S(1)}, u32[]{:S(2)}, u32[]{:S(2)}) collective-permute-start(bf16[32,16,344]{2,1,0:T(8,128)(2,1)S(1)} %pad_maximum_fusion.2), channel_id=1, source_target_pairs={{0,3},{1,0},{2,1},{3,2},{4,7},{5,4},{6,5},{7,6},{8,11},{9,8},{10,9... | collective-permute-start | bytes 1056776 | tf_op jit(solution)/shard_map/ppermute | solution.py:31
  135.9 17.0 %collective-permute-start.17 = (bf16[32,16,344]{2,1,0:T(8,128)(2,1)S(1)}, bf16[32,16,344]{2,1,0:T(8,128)(2,1)S(1)}, u32[]{:S(2)}, u32[]{:S(2)}) collective-permute-start(bf16[32,16,344]{2,1,0:T(8,128)(2,1)S(1)} %pad_maximum_fusion.2), channel_id=1, source_target_pairs={{0,2},{1,3},{2,0},{3,1},{4,6},{5,7},{6,4},{7,5},{8,10},{9,11},{10,... | collective-permute-start | bytes 1056776 | tf_op jit(solution)/shard_map/ppermute | solution.py:31
  136.7 19.9 %collective-permute-start.16 = (bf16[32,16,344]{2,1,0:T(8,128)(2,1)S(1)}, bf16[32,16,344]{2,1,0:T(8,128)(2,1)S(1)}, u32[]{:S(2)}, u32[]{:S(2)}) collective-permute-start(bf16[32,16,344]{2,1,0:T(8,128)(2,1)S(1)} %pad_maximum_fusion.2), channel_id=1, source_target_pairs={{0,1},{1,2},{2,3},{3,0},{4,5},{5,6},{6,7},{7,4},{8,9},{9,10},{10,1... | collective-permute-start | bytes 1056776 | tf_op jit(solution)/shard_map/ppermute | solution.py:31
  163.3 2.2 %collective-permute-start.23 = (bf16[256,1024]{1,0:T(8,128)(2,1)S(1)}, bf16[256,1024]{1,0:T(8,128)(2,1)S(1)}, u32[]{:S(2)}, u32[]{:S(2)}) collective-permute-start(bf16[256,1024]{1,0:T(8,128)(2,1)S(1)} %get-tuple-element.12), channel_id=1, source_target_pairs={{0,4},{4,0},{1,5},{5,1},{2,6},{6,2},{3,7},{7,3},{8,12},{12,8},{9,1... | collective-permute-start | bytes 1572872 | tf_op jit(solution)/shard_map/ppermute | solution.py:39
  163.7 2.6 %collective-permute-start.27 = (bf16[256,1024]{1,0:T(8,128)(2,1)S(1)}, bf16[256,1024]{1,0:T(8,128)(2,1)S(1)}, u32[]{:S(2)}, u32[]{:S(2)}) collective-permute-start(bf16[256,1024]{1,0:T(8,128)(2,1)S(1)} %get-tuple-element.10), channel_id=1, source_target_pairs={{0,4},{4,0},{1,5},{5,1},{2,6},{6,2},{3,7},{7,3},{8,12},{12,8},{9,1... | collective-permute-start | bytes 1572872 | tf_op jit(solution)/shard_map/ppermute | solution.py:39
  164.1 2.9 %collective-permute-start.25 = (bf16[256,1024]{1,0:T(8,128)(2,1)S(1)}, bf16[256,1024]{1,0:T(8,128)(2,1)S(1)}, u32[]{:S(2)}, u32[]{:S(2)}) collective-permute-start(bf16[256,1024]{1,0:T(8,128)(2,1)S(1)} %get-tuple-element.11), channel_id=1, source_target_pairs={{0,4},{4,0},{1,5},{5,1},{2,6},{6,2},{3,7},{7,3},{8,12},{12,8},{9,1... | collective-permute-start | bytes 1572872 | tf_op jit(solution)/shard_map/ppermute | solution.py:39
  164.2 8.3 %collective-permute-start.22 = (bf16[256,1024]{1,0:T(8,128)(2,1)S(1)}, bf16[256,1024]{1,0:T(8,128)(2,1)S(1)}, u32[]{:S(2)}, u32[]{:S(2)}) collective-permute-start(bf16[256,1024]{1,0:T(8,128)(2,1)S(1)} %get-tuple-element.9), channel_id=1, source_target_pairs={{0,4},{4,0},{1,5},{5,1},{2,6},{6,2},{3,7},{7,3},{8,12},{12,8},{9,1... | collective-permute-start | bytes 1572872 | tf_op jit(solution)/shard_map/ppermute | solution.py:39
  167.7 16.1 %collective-permute-start.28 = (bf16[256,1024]{1,0:T(8,128)(2,1)S(1)}, bf16[256,1024]{1,0:T(8,128)(2,1)S(1)}, u32[]{:S(2)}, u32[]{:S(2)}) collective-permute-start(bf16[256,1024]{1,0:T(8,128)(2,1)S(1)} %get-tuple-element.14), channel_id=1, source_target_pairs={{0,8},{4,36},{8,16},{12,44},{16,24},{20,52},{24,0},{28,60},{32,40}... | collective-permute-start | bytes 1572872 | tf_op jit(solution)/shard_map/ppermute | solution.py:35
  168.6 15.2 %collective-permute-start.26 = (bf16[256,1024]{1,0:T(8,128)(2,1)S(1)}, bf16[256,1024]{1,0:T(8,128)(2,1)S(1)}, u32[]{:S(2)}, u32[]{:S(2)}) collective-permute-start(bf16[256,1024]{1,0:T(8,128)(2,1)S(1)} %get-tuple-element.15), channel_id=1, source_target_pairs={{0,16},{4,68},{8,24},{12,76},{16,0},{20,84},{24,8},{28,92},{32,48}... | collective-permute-start | bytes 1572872 | tf_op jit(solution)/shard_map/ppermute | solution.py:35
  170.7 14.0 %collective-permute-start.24 = (bf16[256,1024]{1,0:T(8,128)(2,1)S(1)}, bf16[256,1024]{1,0:T(8,128)(2,1)S(1)}, u32[]{:S(2)}, u32[]{:S(2)}) collective-permute-start(bf16[256,1024]{1,0:T(8,128)(2,1)S(1)} %get-tuple-element.13), channel_id=1, source_target_pairs={{0,24},{4,100},{8,0},{12,108},{16,8},{20,116},{24,16},{28,124},{32... | collective-permute-start | bytes 1572872 | tf_op jit(solution)/shard_map/ppermute | solution.py:35
  185.2 6.3 %collective-permute-start.31 = (bf16[64,1024]{1,0:T(8,128)(2,1)S(1)}, bf16[64,1024]{1,0:T(8,128)(2,1)S(1)}, u32[]{:S(2)}, u32[]{:S(2)}) collective-permute-start(bf16[64,1024]{1,0:T(8,128)(2,1)S(1)} %get-tuple-element.17), channel_id=1, source_target_pairs={{0,32},{4,12},{8,40},{12,20},{16,48},{20,28},{24,56},{28,4},{32,64... | collective-permute-start | bytes 393224 | tf_op jit(solution)/shard_map/ppermute | solution.py:35
  186.3 6.6 %collective-permute-start.30 = (bf16[64,1024]{1,0:T(8,128)(2,1)S(1)}, bf16[64,1024]{1,0:T(8,128)(2,1)S(1)}, u32[]{:S(2)}, u32[]{:S(2)}) collective-permute-start(bf16[64,1024]{1,0:T(8,128)(2,1)S(1)} %get-tuple-element.18), channel_id=1, source_target_pairs={{0,64},{4,20},{8,72},{12,28},{16,80},{20,4},{24,88},{28,12},{32,96... | collective-permute-start | bytes 393224 | tf_op jit(solution)/shard_map/ppermute | solution.py:35
  186.8 7.0 %collective-permute-start.29 = (bf16[64,1024]{1,0:T(8,128)(2,1)S(1)}, bf16[64,1024]{1,0:T(8,128)(2,1)S(1)}, u32[]{:S(2)}, u32[]{:S(2)}) collective-permute-start(bf16[64,1024]{1,0:T(8,128)(2,1)S(1)} %get-tuple-element.16), channel_id=1, source_target_pairs={{0,96},{4,28},{8,104},{12,4},{16,112},{20,12},{24,120},{28,20},{32... | collective-permute-start | bytes 393224 | tf_op jit(solution)/shard_map/ppermute | solution.py:35
Sparse Core Ops, SparseCore 0:
  11.2 61.9 all-gather.1

commit v2 on v1

v2 whole, which is shorter than its diff:
```python
import jax
import jax.numpy as jnp
from jax import lax
from jax.experimental import pallas as pl
from jax.experimental.pallas import tpu as pltpu
from jax.sharding import Mesh, PartitionSpec as P

HD = 128
EPSILON = 1e-05
REP = ("z", "y", "c")
SIDE = 4
CHUNKS = 8
HBM = pl.BlockSpec(memory_space=pltpu.HBM)
VM = pl.BlockSpec(memory_space=pltpu.VMEM)
SM = pl.BlockSpec(memory_space=pltpu.SMEM)


def params(megabytes):
    return pltpu.CompilerParams(vmem_limit_bytes=megabytes * 1024 * 1024)


def in_hbm(value):
    return pltpu.with_memory_space_constraint(value, pltpu.HBM)


def x_ring(shift):
    return [(i, (i + shift) % SIDE) for i in range(SIDE)]


def chip_ring(shift, first):
    pairs = []
    for z in range(SIDE):
        for y in range(SIDE):
            for c in range(2):
                if (c == 0) == first:
                    to = (((z + shift) % SIDE) * SIDE + y) * 2 + c
                else:
                    to = (z * SIDE + (y + shift) % SIDE) * 2 + c
                pairs.append(((z * SIDE + y) * 2 + c, to))
    return pairs


def along_x(value, shift):
    return lax.ppermute(value, "x", x_ring(shift))


def along_chips(value, shift, first):
    return lax.ppermute(value, REP, chip_ring(shift, first))


def other_core(value):
    return lax.ppermute(value, "c", [(0, 1), (1, 0)])


def attend_kernel(table, lengths, place, query, new_kv, hidden, gain, pool, weight, *refs):
    outs = refs[:SIDE]
    pages, weights, queries, pairs, homes, gains, by_head, heads, rows, page_sem, weight_sem, sem = refs[
        SIDE:
    ]
    page_rows = pool.shape[1]
    span_rows = 2 * page_rows
    requests, width = hidden.shape
    group = width // HD
    block = requests // SIDE
    many = HD // group
    scale = HD ** (-0.5)
    share = pool.shape[0] // CHUNKS
    x = place[0]
    home = place[1] * requests

    def page_copy(n):
        part = pl.ds(n * share, share)
        return pltpu.make_async_copy(pool.at[part], pages.at[part], page_sem.at[n])

    def weight_copy(n):
        return pltpu.make_async_copy(
            weight.at[:, pl.ds(n * width, width)], weights.at[n], weight_sem.at[n]
        )

    small = [
        pltpu.make_async_copy(source, into, sem.at[n])
        for n, (source, into) in enumerate(
            ((query, queries), (new_kv, pairs), (hidden, homes), (gain, gains))
        )
    ]
    for copy in small:
        copy.start()
    for n in range(CHUNKS):
        page_copy(n).start()
    for n in range(SIDE):
        weight_copy(n).start()
    for copy in small:
        copy.wait()

    row = lax.broadcasted_iota(jnp.int32, (span_rows, HD), 0)
    is_key = row % 2 == 0
    position = row // 2
    owner = lax.broadcasted_iota(jnp.int32, (HD, HD), 1) // group
    lane = lax.broadcasted_iota(jnp.int32, (1, HD), 1) // group

    def one_group(g):
        r0 = g * many
        for h in range(group):
            by_head[g, pl.ds(h, many, stride=group), :] = queries[
                r0 : r0 + many, h * HD : (h + 1) * HD
            ].astype(jnp.float32)
        q_t = jnp.transpose(by_head[g])
        sides = jnp.concatenate(
            [jnp.where(owner == i, q_t, 0.0).astype(jnp.bfloat16) for i in range(many)], axis=0
        )
        span = jnp.zeros((1, HD), jnp.int32)
        for i in range(many):
            span = jnp.where(lane == i, lengths[home + r0 + i], span)
        if g == 0:
            for n in range(CHUNKS):
                page_copy(n).wait()

        def both(i):
            r = r0 + i
            return jnp.concatenate([pages[table[0, r]], pages[table[1, r]]], axis=0)

        cached = jnp.concatenate([both(i) for i in range(many)], axis=1)
        scores = jnp.dot(cached, sides, preferred_element_type=jnp.float32) * scale
        fresh = [pairs[r0 + i].astype(jnp.float32) for i in range(many)]
        own = jnp.dot(
            jnp.concatenate(fresh, axis=1).astype(jnp.bfloat16),
            sides,
            preferred_element_type=jnp.float32,
        )[0:1] * scale
        valid = is_key & (position < span)
        peak = jnp.maximum(
            jnp.max(jnp.where(valid, scores, -jnp.inf), axis=0, keepdims=True), own
        )
        w = jnp.where(valid, jnp.exp(scores - peak), 0.0)
        w_own = jnp.exp(own - peak)
        total = jnp.sum(w, axis=0, keepdims=True) + w_own
        line = lax.broadcasted_iota(jnp.int32, (HD, HD), 0)
        w = jnp.transpose(pltpu.roll(w, 1, 0))
        last = jnp.transpose(jnp.where(line == 0, w_own, total))
        w_own = last[:, 0:1].astype(jnp.bfloat16).astype(jnp.float32)
        total = last[:, 1:2]
        for i in range(many):
            at = slice(i * group, (i + 1) * group)
            mixed = jnp.dot(w[at].astype(jnp.bfloat16), both(i), preferred_element_type=jnp.float32)
            heads[pl.ds((r0 + i) * group, group), :] = (mixed + w_own[at] * fresh[i][1:2]) / total[at]

    for g in range(requests // many):
        one_group(g)
    attention = jnp.concatenate(
        [heads[pl.ds(h, requests, stride=group), :].astype(jnp.bfloat16) for h in range(group)],
        axis=1,
    )
    for n in range(SIDE):
        weight_copy(n).wait()
        part = jnp.dot(attention, weights[n], preferred_element_type=jnp.float32)
        part = part + jnp.where(x == n, homes[...].astype(jnp.float32), 0.0)
        part = part.astype(jnp.bfloat16)
        for t in range(SIDE):
            rows[t, :, n * width : (n + 1) * width] = part[t * block : (t + 1) * block]
    high = gains[...].astype(jnp.bfloat16).astype(jnp.float32)
    extra = jnp.concatenate([high, gains[...] - high], axis=0).astype(jnp.bfloat16)
    for s in range(SIDE):
        outs[s][:, : SIDE * width] = rows[(x + s) % SIDE]
        outs[s][:, SIDE * width :] = extra


def attend_project(table, lengths, place, query, new_kv, hidden, gain, pool, weight):
    requests, width = hidden.shape
    block = requests // SIDE
    group = width // HD
    groups = requests * group // HD
    page_rows = pool.shape[1] * pool.shape[2]
    out = jax.ShapeDtypeStruct((block, SIDE * width + HD), jnp.bfloat16)
    return pl.pallas_call(
        attend_kernel,
        out_shape=[out] * SIDE,
        in_specs=[SM, SM, SM] + [HBM] * 6,
        out_specs=[VM] * SIDE,
        scratch_shapes=[
            pltpu.VMEM((pool.shape[0], page_rows, HD), jnp.bfloat16),
            pltpu.VMEM((SIDE, weight.shape[0], width), jnp.bfloat16),
            pltpu.VMEM(query.shape, jnp.bfloat16),
            pltpu.VMEM(new_kv.shape, jnp.bfloat16),
            pltpu.VMEM(hidden.shape, jnp.bfloat16),
            pltpu.VMEM((group, HD), jnp.float32),
            pltpu.VMEM((groups, HD, HD), jnp.float32),
            pltpu.VMEM((requests * group, HD), jnp.float32),
            pltpu.VMEM((SIDE, block, SIDE * width), jnp.bfloat16),
            pltpu.SemaphoreType.DMA((CHUNKS,)),
            pltpu.SemaphoreType.DMA((SIDE,)),
            pltpu.SemaphoreType.DMA((4,)),
        ],
        compiler_params=params(36),
        name="attend_project",
    )(
        table,
        lengths,
        place,
        in_hbm(query),
        in_hbm(new_kv),
        in_hbm(hidden),
        in_hbm(gain.reshape(group, HD)),
        in_hbm(pool.reshape(pool.shape[0], page_rows, HD)),
        in_hbm(weight),
    )


def norm_kernel(place, *refs):
    parts, (normed, *pieces, gains, kept) = refs[:SIDE], refs[SIDE:]
    x = place[0]
    width = kept.shape[2]
    lines = width // HD
    for s in range(SIDE):
        extra = parts[s][:, SIDE * width :].astype(jnp.float32)
        gains[(x + SIDE - s) % SIDE] = extra[:lines] + extra[lines:]
    square = 0.0
    residual = []
    for n in range(SIDE):
        at = slice(n * width, (n + 1) * width)
        value = sum(p[:, at].astype(jnp.float32) for p in parts)
        square = square + jnp.sum(value * value, axis=1, keepdims=True)
        kept[n] = value.astype(jnp.bfloat16)
        residual.append(value)
    factor = lax.rsqrt(square / (SIDE * width) + EPSILON)
    for n in range(SIDE):
        gain = gains[n]
        for j in range(lines):
            value = residual[n][:, j * HD : (j + 1) * HD] * factor * gain[j : j + 1]
            normed[:, n * width + j * HD : n * width + (j + 1) * HD] = value.astype(jnp.bfloat16)
    for s in range(SIDE):
        pieces[s][...] = kept[(x + s) % SIDE]


def normalise(place, parts, width):
    block = parts[0].shape[0]
    piece = jax.ShapeDtypeStruct((block, width), jnp.bfloat16)
    return pl.pallas_call(
        norm_kernel,
        out_shape=[jax.ShapeDtypeStruct((block, SIDE * width), jnp.bfloat16)] + [piece] * SIDE,
        in_specs=[SM] + [VM] * SIDE,
        out_specs=[VM] * (SIDE + 1),
        scratch_shapes=[
            pltpu.VMEM((SIDE, width // HD, HD), jnp.float32),
            pltpu.VMEM((SIDE, block, width), jnp.bfloat16),
        ],
        compiler_params=params(16),
        name="normalise",
    )(place, *parts)


def join_kernel(*refs):
    parts, out = refs[:-1], refs[-1]
    rows = parts[0].shape[0]
    for i, part in enumerate(parts):
        out[i * rows : (i + 1) * rows] = part[...]


def join(parts):
    rows, width = parts[0].shape
    return pl.pallas_call(
        join_kernel,
        out_shape=jax.ShapeDtypeStruct((len(parts) * rows, width), parts[0].dtype),
        in_specs=[VM] * len(parts),
        out_specs=VM,
        compiler_params=params(4),
        name="join",
    )(*parts)


def split_kernel(both, gate, up, sem):
    copies = [
        pltpu.make_async_copy(both.at[k], into, sem.at[k]) for k, into in enumerate((gate, up))
    ]
    for c in copies:
        c.start()
    for c in copies:
        c.wait()


def split(both):
    half = jax.ShapeDtypeStruct(both.shape[1:], both.dtype)
    return pl.pallas_call(
        split_kernel,
        out_shape=[half, half],
        in_specs=[HBM],
        out_specs=[VM, VM],
        scratch_shapes=[pltpu.SemaphoreType.DMA((2,))],
        compiler_params=params(4),
        name="split",
    )(in_hbm(both))


def gate_up_kernel(place, source, *refs):
    blocks, sides, out = refs[: 2 * SIDE], refs[2 * SIDE : 4 * SIDE], refs[4 * SIDE]
    inputs, turned, weights, values, moved, in_sem, weight_sem = refs[4 * SIDE + 1 :]
    x = place[0]
    rows = blocks[0].shape[0]
    width = turned.shape[1]
    units = out.shape[1]
    in_copies = [
        pltpu.make_async_copy(b, inputs.at[pl.ds(i * rows, rows)], in_sem.at[i])
        for i, b in enumerate(blocks)
    ]
    weight_copies = [
        pltpu.make_async_copy(v, weights.at[i], weight_sem.at[i]) for i, v in enumerate(sides)
    ]
    for c in in_copies + weight_copies:
        c.start()
    for p in range(SIDE):
        in_copies[2 * p].wait()
        in_copies[2 * p + 1].wait()
        at = slice(2 * p * rows, 2 * (p + 1) * rows)
        for t in range(SIDE):
            turned[t, :, at] = jnp.transpose(inputs[at, t * width : (t + 1) * width])
    sums = [0.0, 0.0]
    for s in range(SIDE):
        these = turned[(x + SIDE - s) % SIDE]
        for k in range(2):
            weight_copies[2 * s + k].wait()
            sums[k] = sums[k] + jnp.dot(
                weights[2 * s + k], these, preferred_element_type=jnp.float32
            )
    value = jax.nn.silu(sums[0]) * sums[1]
    spare = values.shape[1] - units
    value = jnp.concatenate([value, jnp.zeros((spare, value.shape[1]), jnp.float32)], axis=0)
    values[...] = jnp.transpose(value)
    slots = source.shape[0]
    block = values.shape[0] // slots
    for d in range(slots):
        moved[d : d + 1] = values[pl.ds(source[d] * block + block - 1, 1)]
    for d in range(slots):
        values[(d + 1) * block - 1 : (d + 1) * block] = moved[d : d + 1]
    out[...] = values[:, :units].astype(jnp.bfloat16)


def gate_up_act(place, source, blocks, sides):
    rows, features = blocks[0].shape
    rows = rows * len(blocks)
    units, width = sides[0].shape
    padded = -(-units // HD) * HD
    return pl.pallas_call(
        gate_up_kernel,
        out_shape=jax.ShapeDtypeStruct((rows, units), jnp.bfloat16),
        in_specs=[SM, SM] + [HBM] * (4 * SIDE),
        out_specs=VM,
        scratch_shapes=[
            pltpu.VMEM((rows, features), jnp.bfloat16),
            pltpu.VMEM((SIDE, width, rows), jnp.bfloat16),
            pltpu.VMEM((2 * SIDE, units, width), jnp.bfloat16),
            pltpu.VMEM((rows, padded), jnp.float32),
            pltpu.VMEM((source.shape[0], padded), jnp.float32),
            pltpu.SemaphoreType.DMA((2 * SIDE,)),
            pltpu.SemaphoreType.DMA((2 * SIDE,)),
        ],
        compiler_params=params(26),
        name="gate_up_act",
    )(place, source, *map(in_hbm, blocks), *map(in_hbm, sides))


def down_kernel(base, place, slot, weight, *refs):
    acts, homes, outs = refs[:SIDE], refs[SIDE : 2 * SIDE], refs[2 * SIDE : 3 * SIDE]
    inputs, sem = refs[3 * SIDE :]
    x = place[0]
    rows = inputs.shape[1]
    block = homes[0].shape[0]

    def copy(s):
        return pltpu.make_async_copy(acts[s].at[pl.ds(base * block, rows)], inputs.at[s], sem.at[s])

    order = (0, 1, 3, 2)
    for s in order:
        copy(s).start()
    line = lax.broadcasted_iota(jnp.int32, homes[0].shape, 0)
    for s in order:
        from_x = (x + SIDE - s) % SIDE
        copy(s).wait()
        values = jnp.dot(inputs[s], weight[...], preferred_element_type=jnp.float32)
        home = homes[s][...].astype(jnp.float32)
        moves = (line == block - 1) & (from_x == SIDE - 1)
        for d in range(rows // block):
            value = values[d * block : (d + 1) * block]
            adds = moves & (slot[0] == base + d)
            if base + d == 0:
                adds = adds | jnp.logical_not(moves)
            value = value + jnp.where(adds, home, 0.0)
            outs[d // SIDE][d % SIDE, from_x] = value.astype(jnp.bfloat16)


def down(base, place, slot, weight, acts, homes):
    block, width = homes[0].shape
    rows = acts[0].shape[0] // 2
    out = jax.ShapeDtypeStruct((SIDE, SIDE, block, width), jnp.bfloat16)
    return pl.pallas_call(
        lambda *refs: down_kernel(base, *refs),
        out_shape=[out] * SIDE,
        in_specs=[SM, SM, VM] + [HBM] * SIDE + [VM] * SIDE,
        out_specs=[VM] * SIDE,
        scratch_shapes=[
            pltpu.VMEM((SIDE, rows, weight.shape[0]), jnp.bfloat16),
            pltpu.SemaphoreType.DMA((SIDE,)),
        ],
        compiler_params=params(24),
        name="down",
    )(place, slot, weight, *map(in_hbm, acts), *homes)


def slot_sources(dest):
    z, y, c = (lax.axis_index(a) for a in REP)
    other, second, first = jnp.meshgrid(
        jnp.arange(2), jnp.arange(SIDE), jnp.arange(SIDE), indexing="ij"
    )
    core = (c + other) % 2
    slot_z = (z - jnp.where(core == 0, first, second)) % SIDE
    slot_y = (y - jnp.where(core == 0, second, first)) % SIDE
    group = ((slot_z * SIDE + slot_y) * 2 + core).reshape(-1)
    target = jnp.sum(
        jnp.where(group[:, None] == jnp.arange(dest.shape[0])[None, :], dest[None, :], 0), axis=1
    )
    hit = group[:, None] == target[None, :]
    return jnp.sum(jnp.where(hit, jnp.arange(group.shape[0])[None, :], 0), axis=1)


def add(values):
    return sum(v.astype(jnp.float32) for v in values).astype(jnp.bfloat16)


def local(
    hidden_in,
    query,
    new_kv,
    pool,
    page_table,
    lengths,
    dest,
    out_weight,
    norm_gain,
    gate_up,
    down_weight,
):
    rows_here, width = hidden_in.shape
    x = lax.axis_index("x")
    place = jnp.stack([x, lax.axis_index(REP)]).astype(jnp.int32)

    gate, up = split(jnp.transpose(gate_up, (1, 2, 0)))
    gate_1, up_3 = along_x(gate, 1), along_x(up, 3)

    source = slot_sources(dest).astype(jnp.int32)
    slots = source.shape[0]
    identity = jnp.arange(slots, dtype=jnp.int32)
    slot = jnp.sum(jnp.where(source == 0, identity, 0))[None]
    source = jnp.where(x == SIDE - 1, source, identity)

    parts = attend_project(
        page_table.T, lengths, place, query, new_kv, hidden_in, norm_gain, pool, out_weight
    )
    parts = [parts[0]] + [along_x(parts[s], s) for s in (1, 2, 3)]
    *parts, gate_1, up_3 = lax.optimization_barrier((*parts, gate_1, up_3))
    gate_2, up_2 = along_x(gate_1, 1), along_x(up_3, 3)
    normed, *pieces = normalise(place, parts, width)

    first = join([normed] + [along_chips(normed, s, True) for s in (1, 2, 3)])
    first, gate, up, gate_2, up_2 = lax.optimization_barrier((first, gate, up, gate_2, up_2))
    gate_3, up_1 = along_x(gate, 3), along_x(up, 1)
    sides = (gate, up, gate_1, up_1, gate_2, up_2, gate_3, up_3)
    second = [first] + [along_chips(first, s, False) for s in (1, 2, 3)]
    blocks = second + [other_core(v) for v in second]
    homes = [pieces[0]] + [along_x(pieces[s], s) for s in (1, 2, 3)]
    activated = gate_up_act(place, source, blocks, sides)
    activated, *homes = lax.optimization_barrier((activated, *homes))
    acts = [activated] + [along_x(activated, s) for s in (1, 2, 3)]

    theirs = down(slots // 2, place, slot, down_weight, acts, homes)
    theirs = [other_core(v) for v in theirs]
    mine = down(0, place, slot, down_weight, acts, homes)
    summed = [add(pair) for pair in zip(mine, theirs)]
    total = add([summed[0]] + [along_chips(summed[s], -s, False) for s in (1, 2, 3)])
    out = add([total[0]] + [along_chips(total[s], -s, True) for s in (1, 2, 3)])
    return out.reshape(rows_here, width)


def solution(mesh):
    chips = Mesh(mesh.devices.reshape(SIDE, SIDE, 2, SIDE), ("z", "y", "c", "x"))
    return jax.shard_map(
        local,
        mesh=chips,
        in_specs=(
            P(REP, "x"),
            P(REP, "x"),
            P(REP, None, "x"),
            P(REP, None, None, "x"),
            P(REP, None),
            P(),
            P(),
            P("x", None),
            P("x"),
            P("x", None, REP),
            P(REP, "x"),
        ),
        out_specs=P(REP, "x"),
        check_vma=False,
    )
```

time: 202 us -> 149 us (0.74)
  local copies, waits for them, and re-layouts: 60.8 us -> 2.55 us
  Pallas kernels: 0 us -> 33.6 us
  matrix products: 24.9 us -> 0 us
  between operations: 14 us -> 0.27 us
  waiting for transfers between devices: 57.5 us -> 67.1 us
  starting transfers between devices: 37.5 us -> 42.3 us
  other arithmetic: 6.64 us -> 2.89 us
    gather x6 -> x0, local copies, waits for them, and re-layouts: 36.1 us -> none  [the longest x2 32.3 us: local(): cache_rows = pool[page_table].reshape(rows_here, -1, 2, pool.shape[3])]
    pallas_call x0 -> x7, Pallas kernels: none -> 33.6 us  [the longest x1 15 us: attend_project(): pl.pallas_call(attend_kernel, out_shape=[out] * SIDE, in_specs=[SM, SM, S...]
    dot_general x9 -> x0, matrix products: 24.9 us -> none  [the longest x4 9.68 us: local(): lax.dot_general(every[:, t * width:(t + 1) * width], weights[t], (((1,),...]
    dot_general x1 -> x0, local copies, waits for them, and re-layouts: 12.1 us -> none  [local(): jnp.dot(attention, out_weight, preferred_element_type=jnp.float32)]
    ppermute x12, waiting for transfers between devices: 25.5 us -> 36.1 us  [along_chips(): return lax.ppermute(value, REP, chip_ring(shift, first))]
    ppermute x12 -> x15, starting transfers between devices: 14.7 us -> 20.8 us  [along_x(): return lax.ppermute(value, 'x', x_ring(shift))]
    unnamed x30, local copies, waits for them, and re-layouts: 7.09 us -> 2.18 us
    ppermute x8, waiting for transfers between devices: 2.4 us -> 0.02 us  [other_core(): return lax.ppermute(value, 'c', [(0, 1), (1, 0)])]
  transfers between devices with their start and end apart: 33 -> 35, of which waited for: 16 -> 18; matrix products, arithmetic and copies ran while one was open for 36% -> 1% of each run, Pallas kernels for 0% -> 19%
where the time goes in v2:
time: 149 us
  waiting for transfers between devices  67.1 us (45%)
  starting transfers between devices  42.3 us (28%)
  Pallas kernels  33.6 us (23%)
  other arithmetic  2.89 us (2%)
  local copies, waits for them, and re-layouts  2.55 us (2%)
    ppermute x12, waiting for transfers between devices, along_chips(): return lax.ppermute(value, REP, chip_ring(shift, first))  36.1 us
    ppermute x15, waiting for transfers between devices, along_x(): return lax.ppermute(value, 'x', x_ring(shift))  31 us
    ppermute x15, starting transfers between devices, along_x(): return lax.ppermute(value, 'x', x_ring(shift))  20.8 us
    ppermute x12, starting transfers between devices, along_chips(): return lax.ppermute(value, REP, chip_ring(shift, first))  19.3 us
    pallas_call x1, Pallas kernels, attend_project(): pl.pallas_call(attend_kernel, out_shape=[out] * SIDE, in_specs=[SM, SM, S...  15 us
    pallas_call x1, Pallas kernels, gate_up_act(): pl.pallas_call(gate_up_kernel, out_shape=jax.ShapeDtypeStruct((rows, unit...  8.68 us
    pallas_call x2, Pallas kernels, down(): pl.pallas_call(lambda *refs: down_kernel(base, *refs), out_shape=[out] *...  7.79 us
  transfers between devices with their start and end apart: 35, of which 18 were waited for; matrix products, arithmetic and copies ran while one was open for 1% of the time, Pallas kernels for 19%

profile of v2, /device:TPU:0, one launch (start us, length us, event | category | flops | bytes accessed | tf_op | source)
XLA Modules:
  0.0 148.6 jit_solution(18114269696806503322)
XLA Ops:
  0.0 1.3 split.1
  1.4 1.6 %collective-permute-start.3 = (bf16[344,1024]{1,0:T(8,128)(2,1)S(1)}, bf16[344,1024]{1,0:T(8,128)(2,1)S(1)}, u32[]{:S(2)}, u32[]{:S(2)}) collective-permute-start(bf16[344,1024]{1,0:T(8,128)(2,1)S(1)} %get-tuple-element.54.refs_8_), channel_id=1, source_target_pairs={{0,1},{1,2},{2,3},{3,0},{4,5},{5,6},{6,7},{7,4},{8,9},{9,10},{10,1... | collective-permute-start | bytes 2113544 | tf_op jit(solution)/shard_map/ppermute | solution.py:44
  3.0 1.7 %collective-permute-start.4 = (bf16[344,1024]{1,0:T(8,128)(2,1)S(1)}, bf16[344,1024]{1,0:T(8,128)(2,1)}, u32[]{:S(2)}, u32[]{:S(2)}) collective-permute-start(bf16[344,1024]{1,0:T(8,128)(2,1)S(1)} %get-tuple-element.55.refs_9_), channel_id=1, source_target_pairs={{0,3},{1,0},{2,1},{3,2},{4,7},{5,4},{6,5},{7,6},{8,11},{9,8},{10,9... | collective-permute-start | bytes 2113544 | tf_op jit(solution)/shard_map/ppermute | solution.py:44
  4.7 0.7 copy-done.5
  5.4 0.7 copy-done.6
  6.1 15.0 %attend_project.1 = (bf16[16,4224]{1,0:T(8,128)(2,1)S(1)}, bf16[16,4224]{1,0:T(8,128)(2,1)S(1)}, bf16[16,4224]{1,0:T(8,128)(2,1)S(1)}, bf16[16,4224]{1,0:T(8,128)(2,1)S(1)}) custom-call(s32[2,64]{1,0:T(2,128)S(1)} %bitcast.19, s32[2048]{0:T(1024)S(1)} %copy-done.5, s32[2]{0:T(128)S(1)} %pad_add_fusion.place.refs_0_, bf16[64,1024]{1,0:T(8,128)(2,1)} %query.1, ...), custom_call_target="tpu_custom_call" | custom-call | tf_op jit(solution)/shard_map/attend_project/pallas_call | solution.py:174
  21.6 2.7 %collective-permute-start.1 = (bf16[16,4224]{1,0:T(8,128)(2,1)S(1)}, bf16[16,4224]{1,0:T(8,128)(2,1)S(1)}, u32[]{:S(2)}, u32[]{:S(2)}) collective-permute-start(bf16[16,4224]{1,0:T(8,128)(2,1)S(1)} %get-tuple-element.42), channel_id=1, source_target_pairs={{0,2},{1,3},{2,0},{3,1},{4,6},{5,7},{6,4},{7,5},{8,10},{9,11},{10,... | collective-permute-start | bytes 405512 | tf_op jit(solution)/shard_map/ppermute | solution.py:44
  24.3 1.4 collective-permute-start.2
  25.8 4.3 %collective-permute-done.refs_1_ = bf16[16,4224]{1,0:T(8,128)(2,1)S(1)} collective-permute-done((bf16[16,4224]{1,0:T(8,128)(2,1)S(1)}, bf16[16,4224]{1,0:T(8,128)(2,1)S(1)}, u32[]{:S(2)}, u32[]{:S(2)}) %collective-permute-start) | collective-permute-done | bytes 135200 | tf_op jit(solution)/shard_map/ppermute | solution.py:44
  30.7 1.4 collective-permute-start.8
  32.0 1.9 %collective-permute-start.9 = (bf16[344,1024]{1,0:T(8,128)(2,1)}, bf16[344,1024]{1,0:T(8,128)(2,1)S(1)}, u32[]{:S(2)}, u32[]{:S(2)}) collective-permute-start(bf16[344,1024]{1,0:T(8,128)(2,1)} %collective-permute-done.4.refs_15_), channel_id=1, source_target_pairs={{0,3},{1,0},{2,1},{3,2},{4,7},{5,4},{6,5},{7,6},{8,11},{9,8},{10,9... | collective-permute-start | bytes 2113544 | tf_op jit(solution)/shard_map/ppermute | solution.py:44
  34.0 0.7 normalise.1
  34.7 4.2 %collective-permute-start.7 = (bf16[16,4096]{1,0:T(8,128)(2,1)S(1)}, bf16[16,4096]{1,0:T(8,128)(2,1)S(1)}, u32[]{:S(2)}, u32[]{:S(2)}) collective-permute-start(bf16[16,4096]{1,0:T(8,128)(2,1)S(1)} %get-tuple-element.50.refs_0_), channel_id=1, source_target_pairs={{0,96},{4,28},{8,104},{12,4},{16,112},{20,12},{24,120},{28,20},{32... | collective-permute-start | bytes 393224 | tf_op jit(solution)/shard_map/ppermute | solution.py:48
  38.9 1.3 collective-permute-start.5
  40.2 2.7 %collective-permute-done.7.refs_3_ = bf16[16,4096]{1,0:T(8,128)(2,1)S(1)} collective-permute-done((bf16[16,4096]{1,0:T(8,128)(2,1)S(1)}, bf16[16,4096]{1,0:T(8,128)(2,1)S(1)}, u32[]{:S(2)}, u32[]{:S(2)}) %collective-permute-start.7) | collective-permute-done | bytes 131104 | tf_op jit(solution)/shard_map/ppermute | solution.py:48
  42.8 2.7 %collective-permute-done.6.refs_2_ = bf16[16,4096]{1,0:T(8,128)(2,1)S(1)} collective-permute-done((bf16[16,4096]{1,0:T(8,128)(2,1)S(1)}, bf16[16,4096]{1,0:T(8,128)(2,1)S(1)}, u32[]{:S(2)}, u32[]{:S(2)}) %collective-permute-start.6) | collective-permute-done | bytes 131104 | tf_op jit(solution)/shard_map/ppermute | solution.py:48
  45.5 1.0 collective-permute-done.5.refs_1_
  46.5 1.8 %collective-permute-done.8.refs_12_ = bf16[344,1024]{1,0:T(8,128)(2,1)S(1)} collective-permute-done((bf16[344,1024]{1,0:T(8,128)(2,1)S(1)}, bf16[344,1024]{1,0:T(8,128)(2,1)S(1)}, u32[]{:S(2)}, u32[]{:S(2)}) %collective-permute-start.8) | collective-permute-done | bytes 704544 | tf_op jit(solution)/shard_map/ppermute | solution.py:44
  48.8 3.0 %collective-permute-start.12 = (bf16[64,4096]{1,0:T(8,128)(2,1)S(1)}, bf16[64,4096]{1,0:T(8,128)(2,1)}, u32[]{:S(2)}, u32[]{:S(2)}) collective-permute-start(bf16[64,4096]{1,0:T(8,128)(2,1)S(1)} %join.1.refs_0_), channel_id=1, source_target_pairs={{0,24},{4,100},{8,0},{12,108},{16,8},{20,116},{24,16},{28,124},{32... | collective-permute-start | bytes 1572872 | tf_op jit(solution)/shard_map/ppermute | solution.py:48
  51.8 0.6 collective-permute-start.11
  52.4 1.0 collective-permute-start.10
  53.4 3.0 %collective-permute-start.18 = (bf16[344,1024]{1,0:T(8,128)(2,1)S(1)}, bf16[344,1024]{1,0:T(8,128)(2,1)}, u32[]{:S(2)}, u32[]{:S(2)}) collective-permute-start(bf16[344,1024]{1,0:T(8,128)(2,1)S(1)} %get-tuple-element.54.refs_8_), channel_id=1, source_target_pairs={{0,3},{1,0},{2,1},{3,2},{4,7},{5,4},{6,5},{7,6},{8,11},{9,8},{10,9... | collective-permute-start | bytes 2113544 | tf_op jit(solution)/shard_map/ppermute | solution.py:44
  56.5 7.6 %collective-permute-done.12.refs_3_ = bf16[64,4096]{1,0:T(8,128)(2,1)} collective-permute-done((bf16[64,4096]{1,0:T(8,128)(2,1)S(1)}, bf16[64,4096]{1,0:T(8,128)(2,1)}, u32[]{:S(2)}, u32[]{:S(2)}) %collective-permute-start.12) | collective-permute-done | bytes 524320 | tf_op jit(solution)/shard_map/ppermute | solution.py:48
  64.1 0.7 collective-permute-start.16
  65.4 2.8 %collective-permute-done.10.refs_1_ = bf16[64,4096]{1,0:T(8,128)(2,1)} collective-permute-done((bf16[64,4096]{1,0:T(8,128)(2,1)S(1)}, bf16[64,4096]{1,0:T(8,128)(2,1)}, u32[]{:S(2)}, u32[]{:S(2)}) %collective-permute-start.10) | collective-permute-done | bytes 524320 | tf_op jit(solution)/shard_map/ppermute | solution.py:48
  68.7 3.2 %collective-permute-done.18.refs_14_ = bf16[344,1024]{1,0:T(8,128)(2,1)} collective-permute-done((bf16[344,1024]{1,0:T(8,128)(2,1)S(1)}, bf16[344,1024]{1,0:T(8,128)(2,1)}, u32[]{:S(2)}, u32[]{:S(2)}) %collective-permute-start.18) | collective-permute-done | bytes 704544 | tf_op jit(solution)/shard_map/ppermute | solution.py:44
  71.9 0.7 collective-permute-start.19
  72.6 2.9 %collective-permute-done.17.refs_11_ = bf16[344,1024]{1,0:T(8,128)(2,1)} collective-permute-done((bf16[344,1024]{1,0:T(8,128)(2,1)S(1)}, bf16[344,1024]{1,0:T(8,128)(2,1)}, u32[]{:S(2)}, u32[]{:S(2)}) %collective-permute-start.17) | collective-permute-done | bytes 704544 | tf_op jit(solution)/shard_map/ppermute | solution.py:44
  75.5 1.7 %collective-permute-start.20 = (bf16[16,1024]{1,0:T(8,128)(2,1)S(1)}, bf16[16,1024]{1,0:T(8,128)(2,1)S(1)}, u32[]{:S(2)}, u32[]{:S(2)}) collective-permute-start(bf16[16,1024]{1,0:T(8,128)(2,1)S(1)} %get-tuple-element.60), channel_id=1, source_target_pairs={{0,2},{1,3},{2,0},{3,1},{4,6},{5,7},{6,4},{7,5},{8,10},{9,11},{10,... | collective-permute-start | bytes 98312 | tf_op jit(solution)/shard_map/ppermute | solution.py:44
  77.3 0.6 broadcast_select_fusion
  77.9 8.7 %gate_up_act.1.refs_3_ = bf16[512,344]{1,0:T(8,128)(2,1)S(1)} custom-call(s32[2]{0:T(128)S(1)} %pad_add_fusion.place.refs_0_, s32[32]{0:T(128)S(1)} %get-tuple-element.78.source, bf16[64,4096]{1,0:T(8,128)(2,1)} %copy-done.2, bf16[64,4096]{1,0:T(8,128)(2,1)} %collective-permute-done.10.refs_1_, bf16[64,4096]{1,0:T(8,128)(2,1)} %collective-permute-done.11.refs_2_, ...), custom_call_target="tpu_custom_call" | custom-call | tf_op jit(solution)/shard_map/gate_up_act/pallas_call | solution.py:341
  86.6 2.4 %collective-permute-start.24 = (bf16[512,344]{1,0:T(8,128)(2,1)S(1)}, bf16[512,344]{1,0:T(8,128)(2,1)S(1)}, u32[]{:S(2)}, u32[]{:S(2)}) collective-permute-start(bf16[512,344]{1,0:T(8,128)(2,1)S(1)} %gate_up_act.1.refs_3_), channel_id=1, source_target_pairs={{0,3},{1,0},{2,1},{3,2},{4,7},{5,4},{6,5},{7,6},{8,11},{9,8},{10,9... | collective-permute-start | bytes 1056776 | tf_op jit(solution)/shard_map/ppermute | solution.py:44
  89.1 1.7 %collective-permute-start.23 = (bf16[512,344]{1,0:T(8,128)(2,1)S(1)}, bf16[512,344]{1,0:T(8,128)(2,1)S(1)}, u32[]{:S(2)}, u32[]{:S(2)}) collective-permute-start(bf16[512,344]{1,0:T(8,128)(2,1)S(1)} %gate_up_act.1.refs_3_), channel_id=1, source_target_pairs={{0,2},{1,3},{2,0},{3,1},{4,6},{5,7},{6,4},{7,5},{8,10},{9,11},{10,... | collective-permute-start | bytes 1056776 | tf_op jit(solution)/shard_map/ppermute | solution.py:44
  90.7 14.0 %collective-permute-done.24.refs_6_ = bf16[512,344]{1,0:T(8,128)(2,1)S(1)} collective-permute-done((bf16[512,344]{1,0:T(8,128)(2,1)S(1)}, bf16[512,344]{1,0:T(8,128)(2,1)S(1)}, u32[]{:S(2)}, u32[]{:S(2)}) %collective-permute-start.24) | collective-permute-done | bytes 352288 | tf_op jit(solution)/shard_map/ppermute | solution.py:44
  104.7 3.7 %collective-permute-done.22.refs_4_ = bf16[512,344]{1,0:T(8,128)(2,1)S(1)} collective-permute-done((bf16[512,344]{1,0:T(8,128)(2,1)S(1)}, bf16[512,344]{1,0:T(8,128)(2,1)S(1)}, u32[]{:S(2)}, u32[]{:S(2)}) %collective-permute-start.22) | collective-permute-done | bytes 352288 | tf_op jit(solution)/shard_map/ppermute | solution.py:44
  108.4 0.8 copy-done.9
  109.2 3.9 %down.3 = (bf16[4,4,16,1024]{3,2,1,0:T(8,128)(2,1)S(1)}, bf16[4,4,16,1024]{3,2,1,0:T(8,128)(2,1)S(1)}, bf16[4,4,16,1024]{3,2,1,0:T(8,128)(2,1)S(1)}, bf16[4,4,16,1024]{3,2,1,0:T(8,128)(2,1)S(1)}) custom-call(s32[2]{0:T(128)S(1)} %pad_add_fusion.place.refs_0_, s32[1]{0:T(128)} %bitcast.2.refs_1_, bf16[344,1024]{1,0:T(8,128)(2,1)S(1)} %copy-done.1, ...), custom_call_target="tpu_custom_call" | custom-call | tf_op jit(solution)/shard_map/down/pallas_call | solution.py:393
  114.2 3.9 %down.2 = (bf16[4,4,16,1024]{3,2,1,0:T(8,128)(2,1)S(1)}, bf16[4,4,16,1024]{3,2,1,0:T(8,128)(2,1)S(1)}, bf16[4,4,16,1024]{3,2,1,0:T(8,128)(2,1)S(1)}, bf16[4,4,16,1024]{3,2,1,0:T(8,128)(2,1)S(1)}) custom-call(s32[2]{0:T(128)S(1)} %pad_add_fusion.place.refs_0_, s32[1]{0:T(128)} %bitcast.2.refs_1_, bf16[344,1024]{1,0:T(8,128)(2,1)S(1)} %copy-done.1, ...), custom_call_target="tpu_custom_call" | custom-call | tf_op jit(solution)/shard_map/down/pallas_call | solution.py:393
  118.3 3.8 %collective-permute-start.27 = (bf16[4,4,16,1024]{3,2,1,0:T(8,128)(2,1)S(1)}, bf16[4,4,16,1024]{3,2,1,0:T(8,128)(2,1)S(1)}, u32[]{:S(2)}, u32[]{:S(2)}) collective-permute-start(bf16[4,4,16,1024]{3,2,1,0:T(8,128)(2,1)S(1)} %add_convert_fusion.3), channel_id=1, source_target_pairs={{0,24},{4,100},{8,0},{12,108},{16,8},{20,116},{24,16},{28,124},{32... | collective-permute-start | bytes 1572872 | tf_op jit(solution)/shard_map/ppermute | solution.py:48
  122.6 1.2 collective-permute-start.31
  123.8 10.6 %collective-permute-done.27 = bf16[4,4,16,1024]{3,2,1,0:T(8,128)(2,1)S(1)} collective-permute-done((bf16[4,4,16,1024]{3,2,1,0:T(8,128)(2,1)S(1)}, bf16[4,4,16,1024]{3,2,1,0:T(8,128)(2,1)S(1)}, u32[]{:S(2)}, u32[]{:S(2)}) %collective-permute-start.27) | collective-permute-done | bytes 524320 | tf_op jit(solution)/shard_map/ppermute | solution.py:48
  134.4 4.3 %collective-permute-done.31 = bf16[4,4,16,1024]{3,2,1,0:T(8,128)(2,1)S(1)} collective-permute-done((bf16[4,4,16,1024]{3,2,1,0:T(8,128)(2,1)S(1)}, bf16[4,4,16,1024]{3,2,1,0:T(8,128)(2,1)S(1)}, u32[]{:S(2)}, u32[]{:S(2)}) %collective-permute-start.31) | collective-permute-done | bytes 524320 | tf_op jit(solution)/shard_map/ppermute | solution.py:48
  139.7 1.7 %collective-permute-start.34 = (bf16[4,16,1024]{2,1,0:T(8,128)(2,1)S(1)}, bf16[4,16,1024]{2,1,0:T(8,128)(2,1)S(1)}, u32[]{:S(2)}, u32[]{:S(2)}) collective-permute-start(bf16[4,16,1024]{2,1,0:T(8,128)(2,1)S(1)} %get-tuple-element.76), channel_id=1, source_target_pairs={{0,32},{4,12},{8,40},{12,20},{16,48},{20,28},{24,56},{28,4},{32,64... | collective-permute-start | bytes 393224 | tf_op jit(solution)/shard_map/ppermute | solution.py:48
  141.4 2.0 %collective-permute-start.33 = (bf16[4,16,1024]{2,1,0:T(8,128)(2,1)S(1)}, bf16[4,16,1024]{2,1,0:T(8,128)(2,1)S(1)}, u32[]{:S(2)}, u32[]{:S(2)}) collective-permute-start(bf16[4,16,1024]{2,1,0:T(8,128)(2,1)S(1)} %get-tuple-element.77), channel_id=1, source_target_pairs={{0,64},{4,20},{8,72},{12,28},{16,80},{20,4},{24,88},{28,12},{32,96... | collective-permute-start | bytes 393224 | tf_op jit(solution)/shard_map/ppermute | solution.py:48
  143.4 0.9 collective-permute-done.32
  144.3 1.6 %collective-permute-done.34 = bf16[4,16,1024]{2,1,0:T(8,128)(2,1)S(1)} collective-permute-done((bf16[4,16,1024]{2,1,0:T(8,128)(2,1)S(1)}, bf16[4,16,1024]{2,1,0:T(8,128)(2,1)S(1)}, u32[]{:S(2)}, u32[]{:S(2)}) %collective-permute-start.34) | collective-permute-done | bytes 131104 | tf_op jit(solution)/shard_map/ppermute | solution.py:48
  145.9 2.0 %collective-permute-done.33 = bf16[4,16,1024]{2,1,0:T(8,128)(2,1)S(1)} collective-permute-done((bf16[4,16,1024]{2,1,0:T(8,128)(2,1)S(1)}, bf16[4,16,1024]{2,1,0:T(8,128)(2,1)S(1)}, u32[]{:S(2)}, u32[]{:S(2)}) %collective-permute-start.33) | collective-permute-done | bytes 131104 | tf_op jit(solution)/shard_map/ppermute | solution.py:48
  147.9 0.7 fusion.2
  (77 shorter events, 5.7 us)
Async XLA Ops:
  1.3 52.0 %copy-start.3 = (bf16[344,1024]{1,0:T(8,128)(2,1)}, bf16[344,1024]{1,0:T(8,128)(2,1)S(1)}, u32[]{:S(2)}) copy-start(bf16[344,1024]{1,0:T(8,128)(2,1)S(1)} %get-tuple-element.54.refs_8_) | copy-start | bytes 2113540
  1.4 55.0 %copy-start.4 = (bf16[344,1024]{1,0:T(8,128)(2,1)}, bf16[344,1024]{1,0:T(8,128)(2,1)S(1)}, u32[]{:S(2)}) copy-start(bf16[344,1024]{1,0:T(8,128)(2,1)S(1)} %get-tuple-element.55.refs_9_) | copy-start | bytes 2113540
  1.4 29.3 %collective-permute-start.3 = (bf16[344,1024]{1,0:T(8,128)(2,1)S(1)}, bf16[344,1024]{1,0:T(8,128)(2,1)S(1)}, u32[]{:S(2)}, u32[]{:S(2)}) collective-permute-start(bf16[344,1024]{1,0:T(8,128)(2,1)S(1)} %get-tuple-element.54.refs_8_), channel_id=1, source_target_pairs={{0,1},{1,2},{2,3},{3,0},{4,5},{5,6},{6,7},{7,4},{8,9},{9,10},{10,1... | collective-permute-start | bytes 2113544 | tf_op jit(solution)/shard_map/ppermute | solution.py:44
  3.0 27.6 %collective-permute-start.4 = (bf16[344,1024]{1,0:T(8,128)(2,1)S(1)}, bf16[344,1024]{1,0:T(8,128)(2,1)}, u32[]{:S(2)}, u32[]{:S(2)}) collective-permute-start(bf16[344,1024]{1,0:T(8,128)(2,1)S(1)} %get-tuple-element.55.refs_9_), channel_id=1, source_target_pairs={{0,3},{1,0},{2,1},{3,2},{4,7},{5,4},{6,5},{7,6},{8,11},{9,8},{10,9... | collective-permute-start | bytes 2113544 | tf_op jit(solution)/shard_map/ppermute | solution.py:44
  6.1 62.2 %copy-start.14 = (s32[32]{0:T(128)S(1)}, s32[32]{0:T(128)}, u32[]{:S(2)}) copy-start(s32[32]{0:T(128)} %param.17) | copy-start | bytes 388
  21.1 88.0 %copy-start.1 = (bf16[344,1024]{1,0:T(8,128)(2,1)S(1)}, bf16[344,1024]{1,0:T(8,128)(2,1)}, u32[]{:S(2)}) copy-start(bf16[344,1024]{1,0:T(8,128)(2,1)} %refs_2_.3) | copy-start | bytes 2113540
  21.2 8.9 %collective-permute-start = (bf16[16,4224]{1,0:T(8,128)(2,1)S(1)}, bf16[16,4224]{1,0:T(8,128)(2,1)S(1)}, u32[]{:S(2)}, u32[]{:S(2)}) collective-permute-start(bf16[16,4224]{1,0:T(8,128)(2,1)S(1)} %get-tuple-element.41), channel_id=1, source_target_pairs={{0,1},{1,2},{2,3},{3,0},{4,5},{5,6},{6,7},{7,4},{8,9},{9,10},{10,1... | collective-permute-start | bytes 405512 | tf_op jit(solution)/shard_map/ppermute | solution.py:44
  21.6 8.5 %collective-permute-start.1 = (bf16[16,4224]{1,0:T(8,128)(2,1)S(1)}, bf16[16,4224]{1,0:T(8,128)(2,1)S(1)}, u32[]{:S(2)}, u32[]{:S(2)}) collective-permute-start(bf16[16,4224]{1,0:T(8,128)(2,1)S(1)} %get-tuple-element.42), channel_id=1, source_target_pairs={{0,2},{1,3},{2,0},{3,1},{4,6},{5,7},{6,4},{7,5},{8,10},{9,11},{10,... | collective-permute-start | bytes 405512 | tf_op jit(solution)/shard_map/ppermute | solution.py:44
  24.3 6.3 %collective-permute-start.2 = (bf16[16,4224]{1,0:T(8,128)(2,1)S(1)}, bf16[16,4224]{1,0:T(8,128)(2,1)S(1)}, u32[]{:S(2)}, u32[]{:S(2)}) collective-permute-start(bf16[16,4224]{1,0:T(8,128)(2,1)S(1)} %get-tuple-element.43), channel_id=1, source_target_pairs={{0,3},{1,0},{2,1},{3,2},{4,7},{5,4},{6,5},{7,6},{8,11},{9,8},{10,9... | collective-permute-start | bytes 405512 | tf_op jit(solution)/shard_map/ppermute | solution.py:44
  30.6 47.3 %copy-start.10 = (bf16[344,1024]{1,0:T(8,128)(2,1)}, bf16[344,1024]{1,0:T(8,128)(2,1)S(1)}, u32[]{:S(2)}) copy-start(bf16[344,1024]{1,0:T(8,128)(2,1)S(1)} %collective-permute-done.3.refs_10_) | copy-start | bytes 2113540
  30.7 17.6 %collective-permute-start.8 = (bf16[344,1024]{1,0:T(8,128)(2,1)S(1)}, bf16[344,1024]{1,0:T(8,128)(2,1)S(1)}, u32[]{:S(2)}, u32[]{:S(2)}) collective-permute-start(bf16[344,1024]{1,0:T(8,128)(2,1)S(1)} %collective-permute-done.3.refs_10_), channel_id=1, source_target_pairs={{0,1},{1,2},{2,3},{3,0},{4,5},{5,6},{6,7},{7,4},{8,9},{9,10},{10,1... | collective-permute-start | bytes 2113544 | tf_op jit(solution)/shard_map/ppermute | solution.py:44
  32.0 16.7 %collective-permute-start.9 = (bf16[344,1024]{1,0:T(8,128)(2,1)}, bf16[344,1024]{1,0:T(8,128)(2,1)S(1)}, u32[]{:S(2)}, u32[]{:S(2)}) collective-permute-start(bf16[344,1024]{1,0:T(8,128)(2,1)} %collective-permute-done.4.refs_15_), channel_id=1, source_target_pairs={{0,3},{1,0},{2,1},{3,2},{4,7},{5,4},{6,5},{7,6},{8,11},{9,8},{10,9... | collective-permute-start | bytes 2113544 | tf_op jit(solution)/shard_map/ppermute | solution.py:44
  34.7 8.1 %collective-permute-start.7 = (bf16[16,4096]{1,0:T(8,128)(2,1)S(1)}, bf16[16,4096]{1,0:T(8,128)(2,1)S(1)}, u32[]{:S(2)}, u32[]{:S(2)}) collective-permute-start(bf16[16,4096]{1,0:T(8,128)(2,1)S(1)} %get-tuple-element.50.refs_0_), channel_id=1, source_target_pairs={{0,96},{4,28},{8,104},{12,4},{16,112},{20,12},{24,120},{28,20},{32... | collective-permute-start | bytes 393224 | tf_op jit(solution)/shard_map/ppermute | solution.py:48
  38.9 6.6 %collective-permute-start.6 = (bf16[16,4096]{1,0:T(8,128)(2,1)S(1)}, bf16[16,4096]{1,0:T(8,128)(2,1)S(1)}, u32[]{:S(2)}, u32[]{:S(2)}) collective-permute-start(bf16[16,4096]{1,0:T(8,128)(2,1)S(1)} %get-tuple-element.50.refs_0_), channel_id=1, source_target_pairs={{0,64},{4,20},{8,72},{12,28},{16,80},{20,4},{24,88},{28,12},{32,96... | collective-permute-start | bytes 393224 | tf_op jit(solution)/shard_map/ppermute | solution.py:48
  38.9 7.6 %collective-permute-start.5 = (bf16[16,4096]{1,0:T(8,128)(2,1)S(1)}, bf16[16,4096]{1,0:T(8,128)(2,1)S(1)}, u32[]{:S(2)}, u32[]{:S(2)}) collective-permute-start(bf16[16,4096]{1,0:T(8,128)(2,1)S(1)} %get-tuple-element.50.refs_0_), channel_id=1, source_target_pairs={{0,32},{4,12},{8,40},{12,20},{16,48},{20,28},{24,56},{28,4},{32,64... | collective-permute-start | bytes 393224 | tf_op jit(solution)/shard_map/ppermute | solution.py:48
  46.5 31.4 %copy-start.2 = (bf16[64,4096]{1,0:T(8,128)(2,1)}, bf16[64,4096]{1,0:T(8,128)(2,1)S(1)}, u32[]{:S(2)}) copy-start(bf16[64,4096]{1,0:T(8,128)(2,1)S(1)} %join.1.refs_0_) | copy-start | bytes 1572868
  48.3 15.8 %copy-start.11 = (bf16[344,1024]{1,0:T(8,128)(2,1)}, bf16[344,1024]{1,0:T(8,128)(2,1)S(1)}, u32[]{:S(2)}) copy-start(bf16[344,1024]{1,0:T(8,128)(2,1)S(1)} %collective-permute-done.8.refs_12_) | copy-start | bytes 2113540
  48.8 16.0 %copy-start.12 = (bf16[344,1024]{1,0:T(8,128)(2,1)}, bf16[344,1024]{1,0:T(8,128)(2,1)S(1)}, u32[]{:S(2)}) copy-start(bf16[344,1024]{1,0:T(8,128)(2,1)S(1)} %collective-permute-done.9.refs_13_) | copy-start | bytes 2113540
  48.8 7.6 %collective-permute-start.13 = (bf16[64,4096]{1,0:T(8,128)(2,1)S(1)}, bf16[64,4096]{1,0:T(8,128)(2,1)S(1)}, u32[]{:S(2)}, u32[]{:S(2)}) collective-permute-start(bf16[64,4096]{1,0:T(8,128)(2,1)S(1)} %join.1.refs_0_), channel_id=1, source_target_pairs={{0,4},{4,0},{1,5},{5,1},{2,6},{6,2},{3,7},{7,3},{8,12},{12,8},{9,1... | collective-permute-start | bytes 1572872 | tf_op jit(solution)/shard_map/ppermute | solution.py:52
  48.8 15.3 %collective-permute-start.12 = (bf16[64,4096]{1,0:T(8,128)(2,1)S(1)}, bf16[64,4096]{1,0:T(8,128)(2,1)}, u32[]{:S(2)}, u32[]{:S(2)}) collective-permute-start(bf16[64,4096]{1,0:T(8,128)(2,1)S(1)} %join.1.refs_0_), channel_id=1, source_target_pairs={{0,24},{4,100},{8,0},{12,108},{16,8},{20,116},{24,16},{28,124},{32... | collective-permute-start | bytes 1572872 | tf_op jit(solution)/shard_map/ppermute | solution.py:48
  51.8 13.4 %collective-permute-start.11 = (bf16[64,4096]{1,0:T(8,128)(2,1)S(1)}, bf16[64,4096]{1,0:T(8,128)(2,1)}, u32[]{:S(2)}, u32[]{:S(2)}) collective-permute-start(bf16[64,4096]{1,0:T(8,128)(2,1)S(1)} %join.1.refs_0_), channel_id=1, source_target_pairs={{0,16},{4,68},{8,24},{12,76},{16,0},{20,84},{24,8},{28,92},{32,48}... | collective-permute-start | bytes 1572872 | tf_op jit(solution)/shard_map/ppermute | solution.py:48
  52.4 15.8 %collective-permute-start.10 = (bf16[64,4096]{1,0:T(8,128)(2,1)S(1)}, bf16[64,4096]{1,0:T(8,128)(2,1)}, u32[]{:S(2)}, u32[]{:S(2)}) collective-permute-start(bf16[64,4096]{1,0:T(8,128)(2,1)S(1)} %join.1.refs_0_), channel_id=1, source_target_pairs={{0,8},{4,36},{8,16},{12,44},{16,24},{20,52},{24,0},{28,60},{32,40}... | collective-permute-start | bytes 1572872 | tf_op jit(solution)/shard_map/ppermute | solution.py:48
  53.4 18.6 %collective-permute-start.18 = (bf16[344,1024]{1,0:T(8,128)(2,1)S(1)}, bf16[344,1024]{1,0:T(8,128)(2,1)}, u32[]{:S(2)}, u32[]{:S(2)}) collective-permute-start(bf16[344,1024]{1,0:T(8,128)(2,1)S(1)} %get-tuple-element.54.refs_8_), channel_id=1, source_target_pairs={{0,3},{1,0},{2,1},{3,2},{4,7},{5,4},{6,5},{7,6},{8,11},{9,8},{10,9... | collective-permute-start | bytes 2113544 | tf_op jit(solution)/shard_map/ppermute | solution.py:44
  56.4 7.7 %copy-start.13 = (bf16[64,4096]{1,0:T(8,128)(2,1)}, bf16[64,4096]{1,0:T(8,128)(2,1)S(1)}, u32[]{:S(2)}) copy-start(bf16[64,4096]{1,0:T(8,128)(2,1)S(1)} %collective-permute-done.13.refs_4_) | copy-start | bytes 1572868
  56.4 19.1 %collective-permute-start.17 = (bf16[344,1024]{1,0:T(8,128)(2,1)S(1)}, bf16[344,1024]{1,0:T(8,128)(2,1)}, u32[]{:S(2)}, u32[]{:S(2)}) collective-permute-start(bf16[344,1024]{1,0:T(8,128)(2,1)S(1)} %get-tuple-element.55.refs_9_), channel_id=1, source_target_pairs={{0,1},{1,2},{2,3},{3,0},{4,5},{5,6},{6,7},{7,4},{8,9},{9,10},{10,1... | collective-permute-start | bytes 2113544 | tf_op jit(solution)/shard_map/ppermute | solution.py:44
  64.1 13.1 %collective-permute-start.16 = (bf16[64,4096]{1,0:T(8,128)(2,1)}, bf16[64,4096]{1,0:T(8,128)(2,1)}, u32[]{:S(2)}, u32[]{:S(2)}) collective-permute-start(bf16[64,4096]{1,0:T(8,128)(2,1)} %collective-permute-done.12.refs_3_), channel_id=1, source_target_pairs={{0,4},{4,0},{1,5},{5,1},{2,6},{6,2},{3,7},{7,3},{8,12},{12,8},{9,1... | collective-permute-start | bytes 1572872 | tf_op jit(solution)/shard_map/ppermute | solution.py:52
  65.1 12.8 %collective-permute-start.15 = (bf16[64,4096]{1,0:T(8,128)(2,1)}, bf16[64,4096]{1,0:T(8,128)(2,1)}, u32[]{:S(2)}, u32[]{:S(2)}) collective-permute-start(bf16[64,4096]{1,0:T(8,128)(2,1)} %collective-permute-done.11.refs_2_), channel_id=1, source_target_pairs={{0,4},{4,0},{1,5},{5,1},{2,6},{6,2},{3,7},{7,3},{8,12},{12,8},{9,1... | collective-permute-start | bytes 1572872 | tf_op jit(solution)/shard_map/ppermute | solution.py:52
  68.2 9.7 %collective-permute-start.14 = (bf16[64,4096]{1,0:T(8,128)(2,1)}, bf16[64,4096]{1,0:T(8,128)(2,1)}, u32[]{:S(2)}, u32[]{:S(2)}) collective-permute-start(bf16[64,4096]{1,0:T(8,128)(2,1)} %collective-permute-done.10.refs_1_), channel_id=1, source_target_pairs={{0,4},{4,0},{1,5},{5,1},{2,6},{6,2},{3,7},{7,3},{8,12},{12,8},{9,1... | collective-permute-start | bytes 1572872 | tf_op jit(solution)/shard_map/ppermute | solution.py:52
  71.9 14.7 %collective-permute-start.19 = (bf16[16,1024]{1,0:T(8,128)(2,1)S(1)}, bf16[16,1024]{1,0:T(8,128)(2,1)S(1)}, u32[]{:S(2)}, u32[]{:S(2)}) collective-permute-start(bf16[16,1024]{1,0:T(8,128)(2,1)S(1)} %get-tuple-element.59), channel_id=1, source_target_pairs={{0,1},{1,2},{2,3},{3,0},{4,5},{5,6},{6,7},{7,4},{8,9},{9,10},{10,1... | collective-permute-start | bytes 98312 | tf_op jit(solution)/shard_map/ppermute | solution.py:44
  75.5 11.1 %collective-permute-start.20 = (bf16[16,1024]{1,0:T(8,128)(2,1)S(1)}, bf16[16,1024]{1,0:T(8,128)(2,1)S(1)}, u32[]{:S(2)}, u32[]{:S(2)}) collective-permute-start(bf16[16,1024]{1,0:T(8,128)(2,1)S(1)} %get-tuple-element.60), channel_id=1, source_target_pairs={{0,2},{1,3},{2,0},{3,1},{4,6},{5,7},{6,4},{7,5},{8,10},{9,11},{10,... | collective-permute-start | bytes 98312 | tf_op jit(solution)/shard_map/ppermute | solution.py:44
  77.2 9.4 %collective-permute-start.21 = (bf16[16,1024]{1,0:T(8,128)(2,1)S(1)}, bf16[16,1024]{1,0:T(8,128)(2,1)S(1)}, u32[]{:S(2)}, u32[]{:S(2)}) collective-permute-start(bf16[16,1024]{1,0:T(8,128)(2,1)S(1)} %get-tuple-element.61), channel_id=1, source_target_pairs={{0,3},{1,0},{2,1},{3,2},{4,7},{5,4},{6,5},{7,6},{8,11},{9,8},{10,9... | collective-permute-start | bytes 98312 | tf_op jit(solution)/shard_map/ppermute | solution.py:44
  86.6 21.8 %copy-start = (bf16[512,344]{1,0:T(8,128)(2,1)}, bf16[512,344]{1,0:T(8,128)(2,1)S(1)}, u32[]{:S(2)}) copy-start(bf16[512,344]{1,0:T(8,128)(2,1)S(1)} %gate_up_act.1.refs_3_) | copy-start | bytes 1056772
  86.6 18.1 %collective-permute-start.24 = (bf16[512,344]{1,0:T(8,128)(2,1)S(1)}, bf16[512,344]{1,0:T(8,128)(2,1)S(1)}, u32[]{:S(2)}, u32[]{:S(2)}) collective-permute-start(bf16[512,344]{1,0:T(8,128)(2,1)S(1)} %gate_up_act.1.refs_3_), channel_id=1, source_target_pairs={{0,3},{1,0},{2,1},{3,2},{4,7},{5,4},{6,5},{7,6},{8,11},{9,8},{10,9... | collective-permute-start | bytes 1056776 | tf_op jit(solution)/shard_map/ppermute | solution.py:44
  89.1 15.7 %collective-permute-start.23 = (bf16[512,344]{1,0:T(8,128)(2,1)S(1)}, bf16[512,344]{1,0:T(8,128)(2,1)S(1)}, u32[]{:S(2)}, u32[]{:S(2)}) collective-permute-start(bf16[512,344]{1,0:T(8,128)(2,1)S(1)} %gate_up_act.1.refs_3_), channel_id=1, source_target_pairs={{0,2},{1,3},{2,0},{3,1},{4,6},{5,7},{6,4},{7,5},{8,10},{9,11},{10,... | collective-permute-start | bytes 1056776 | tf_op jit(solution)/shard_map/ppermute | solution.py:44
  90.7 17.7 %collective-permute-start.22 = (bf16[512,344]{1,0:T(8,128)(2,1)S(1)}, bf16[512,344]{1,0:T(8,128)(2,1)S(1)}, u32[]{:S(2)}, u32[]{:S(2)}) collective-permute-start(bf16[512,344]{1,0:T(8,128)(2,1)S(1)} %gate_up_act.1.refs_3_), channel_id=1, source_target_pairs={{0,1},{1,2},{2,3},{3,0},{4,5},{5,6},{6,7},{7,4},{8,9},{9,10},{10,1... | collective-permute-start | bytes 1056776 | tf_op jit(solution)/shard_map/ppermute | solution.py:44
  104.7 3.7 %copy-start.7 = (bf16[512,344]{1,0:T(8,128)(2,1)}, bf16[512,344]{1,0:T(8,128)(2,1)S(1)}, u32[]{:S(2)}) copy-start(bf16[512,344]{1,0:T(8,128)(2,1)S(1)} %collective-permute-done.24.refs_6_) | copy-start | bytes 1056772
  104.7 3.7 %copy-start.8 = (bf16[512,344]{1,0:T(8,128)(2,1)}, bf16[512,344]{1,0:T(8,128)(2,1)S(1)}, u32[]{:S(2)}) copy-start(bf16[512,344]{1,0:T(8,128)(2,1)S(1)} %collective-permute-done.23.refs_5_) | copy-start | bytes 1056772
  108.4 0.8 copy-start.9
  113.1 5.0 %collective-permute-start.26 = (bf16[4,4,16,1024]{3,2,1,0:T(8,128)(2,1)S(1)}, bf16[4,4,16,1024]{3,2,1,0:T(8,128)(2,1)S(1)}, u32[]{:S(2)}, u32[]{:S(2)}) collective-permute-start(bf16[4,4,16,1024]{3,2,1,0:T(8,128)(2,1)S(1)} %get-tuple-element.70), channel_id=1, source_target_pairs={{0,4},{4,0},{1,5},{5,1},{2,6},{6,2},{3,7},{7,3},{8,12},{12,8},{9,1... | collective-permute-start | bytes 1572872 | tf_op jit(solution)/shard_map/ppermute | solution.py:52
  113.2 8.9 %collective-permute-start.28 = (bf16[4,4,16,1024]{3,2,1,0:T(8,128)(2,1)S(1)}, bf16[4,4,16,1024]{3,2,1,0:T(8,128)(2,1)S(1)}, u32[]{:S(2)}, u32[]{:S(2)}) collective-permute-start(bf16[4,4,16,1024]{3,2,1,0:T(8,128)(2,1)S(1)} %get-tuple-element.72), channel_id=1, source_target_pairs={{0,4},{4,0},{1,5},{5,1},{2,6},{6,2},{3,7},{7,3},{8,12},{12,8},{9,1... | collective-permute-start | bytes 1572872 | tf_op jit(solution)/shard_map/ppermute | solution.py:52
  113.7 10.1 %collective-permute-start.25 = (bf16[4,4,16,1024]{3,2,1,0:T(8,128)(2,1)S(1)}, bf16[4,4,16,1024]{3,2,1,0:T(8,128)(2,1)S(1)}, u32[]{:S(2)}, u32[]{:S(2)}) collective-permute-start(bf16[4,4,16,1024]{3,2,1,0:T(8,128)(2,1)S(1)} %get-tuple-element.68), channel_id=1, source_target_pairs={{0,4},{4,0},{1,5},{5,1},{2,6},{6,2},{3,7},{7,3},{8,12},{12,8},{9,1... | collective-permute-start | bytes 1572872 | tf_op jit(solution)/shard_map/ppermute | solution.py:52
  113.8 8.6 %collective-permute-start.30 = (bf16[4,4,16,1024]{3,2,1,0:T(8,128)(2,1)S(1)}, bf16[4,4,16,1024]{3,2,1,0:T(8,128)(2,1)S(1)}, u32[]{:S(2)}, u32[]{:S(2)}) collective-permute-start(bf16[4,4,16,1024]{3,2,1,0:T(8,128)(2,1)S(1)} %get-tuple-element.74), channel_id=1, source_target_pairs={{0,4},{4,0},{1,5},{5,1},{2,6},{6,2},{3,7},{7,3},{8,12},{12,8},{9,1... | collective-permute-start | bytes 1572872 | tf_op jit(solution)/shard_map/ppermute | solution.py:52
  118.3 16.1 %collective-permute-start.27 = (bf16[4,4,16,1024]{3,2,1,0:T(8,128)(2,1)S(1)}, bf16[4,4,16,1024]{3,2,1,0:T(8,128)(2,1)S(1)}, u32[]{:S(2)}, u32[]{:S(2)}) collective-permute-start(bf16[4,4,16,1024]{3,2,1,0:T(8,128)(2,1)S(1)} %add_convert_fusion.3), channel_id=1, source_target_pairs={{0,24},{4,100},{8,0},{12,108},{16,8},{20,116},{24,16},{28,124},{32... | collective-permute-start | bytes 1572872 | tf_op jit(solution)/shard_map/ppermute | solution.py:48
  122.3 12.1 %collective-permute-start.29 = (bf16[4,4,16,1024]{3,2,1,0:T(8,128)(2,1)S(1)}, bf16[4,4,16,1024]{3,2,1,0:T(8,128)(2,1)S(1)}, u32[]{:S(2)}, u32[]{:S(2)}) collective-permute-start(bf16[4,4,16,1024]{3,2,1,0:T(8,128)(2,1)S(1)} %add_convert_fusion.2), channel_id=1, source_target_pairs={{0,16},{4,68},{8,24},{12,76},{16,0},{20,84},{24,8},{28,92},{32,48}... | collective-permute-start | bytes 1572872 | tf_op jit(solution)/shard_map/ppermute | solution.py:48
  122.6 16.1 %collective-permute-start.31 = (bf16[4,4,16,1024]{3,2,1,0:T(8,128)(2,1)S(1)}, bf16[4,4,16,1024]{3,2,1,0:T(8,128)(2,1)S(1)}, u32[]{:S(2)}, u32[]{:S(2)}) collective-permute-start(bf16[4,4,16,1024]{3,2,1,0:T(8,128)(2,1)S(1)} %add_convert_fusion.1), channel_id=1, source_target_pairs={{0,8},{4,36},{8,16},{12,44},{16,24},{20,52},{24,0},{28,60},{32,40}... | collective-permute-start | bytes 1572872 | tf_op jit(solution)/shard_map/ppermute | solution.py:48
  139.2 5.1 %collective-permute-start.32 = (bf16[4,16,1024]{2,1,0:T(8,128)(2,1)S(1)}, bf16[4,16,1024]{2,1,0:T(8,128)(2,1)S(1)}, u32[]{:S(2)}, u32[]{:S(2)}) collective-permute-start(bf16[4,16,1024]{2,1,0:T(8,128)(2,1)S(1)} %get-tuple-element.75), channel_id=1, source_target_pairs={{0,96},{4,28},{8,104},{12,4},{16,112},{20,12},{24,120},{28,20},{32... | collective-permute-start | bytes 393224 | tf_op jit(solution)/shard_map/ppermute | solution.py:48
  139.7 6.2 %collective-permute-start.34 = (bf16[4,16,1024]{2,1,0:T(8,128)(2,1)S(1)}, bf16[4,16,1024]{2,1,0:T(8,128)(2,1)S(1)}, u32[]{:S(2)}, u32[]{:S(2)}) collective-permute-start(bf16[4,16,1024]{2,1,0:T(8,128)(2,1)S(1)} %get-tuple-element.76), channel_id=1, source_target_pairs={{0,32},{4,12},{8,40},{12,20},{16,48},{20,28},{24,56},{28,4},{32,64... | collective-permute-start | bytes 393224 | tf_op jit(solution)/shard_map/ppermute | solution.py:48
  141.4 6.5 %collective-permute-start.33 = (bf16[4,16,1024]{2,1,0:T(8,128)(2,1)S(1)}, bf16[4,16,1024]{2,1,0:T(8,128)(2,1)S(1)}, u32[]{:S(2)}, u32[]{:S(2)}) collective-permute-start(bf16[4,16,1024]{2,1,0:T(8,128)(2,1)S(1)} %get-tuple-element.77), channel_id=1, source_target_pairs={{0,64},{4,20},{8,72},{12,28},{16,80},{20,4},{24,88},{28,12},{32,96... | collective-permute-start | bytes 393224 | tf_op jit(solution)/shard_map/ppermute | solution.py:48
  (2 other events, 1.4 us)

commit v3 on v2

v3 whole, which is shorter than its diff:
```python
import jax
import jax.numpy as jnp
from jax import lax
from jax.experimental import pallas as pl
from jax.experimental.pallas import tpu as pltpu
from jax.sharding import Mesh, PartitionSpec as P

HD = 128
EPSILON = 1e-05
REP = ("z", "y", "c")
SIDE = 4
GROUP_LANES = 128
HBM = pl.BlockSpec(memory_space=pltpu.HBM)
VM = pl.BlockSpec(memory_space=pltpu.VMEM)
SM = pl.BlockSpec(memory_space=pltpu.SMEM)


def params(megabytes):
    return pltpu.CompilerParams(vmem_limit_bytes=megabytes * 1024 * 1024)


def in_hbm(value):
    return pltpu.with_memory_space_constraint(value, pltpu.HBM)


def cost(flops, moved):
    return pl.CostEstimate(flops=int(flops), transcendentals=0, bytes_accessed=int(moved))


def x_ring(shift):
    return [(i, (i + shift) % SIDE) for i in range(SIDE)]


def chip_ring(shift, first):
    pairs = []
    for z in range(SIDE):
        for y in range(SIDE):
            for c in range(2):
                if (c == 0) == first:
                    to = (((z + shift) % SIDE) * SIDE + y) * 2 + c
                else:
                    to = (z * SIDE + (y + shift) % SIDE) * 2 + c
                pairs.append(((z * SIDE + y) * 2 + c, to))
    return pairs


def along_x(value, shift):
    return lax.ppermute(value, "x", x_ring(shift))


def along_chips(value, shift, first):
    return lax.ppermute(value, REP, chip_ring(shift, first))


def other_core(value):
    return lax.ppermute(value, "c", [(0, 1), (1, 0)])


def attend_kernel(place, tables, spans, query, new_kv, hidden, gain, pool, weight, *refs):
    outs = refs[:SIDE]
    pages, weights, queries, pairs, homes, gains, table, lengths, by_head, heads, rows = refs[
        SIDE : SIDE + 11
    ]
    page_sem, weight_sem, sem = refs[SIDE + 11 :]
    groups, many, span_rows = pages.shape[:3]
    page_rows = pool.shape[1]
    requests, width = hidden.shape
    group = width // HD
    lanes = many * group
    block = requests // SIDE
    scale = HD ** (-0.5)
    x = place[0]
    home = place[1] * requests

    def weight_copy(n):
        return pltpu.make_async_copy(
            weight.at[:, pl.ds(n * width, width)], weights.at[n], weight_sem.at[n]
        )

    small = [
        pltpu.make_async_copy(source, into, sem.at[n])
        for n, (source, into) in enumerate(
            (
                (tables, table),
                (spans, lengths),
                (query, queries),
                (new_kv, pairs),
                (hidden, homes),
                (gain, gains),
            )
        )
    ]
    for copy in small:
        copy.start()
    small[0].wait()
    for g in range(groups):
        for i in range(many):
            for j in range(2):
                pltpu.make_async_copy(
                    pool.at[table[j, g * many + i]],
                    pages.at[g, i, pl.ds(j * page_rows, page_rows)],
                    page_sem.at[g],
                ).start()
    for n in range(SIDE):
        weight_copy(n).start()
    for copy in small[1:]:
        copy.wait()

    row = lax.broadcasted_iota(jnp.int32, (span_rows, lanes), 0)
    is_key = row % 2 == 0
    position = row // 2
    owner = lax.broadcasted_iota(jnp.int32, (HD, lanes), 1) // group
    lane = lax.broadcasted_iota(jnp.int32, (1, lanes), 1) // group

    def one_group(g):
        r0 = g * many
        for h in range(group):
            by_head[g, pl.ds(h, many, stride=group), :] = queries[
                r0 : r0 + many, h * HD : (h + 1) * HD
            ].astype(jnp.float32)
        q_t = jnp.transpose(by_head[g])
        sides = jnp.concatenate(
            [jnp.where(owner == i, q_t, 0.0).astype(jnp.bfloat16) for i in range(many)], axis=0
        )
        span = jnp.zeros((1, lanes), jnp.int32)
        for i in range(many):
            span = jnp.where(lane == i, lengths[home + r0 + i], span)
        pltpu.make_async_copy(pages.at[g], pages.at[g], page_sem.at[g]).wait()
        cached = jnp.concatenate([pages[g, i] for i in range(many)], axis=1)
        scores = jnp.dot(cached, sides, preferred_element_type=jnp.float32) * scale
        fresh = [pairs[r0 + i].astype(jnp.float32) for i in range(many)]
        own = jnp.dot(
            jnp.concatenate(fresh, axis=1).astype(jnp.bfloat16),
            sides,
            preferred_element_type=jnp.float32,
        )[0:1] * scale
        valid = is_key & (position < span)
        peak = jnp.maximum(
            jnp.max(jnp.where(valid, scores, -jnp.inf), axis=0, keepdims=True), own
        )
        w = jnp.where(valid, jnp.exp(scores - peak), 0.0)
        w_own = jnp.exp(own - peak)
        total = jnp.sum(w, axis=0, keepdims=True) + w_own
        line = lax.broadcasted_iota(jnp.int32, (HD, lanes), 0)
        w = jnp.transpose(pltpu.roll(w, 1, 0)).astype(jnp.bfloat16)
        last = jnp.transpose(jnp.where(line == 0, w_own, total))
        w_own = last[:, 0:1].astype(jnp.bfloat16).astype(jnp.float32)
        total = last[:, 1:2]
        for i in range(0, many, 2):
            two = jnp.concatenate([pages[g, i], pages[g, i + 1]], axis=1)
            mixed = jnp.dot(
                w[i * group : (i + 2) * group], two, preferred_element_type=jnp.float32
            )
            for k in range(2):
                at = slice((i + k) * group, (i + k + 1) * group)
                value = mixed[k * group : (k + 1) * group, k * HD : (k + 1) * HD]
                value = (value + w_own[at] * fresh[i + k][1:2]) / total[at]
                heads[pl.ds((r0 + i + k) * group, group), :] = value

    for g in range(groups):
        one_group(g)
    attention = jnp.concatenate(
        [heads[pl.ds(h, requests, stride=group), :].astype(jnp.bfloat16) for h in range(group)],
        axis=1,
    )
    for n in range(SIDE):
        weight_copy(n).wait()
        part = jnp.dot(attention, weights[n], preferred_element_type=jnp.float32)
        part = part + jnp.where(x == n, homes[...].astype(jnp.float32), 0.0)
        part = part.astype(jnp.bfloat16)
        for t in range(SIDE):
            rows[t, :, n * width : (n + 1) * width] = part[t * block : (t + 1) * block]
    high = gains[...].astype(jnp.bfloat16).astype(jnp.float32)
    extra = jnp.concatenate([high, gains[...] - high], axis=0).astype(jnp.bfloat16)
    for s in range(SIDE):
        outs[s][:, : SIDE * width] = rows[(x + s) % SIDE]
        outs[s][:, SIDE * width :] = extra


def attend_project(table, lengths, place, query, new_kv, hidden, gain, pool, weight):
    requests, width = hidden.shape
    block = requests // SIDE
    group = width // HD
    many = GROUP_LANES // group
    groups = requests // many
    page_rows = pool.shape[1] * pool.shape[2]
    out = jax.ShapeDtypeStruct((block, SIDE * width + HD), jnp.bfloat16)
    return pl.pallas_call(
        attend_kernel,
        out_shape=[out] * SIDE,
        in_specs=[SM] + [HBM] * 8,
        out_specs=[VM] * SIDE,
        scratch_shapes=[
            pltpu.VMEM((groups, many, 2 * page_rows, HD), jnp.bfloat16),
            pltpu.VMEM((SIDE, weight.shape[0], width), jnp.bfloat16),
            pltpu.VMEM(query.shape, jnp.bfloat16),
            pltpu.VMEM(new_kv.shape, jnp.bfloat16),
            pltpu.VMEM(hidden.shape, jnp.bfloat16),
            pltpu.VMEM((group, HD), jnp.float32),
            pltpu.SMEM(table.shape, jnp.int32),
            pltpu.SMEM(lengths.shape, jnp.int32),
            pltpu.VMEM((groups, many * group, HD), jnp.float32),
            pltpu.VMEM((requests * group, HD), jnp.float32),
            pltpu.VMEM((SIDE, block, SIDE * width), jnp.bfloat16),
            pltpu.SemaphoreType.DMA((groups,)),
            pltpu.SemaphoreType.DMA((SIDE,)),
            pltpu.SemaphoreType.DMA((6,)),
        ],
        compiler_params=params(36),
        cost_estimate=cost(2 * requests * width * SIDE * width, 2 * (pool.size + weight.size)),
        name="attend_project",
    )(
        place,
        in_hbm(table),
        in_hbm(lengths),
        in_hbm(query),
        in_hbm(new_kv),
        in_hbm(hidden),
        in_hbm(gain.reshape(group, HD)),
        in_hbm(pool.reshape(pool.shape[0], page_rows, HD)),
        in_hbm(weight),
    )


def norm_kernel(place, *refs):
    parts, (normed, kept, gains) = refs[:SIDE], refs[SIDE:]
    x = place[0]
    width = kept.shape[2]
    lines = width // HD
    for s in range(SIDE):
        extra = parts[s][:, SIDE * width :].astype(jnp.float32)
        gains[(x + SIDE - s) % SIDE] = extra[:lines] + extra[lines:]
    square = 0.0
    residual = []
    for n in range(SIDE):
        at = slice(n * width, (n + 1) * width)
        value = sum(p[:, at].astype(jnp.float32) for p in parts)
        square = square + jnp.sum(value * value, axis=1, keepdims=True)
        kept[n] = value.astype(jnp.bfloat16)
        residual.append(value)
    factor = lax.rsqrt(square / (SIDE * width) + EPSILON)
    for n in range(SIDE):
        gain = gains[n]
        for j in range(lines):
            value = residual[n][:, j * HD : (j + 1) * HD] * factor * gain[j : j + 1]
            normed[:, n * width + j * HD : n * width + (j + 1) * HD] = value.astype(jnp.bfloat16)


def normalise(place, parts, width):
    block = parts[0].shape[0]
    return pl.pallas_call(
        norm_kernel,
        out_shape=[
            jax.ShapeDtypeStruct((block, SIDE * width), jnp.bfloat16),
            jax.ShapeDtypeStruct((SIDE, block, width), jnp.bfloat16),
        ],
        in_specs=[SM] + [VM] * SIDE,
        out_specs=[VM, VM],
        scratch_shapes=[pltpu.VMEM((SIDE, width // HD, HD), jnp.float32)],
        compiler_params=params(16),
        cost_estimate=cost(0, 12 * SIDE * block * width),
        name="normalise",
    )(place, *parts)


def join_kernel(*refs):
    parts, out = refs[:-1], refs[-1]
    rows = parts[0].shape[0]
    for i, part in enumerate(parts):
        out[i * rows : (i + 1) * rows] = part[...]


def join(parts):
    rows, width = parts[0].shape
    return pl.pallas_call(
        join_kernel,
        out_shape=jax.ShapeDtypeStruct((len(parts) * rows, width), parts[0].dtype),
        in_specs=[VM] * len(parts),
        out_specs=VM,
        compiler_params=params(4),
        cost_estimate=cost(0, 4 * len(parts) * rows * width),
        name="join",
    )(*parts)


def split_kernel(both, gate, up, sem):
    copies = [
        pltpu.make_async_copy(both.at[k], into, sem.at[k]) for k, into in enumerate((gate, up))
    ]
    for c in copies:
        c.start()
    for c in copies:
        c.wait()


def split(both):
    half = jax.ShapeDtypeStruct(both.shape[1:], both.dtype)
    return pl.pallas_call(
        split_kernel,
        out_shape=[half, half],
        in_specs=[HBM],
        out_specs=[VM, VM],
        scratch_shapes=[pltpu.SemaphoreType.DMA((2,))],
        compiler_params=params(4),
        name="split",
    )(in_hbm(both))


def gate_up_kernel(place, source, *refs):
    blocks, sides, outs = refs[: 2 * SIDE], refs[2 * SIDE : 4 * SIDE], refs[4 * SIDE : 4 * SIDE + 2]
    turned, weights, values, moved, sem = refs[4 * SIDE + 2 :]
    x = place[0]
    rows = blocks[0].shape[0]
    units, width = sides[0].shape
    apart = weights.shape[0] // 2
    copies = []
    for i, side in enumerate(sides):
        start = pl.multiple_of(((x + SIDE - i // 2) % SIDE) * width, width)
        into = weights.at[pl.ds((i % 2) * apart, units), pl.ds(start, width)]
        copies.append(pltpu.make_async_copy(side, into, sem.at[i]))
    for c in copies:
        c.start()
    for p in range(SIDE):
        pair = jnp.concatenate([blocks[2 * p][...], blocks[2 * p + 1][...]], axis=0)
        turned[:, 2 * p * rows : 2 * (p + 1) * rows] = jnp.transpose(pair)
    for c in copies:
        c.wait()
    both = jnp.dot(weights[...], turned[...], preferred_element_type=jnp.float32)
    value = jax.nn.silu(both[:units]) * both[apart : apart + units]
    spare = values.shape[1] - units
    value = jnp.concatenate([value, jnp.zeros((spare, value.shape[1]), jnp.float32)], axis=0)
    values[...] = jnp.transpose(value)
    slots = source.shape[0]
    block = values.shape[0] // slots
    for d in range(slots):
        moved[d : d + 1] = values[pl.ds(source[d] * block + block - 1, 1)]
    for d in range(slots):
        values[(d + 1) * block - 1 : (d + 1) * block] = moved[d : d + 1]
    half = values.shape[0] // 2
    for k in range(2):
        outs[k][...] = values[k * half : (k + 1) * half, :units].astype(jnp.bfloat16)


def gate_up_act(place, source, blocks, sides):
    rows, features = blocks[0].shape
    rows = rows * len(blocks)
    units = sides[0].shape[0]
    padded = -(-units // HD) * HD
    return pl.pallas_call(
        gate_up_kernel,
        out_shape=[jax.ShapeDtypeStruct((rows // 2, units), jnp.bfloat16)] * 2,
        in_specs=[SM, SM] + [VM] * (2 * SIDE) + [HBM] * (2 * SIDE),
        out_specs=[VM, VM],
        scratch_shapes=[
            pltpu.VMEM((features, rows), jnp.bfloat16),
            pltpu.VMEM((2 * (-(-units // 16) * 16), features), jnp.bfloat16),
            pltpu.VMEM((rows, padded), jnp.float32),
            pltpu.VMEM((source.shape[0], padded), jnp.float32),
            pltpu.SemaphoreType.DMA((2 * SIDE,)),
        ],
        compiler_params=params(24),
        cost_estimate=cost(4 * rows * features * units, 10 * units * features),
        name="gate_up_act",
    )(place, source, *blocks, *map(in_hbm, sides))


def down_kernel(base, start, place, slot, weight, *refs):
    acts, homes, theirs, out = refs[:SIDE], refs[SIDE], refs[SIDE + 1 : -1], refs[-1]
    x = place[0]
    block = homes.shape[1]
    rows = SIDE * block
    inputs = jnp.concatenate([a[start * block : start * block + rows] for a in acts], axis=0)
    values = jnp.dot(inputs, weight[...], preferred_element_type=jnp.float32)
    line = lax.broadcasted_iota(jnp.int32, homes.shape[1:], 0)
    for s in range(SIDE):
        from_x = (x + SIDE - s) % SIDE
        home = homes[from_x].astype(jnp.float32)
        moves = (line == block - 1) & (from_x == SIDE - 1)
        for d in range(SIDE):
            value = values[s * rows + d * block : s * rows + (d + 1) * block]
            adds = moves & (slot[0] == base + d)
            if base + d == 0:
                adds = adds | jnp.logical_not(moves)
            value = value + jnp.where(adds, home, 0.0)
            for other in theirs:
                value = value + other[d, from_x].astype(jnp.float32)
            out[d, from_x] = value.astype(jnp.bfloat16)


def down(base, start, place, slot, weight, acts, homes, theirs=()):
    block, width = homes.shape[1:]
    return pl.pallas_call(
        lambda *refs: down_kernel(base, start, *refs),
        out_shape=jax.ShapeDtypeStruct((SIDE, SIDE, block, width), jnp.bfloat16),
        in_specs=[SM, SM, VM] + [VM] * (SIDE + 1 + len(theirs)),
        out_specs=VM,
        compiler_params=params(12),
        cost_estimate=cost(2 * SIDE * SIDE * block * weight.size, 2 * weight.size),
        name="down",
    )(place, slot, weight, *acts, homes, *theirs)


def slot_sources(dest):
    z, y, c = (lax.axis_index(a) for a in REP)
    other, second, first = jnp.meshgrid(
        jnp.arange(2), jnp.arange(SIDE), jnp.arange(SIDE), indexing="ij"
    )
    core = (c + other) % 2
    slot_z = (z - jnp.where(core == 0, first, second)) % SIDE
    slot_y = (y - jnp.where(core == 0, second, first)) % SIDE
    group = ((slot_z * SIDE + slot_y) * 2 + core).reshape(-1)
    target = jnp.sum(
        jnp.where(group[:, None] == jnp.arange(dest.shape[0])[None, :], dest[None, :], 0), axis=1
    )
    hit = group[:, None] == target[None, :]
    return jnp.sum(jnp.where(hit, jnp.arange(group.shape[0])[None, :], 0), axis=1)


def add(values):
    return sum(v.astype(jnp.float32) for v in values).astype(jnp.bfloat16)


def local(
    hidden_in,
    query,
    new_kv,
    pool,
    page_table,
    lengths,
    dest,
    out_weight,
    norm_gain,
    gate_up,
    down_weight,
):
    rows_here, width = hidden_in.shape
    x = lax.axis_index("x")
    place = jnp.stack([x, lax.axis_index(REP)]).astype(jnp.int32)

    gate, up = split(jnp.transpose(gate_up, (1, 2, 0)))
    gate_1, up_3 = along_x(gate, 1), along_x(up, 3)

    source = slot_sources(dest).astype(jnp.int32)
    slots = source.shape[0]
    identity = jnp.arange(slots, dtype=jnp.int32)
    slot = jnp.sum(jnp.where(source == 0, identity, 0))[None]
    source = jnp.where(x == SIDE - 1, source, identity)

    parts = attend_project(
        page_table.T, lengths, place, query, new_kv, hidden_in, norm_gain, pool, out_weight
    )
    parts = [parts[0]] + [along_x(parts[s], s) for s in (1, 2, 3)]
    normed, kept = normalise(place, parts, width)
    homes = lax.all_to_all(kept, "x", 0, 0, tiled=True)
    normed, gate_1, up_3 = lax.optimization_barrier((normed, gate_1, up_3))
    gate_2, up_2 = along_x(gate_1, 1), along_x(up_3, 3)

    first = join([normed] + [along_chips(normed, s, True) for s in (1, 2, 3)])
    first, gate, up, gate_2, up_2, homes = lax.optimization_barrier(
        (first, gate, up, gate_2, up_2, homes)
    )
    gate_3, up_1 = along_x(gate, 3), along_x(up, 1)
    sides = (gate, up, gate_1, up_1, gate_2, up_2, gate_3, up_3)
    second = [first] + [along_chips(first, s, False) for s in (1, 2, 3)]
    second[0], second[1] = lax.optimization_barrier((second[0], second[1]))
    blocks = second + [other_core(v) for v in second]
    mine, theirs = gate_up_act(place, source, blocks, sides)
    mine, theirs, homes = lax.optimization_barrier((mine, theirs, homes))
    theirs_1, theirs_3 = along_x(theirs, 1), along_x(theirs, 3)
    mine_1, mine_3 = along_x(mine, 1), along_x(mine, 3)
    theirs_2 = along_x(theirs_1, 1)
    theirs_2, theirs_3, mine_1, mine_3 = lax.optimization_barrier(
        (theirs_2, theirs_3, mine_1, mine_3)
    )
    theirs = [theirs, theirs_1, theirs_2, theirs_3]
    mine = [mine, mine_1, along_x(mine_3, 3), mine_3]

    half = slots // 2
    shifts = (2, 1, 3, 0)
    sent = [
        down(half + s * SIDE, s * SIDE, place, slot, down_weight, theirs, homes) for s in shifts
    ]
    sent[1], mine[2] = lax.optimization_barrier((sent[1], mine[2]))
    sent = [other_core(v) for v in sent]
    total = []
    for s, received in zip(shifts, sent):
        value = down(s * SIDE, s * SIDE, place, slot, down_weight, mine, homes, (received,))
        total.append(along_chips(value, -s, False) if s else value)
    total = add(total)
    out = add([total[0]] + [along_chips(total[s], -s, True) for s in (1, 2, 3)])
    return out.reshape(rows_here, width)


def solution(mesh):
    chips = Mesh(mesh.devices.reshape(SIDE, SIDE, 2, SIDE), ("z", "y", "c", "x"))
    return jax.shard_map(
        local,
        mesh=chips,
        in_specs=(
            P(REP, "x"),
            P(REP, "x"),
            P(REP, None, "x"),
            P(REP, None, None, "x"),
            P(REP, None),
            P(),
            P(),
            P("x", None),
            P("x"),
            P("x", None, REP),
            P(REP, "x"),
        ),
        out_specs=P(REP, "x"),
        check_vma=False,
    )
```

time: 149 us -> 136 us (0.913)
  waiting for transfers between devices: 67.1 us -> 45.8 us
  starting transfers between devices: 42.3 us -> 49.6 us
  Pallas kernels: 33.6 us -> 37 us
  local copies, waits for them, and re-layouts: 2.55 us -> 0.38 us
    ppermute x15, waiting for transfers between devices: 31 us -> 16.5 us  [along_x(): return lax.ppermute(value, 'x', x_ring(shift))]
    ppermute x12, waiting for transfers between devices: 36.1 us -> 24 us  [along_chips(): return lax.ppermute(value, REP, chip_ring(shift, first))]
    all_to_all x0 -> x1, waiting for transfers between devices: none -> 5.36 us  [local(): homes = lax.all_to_all(kept, 'x', 0, 0, tiled=True)]
    ppermute x12, starting transfers between devices: 19.3 us -> 23 us  [along_chips(): return lax.ppermute(value, REP, chip_ring(shift, first))]
    all_to_all x0 -> x1, starting transfers between devices: none -> 3.33 us  [local(): homes = lax.all_to_all(kept, 'x', 0, 0, tiled=True)]
    pallas_call x4 -> x10, Pallas kernels: 31.5 us -> 34.3 us  [the longest x8 13 us: down(): pl.pallas_call(lambda *refs: down_kernel(base, start, *refs), out_shape=j...]
    unnamed x30 -> x8, local copies, waits for them, and re-layouts: 2.18 us -> 0.02 us
  transfers between devices with their start and end apart: 35 -> 36, of which waited for: 18 -> 18; matrix products, arithmetic and copies ran while one was open for 1% -> 1% of each run, Pallas kernels for 19% -> 20%
where the time goes in v3:
time: 136 us; the launch traced here: 135 us
  starting transfers between devices  49.6 us (36%)
  waiting for transfers between devices  45.8 us (34%)
  Pallas kernels  37 us (27%)
  other arithmetic  2.19 us (2%)
    ppermute x12, waiting for transfers between devices, along_chips(): return lax.ppermute(value, REP, chip_ring(shift, first))  24 us
    ppermute x12, starting transfers between devices, along_chips(): return lax.ppermute(value, REP, chip_ring(shift, first))  23 us
    ppermute x15, starting transfers between devices, along_x(): return lax.ppermute(value, 'x', x_ring(shift))  19.8 us
    ppermute x15, waiting for transfers between devices, along_x(): return lax.ppermute(value, 'x', x_ring(shift))  16.5 us
    pallas_call x8, Pallas kernels, down(): pl.pallas_call(lambda *refs: down_kernel(base, start, *refs), out_shape=j...  13 us
    pallas_call x1, Pallas kernels, attend_project(): pl.pallas_call(attend_kernel, out_shape=[out] * SIDE, in_specs=[SM] + [HB...  12.9 us
    pallas_call x1, Pallas kernels, gate_up_act(): pl.pallas_call(gate_up_kernel, out_shape=[jax.ShapeDtypeStruct((rows // 2...  8.47 us
    all_to_all x1, waiting for transfers between devices, local(): homes = lax.all_to_all(kept, 'x', 0, 0, tiled=True)  5.36 us
  transfers between devices with their start and end apart: 36, of which 18 were waited for; matrix products, arithmetic and copies ran while one was open for 1% of the time, Pallas kernels for 20%

profile of v3, /device:TPU:0, one launch (start us, length us, event | category | flops | bytes accessed | tf_op | source)
XLA Modules:
  0.0 135.2 jit_solution(16457747152321653968)
XLA Ops:
  0.0 1.3 split.1
  1.4 1.6 %collective-permute-start.3 = (bf16[344,1024]{1,0:T(8,128)(2,1)S(1)}, bf16[344,1024]{1,0:T(8,128)(2,1)}, u32[]{:S(2)}, u32[]{:S(2)}) collective-permute-start(bf16[344,1024]{1,0:T(8,128)(2,1)S(1)} %get-tuple-element.49.refs_8_), channel_id=1, source_target_pairs={{0,1},{1,2},{2,3},{3,0},{4,5},{5,6},{6,7},{7,4},{8,9},{9,10},{10,1... | collective-permute-start | bytes 2113544 | tf_op jit(solution)/shard_map/ppermute | solution.py:48
  3.0 1.7 %collective-permute-start.4 = (bf16[344,1024]{1,0:T(8,128)(2,1)S(1)}, bf16[344,1024]{1,0:T(8,128)(2,1)}, u32[]{:S(2)}, u32[]{:S(2)}) collective-permute-start(bf16[344,1024]{1,0:T(8,128)(2,1)S(1)} %get-tuple-element.50.refs_9_), channel_id=1, source_target_pairs={{0,3},{1,0},{2,1},{3,2},{4,7},{5,4},{6,5},{7,6},{8,11},{9,8},{10,9... | collective-permute-start | bytes 2113544 | tf_op jit(solution)/shard_map/ppermute | solution.py:48
  4.7 12.9 %attend_project.1 = (bf16[16,4224]{1,0:T(8,128)(2,1)S(1)}, bf16[16,4224]{1,0:T(8,128)(2,1)S(1)}, bf16[16,4224]{1,0:T(8,128)(2,1)S(1)}, bf16[16,4224]{1,0:T(8,128)(2,1)S(1)}) custom-call(s32[2]{0:T(128)S(1)} %pad_add_fusion.place.refs_0_, s32[2,64]{1,0:T(2,128)} %bitcast.22, s32[2048]{0:T(1024)} %spans.1, bf16[64,1024]{1,0:T(8,128)(2,1)} %query.1, ...), custom_call_target="tpu_custom_call" | custom-call | flops 536870912 | bytes 16777216 | tf_op jit(solution)/shard_map/attend_project/pallas_call | solution.py:188
  18.1 2.7 %collective-permute-start.1 = (bf16[16,4224]{1,0:T(8,128)(2,1)S(1)}, bf16[16,4224]{1,0:T(8,128)(2,1)S(1)}, u32[]{:S(2)}, u32[]{:S(2)}) collective-permute-start(bf16[16,4224]{1,0:T(8,128)(2,1)S(1)} %get-tuple-element.37), channel_id=1, source_target_pairs={{0,2},{1,3},{2,0},{3,1},{4,6},{5,7},{6,4},{7,5},{8,10},{9,11},{10,... | collective-permute-start | bytes 405512 | tf_op jit(solution)/shard_map/ppermute | solution.py:48
  20.8 1.4 %collective-permute-start.2 = (bf16[16,4224]{1,0:T(8,128)(2,1)S(1)}, bf16[16,4224]{1,0:T(8,128)(2,1)S(1)}, u32[]{:S(2)}, u32[]{:S(2)}) collective-permute-start(bf16[16,4224]{1,0:T(8,128)(2,1)S(1)} %get-tuple-element.38), channel_id=1, source_target_pairs={{0,3},{1,0},{2,1},{3,2},{4,7},{5,4},{6,5},{7,6},{8,11},{9,8},{10,9... | collective-permute-start | bytes 405512 | tf_op jit(solution)/shard_map/ppermute | solution.py:48
  22.3 2.7 %collective-permute-done.refs_1_ = bf16[16,4224]{1,0:T(8,128)(2,1)S(1)} collective-permute-done((bf16[16,4224]{1,0:T(8,128)(2,1)S(1)}, bf16[16,4224]{1,0:T(8,128)(2,1)S(1)}, u32[]{:S(2)}, u32[]{:S(2)}) %collective-permute-start) | collective-permute-done | bytes 135200 | tf_op jit(solution)/shard_map/ppermute | solution.py:48
  24.9 2.1 %collective-permute-done.1.refs_2_ = bf16[16,4224]{1,0:T(8,128)(2,1)S(1)} collective-permute-done((bf16[16,4224]{1,0:T(8,128)(2,1)S(1)}, bf16[16,4224]{1,0:T(8,128)(2,1)S(1)}, u32[]{:S(2)}, u32[]{:S(2)}) %collective-permute-start.1) | collective-permute-done | bytes 135200 | tf_op jit(solution)/shard_map/ppermute | solution.py:48
  27.1 1.3 normalise.1
  28.4 1.3 collective-permute-start.8
  29.8 1.9 %collective-permute-start.9 = (bf16[344,1024]{1,0:T(8,128)(2,1)}, bf16[344,1024]{1,0:T(8,128)(2,1)}, u32[]{:S(2)}, u32[]{:S(2)}) collective-permute-start(bf16[344,1024]{1,0:T(8,128)(2,1)} %collective-permute-done.4.refs_15_), channel_id=1, source_target_pairs={{0,3},{1,0},{2,1},{3,2},{4,7},{5,4},{6,5},{7,6},{8,11},{9,8},{10,9... | collective-permute-start | bytes 2113544 | tf_op jit(solution)/shard_map/ppermute | solution.py:48
  31.7 4.2 %collective-permute-start.7 = (bf16[16,4096]{1,0:T(8,128)(2,1)S(1)}, bf16[16,4096]{1,0:T(8,128)(2,1)S(1)}, u32[]{:S(2)}, u32[]{:S(2)}) collective-permute-start(bf16[16,4096]{1,0:T(8,128)(2,1)S(1)} %get-tuple-element.42.refs_0_), channel_id=1, source_target_pairs={{0,96},{4,28},{8,104},{12,4},{16,112},{20,12},{24,120},{28,20},{32... | collective-permute-start | bytes 393224 | tf_op jit(solution)/shard_map/ppermute | solution.py:52
  35.8 1.3 collective-permute-start.5
  37.1 3.3 %all-to-all-start = ((bf16[4,16,1024]{2,1,0:T(8,128)(2,1)}), bf16[4,16,1024]{2,1,0:T(8,128)(2,1)S(1)}, u32[]{:S(2)}, u32[]{:S(2)}) async-start(bf16[4,16,1024]{2,1,0:T(8,128)(2,1)} %get-tuple-element.45), calls=%async_computation | async-start | bytes 262144 | tf_op jit(solution)/shard_map/all_to_all | solution.py:454
  40.4 2.0 %collective-permute-done.6.refs_2_ = bf16[16,4096]{1,0:T(8,128)(2,1)S(1)} collective-permute-done((bf16[16,4096]{1,0:T(8,128)(2,1)S(1)}, bf16[16,4096]{1,0:T(8,128)(2,1)S(1)}, u32[]{:S(2)}, u32[]{:S(2)}) %collective-permute-start.6) | collective-permute-done | bytes 131104 | tf_op jit(solution)/shard_map/ppermute | solution.py:52
  42.4 1.0 collective-permute-done.5.refs_1_
  43.4 5.4 %all-to-all-done.refs_7_ = bf16[4,16,1024]{2,1,0:T(8,128)(2,1)S(1)} async-done(((bf16[4,16,1024]{2,1,0:T(8,128)(2,1)}), bf16[4,16,1024]{2,1,0:T(8,128)(2,1)S(1)}, u32[]{:S(2)}, u32[]{:S(2)}) %all-to-all-start) | async-done | bytes 131104 | tf_op jit(solution)/shard_map/all_to_all | solution.py:454
  48.8 2.0 %collective-permute-start.18 = (bf16[344,1024]{1,0:T(8,128)(2,1)S(1)}, bf16[344,1024]{1,0:T(8,128)(2,1)}, u32[]{:S(2)}, u32[]{:S(2)}) collective-permute-start(bf16[344,1024]{1,0:T(8,128)(2,1)S(1)} %get-tuple-element.49.refs_8_), channel_id=1, source_target_pairs={{0,3},{1,0},{2,1},{3,2},{4,7},{5,4},{6,5},{7,6},{8,11},{9,8},{10,9... | collective-permute-start | bytes 2113544 | tf_op jit(solution)/shard_map/ppermute | solution.py:48
  50.8 1.7 %collective-permute-start.10 = (bf16[64,4096]{1,0:T(8,128)(2,1)S(1)}, bf16[64,4096]{1,0:T(8,128)(2,1)}, u32[]{:S(2)}, u32[]{:S(2)}) collective-permute-start(bf16[64,4096]{1,0:T(8,128)(2,1)S(1)} %join.1.refs_0_), channel_id=1, source_target_pairs={{0,8},{4,36},{8,16},{12,44},{16,24},{20,52},{24,0},{28,60},{32,40}... | collective-permute-start | bytes 1572872 | tf_op jit(solution)/shard_map/ppermute | solution.py:52
  52.5 1.5 %collective-permute-start.12 = (bf16[64,4096]{1,0:T(8,128)(2,1)S(1)}, bf16[64,4096]{1,0:T(8,128)(2,1)}, u32[]{:S(2)}, u32[]{:S(2)}) collective-permute-start(bf16[64,4096]{1,0:T(8,128)(2,1)S(1)} %join.1.refs_0_), channel_id=1, source_target_pairs={{0,24},{4,100},{8,0},{12,108},{16,8},{20,116},{24,16},{28,124},{32... | collective-permute-start | bytes 1572872 | tf_op jit(solution)/shard_map/ppermute | solution.py:52
  54.0 2.1 %collective-permute-start.11 = (bf16[64,4096]{1,0:T(8,128)(2,1)S(1)}, bf16[64,4096]{1,0:T(8,128)(2,1)}, u32[]{:S(2)}, u32[]{:S(2)}) collective-permute-start(bf16[64,4096]{1,0:T(8,128)(2,1)S(1)} %join.1.refs_0_), channel_id=1, source_target_pairs={{0,16},{4,68},{8,24},{12,76},{16,0},{20,84},{24,8},{28,92},{32,48}... | collective-permute-start | bytes 1572872 | tf_op jit(solution)/shard_map/ppermute | solution.py:52
  56.7 4.6 %collective-permute-done.10.refs_1_ = bf16[64,4096]{1,0:T(8,128)(2,1)} collective-permute-done((bf16[64,4096]{1,0:T(8,128)(2,1)S(1)}, bf16[64,4096]{1,0:T(8,128)(2,1)}, u32[]{:S(2)}, u32[]{:S(2)}) %collective-permute-start.10) | collective-permute-done | bytes 524320 | tf_op jit(solution)/shard_map/ppermute | solution.py:52
  61.8 1.6 %collective-permute-start.14 = (bf16[64,4096]{1,0:T(8,128)(2,1)}, bf16[64,4096]{1,0:T(8,128)(2,1)}, u32[]{:S(2)}, u32[]{:S(2)}) collective-permute-start(bf16[64,4096]{1,0:T(8,128)(2,1)} %collective-permute-done.10.refs_1_), channel_id=1, source_target_pairs={{0,4},{4,0},{1,5},{5,1},{2,6},{6,2},{3,7},{7,3},{8,12},{12,8},{9,1... | collective-permute-start | bytes 1572872 | tf_op jit(solution)/shard_map/ppermute | solution.py:56
  63.4 4.9 %collective-permute-done.11.refs_2_ = bf16[64,4096]{1,0:T(8,128)(2,1)} collective-permute-done((bf16[64,4096]{1,0:T(8,128)(2,1)S(1)}, bf16[64,4096]{1,0:T(8,128)(2,1)}, u32[]{:S(2)}, u32[]{:S(2)}) %collective-permute-start.11) | collective-permute-done | bytes 524320 | tf_op jit(solution)/shard_map/ppermute | solution.py:52
  69.8 2.2 %collective-permute-done.17.refs_11_ = bf16[344,1024]{1,0:T(8,128)(2,1)} collective-permute-done((bf16[344,1024]{1,0:T(8,128)(2,1)S(1)}, bf16[344,1024]{1,0:T(8,128)(2,1)}, u32[]{:S(2)}, u32[]{:S(2)}) %collective-permute-start.17) | collective-permute-done | bytes 704544 | tf_op jit(solution)/shard_map/ppermute | solution.py:48
  72.0 8.5 %gate_up_act.1 = (bf16[256,344]{1,0:T(8,128)(2,1)S(1)}, bf16[256,344]{1,0:T(8,128)(2,1)S(1)}) custom-call(s32[2]{0:T(128)S(1)} %pad_add_fusion.place.refs_0_, s32[32]{0:T(128)S(1)} %get-tuple-element.68.source, bf16[64,4096]{1,0:T(8,128)(2,1)S(1)} %join.1.refs_0_, bf16[64,4096]{1,0:T(8,128)(2,1)} %collective-permute-done.10.refs_1_, ...), custom_call_target="tpu_custom_call" | custom-call | flops 2885681152 | bytes 14090240 | tf_op jit(solution)/shard_map/gate_up_act/pallas_call | solution.py:349
  80.6 3.2 %collective-permute-start.23 = (bf16[256,344]{1,0:T(8,128)(2,1)S(1)}, bf16[256,344]{1,0:T(8,128)(2,1)S(1)}, u32[]{:S(2)}, u32[]{:S(2)}) collective-permute-start(bf16[256,344]{1,0:T(8,128)(2,1)S(1)} %get-tuple-element.56.refs_3_), channel_id=1, source_target_pairs={{0,3},{1,0},{2,1},{3,2},{4,7},{5,4},{6,5},{7,6},{8,11},{9,8},{10,9... | collective-permute-start | bytes 528392 | tf_op jit(solution)/shard_map/ppermute | solution.py:48
  83.8 3.2 %collective-permute-start.21 = (bf16[256,344]{1,0:T(8,128)(2,1)S(1)}, bf16[256,344]{1,0:T(8,128)(2,1)S(1)}, u32[]{:S(2)}, u32[]{:S(2)}) collective-permute-start(bf16[256,344]{1,0:T(8,128)(2,1)S(1)} %get-tuple-element.57.refs_3_), channel_id=1, source_target_pairs={{0,3},{1,0},{2,1},{3,2},{4,7},{5,4},{6,5},{7,6},{8,11},{9,8},{10,9... | collective-permute-start | bytes 528392 | tf_op jit(solution)/shard_map/ppermute | solution.py:48
  87.0 2.4 %collective-permute-done.19.refs_4_ = bf16[256,344]{1,0:T(8,128)(2,1)S(1)} collective-permute-done((bf16[256,344]{1,0:T(8,128)(2,1)S(1)}, bf16[256,344]{1,0:T(8,128)(2,1)S(1)}, u32[]{:S(2)}, u32[]{:S(2)}) %collective-permute-start.19) | collective-permute-done | bytes 176160 | tf_op jit(solution)/shard_map/ppermute | solution.py:48
  89.4 4.2 %collective-permute-done.22.refs_4_ = bf16[256,344]{1,0:T(8,128)(2,1)S(1)} collective-permute-done((bf16[256,344]{1,0:T(8,128)(2,1)S(1)}, bf16[256,344]{1,0:T(8,128)(2,1)S(1)}, u32[]{:S(2)}, u32[]{:S(2)}) %collective-permute-start.22) | collective-permute-done | bytes 176160 | tf_op jit(solution)/shard_map/ppermute | solution.py:48
  93.7 2.7 %collective-permute-done.20.refs_5_ = bf16[256,344]{1,0:T(8,128)(2,1)S(1)} collective-permute-done((bf16[256,344]{1,0:T(8,128)(2,1)S(1)}, bf16[256,344]{1,0:T(8,128)(2,1)S(1)}, u32[]{:S(2)}, u32[]{:S(2)}) %collective-permute-start.20) | collective-permute-done | bytes 176160 | tf_op jit(solution)/shard_map/ppermute | solution.py:48
  96.3 1.6 %down.9 = bf16[4,4,16,1024]{3,2,1,0:T(8,128)(2,1)S(1)} custom-call(s32[2]{0:T(128)S(1)} %pad_add_fusion.place.refs_0_, s32[1]{0:T(128)} %bitcast.2.refs_1_, bf16[344,1024]{1,0:T(8,128)(2,1)S(1)} %copy-done, bf16[256,344]{1,0:T(8,128)(2,1)S(1)} %get-tuple-element.57.refs_3_, bf16[256,344]{1,0:T(8,128)(2,1)S(1)} %collective-permute-done.19.refs_4_, ...), custom_call_target="tpu_custom_call" | custom-call | flops 180355072 | bytes 704512 | tf_op jit(solution)/shard_map/down/pallas_call | solution.py:392
  98.1 1.6 %down.12 = bf16[4,4,16,1024]{3,2,1,0:T(8,128)(2,1)S(1)} custom-call(s32[2]{0:T(128)S(1)} %pad_add_fusion.place.refs_0_, s32[1]{0:T(128)} %bitcast.2.refs_1_, bf16[344,1024]{1,0:T(8,128)(2,1)S(1)} %copy-done, bf16[256,344]{1,0:T(8,128)(2,1)S(1)} %get-tuple-element.57.refs_3_, bf16[256,344]{1,0:T(8,128)(2,1)S(1)} %collective-permute-done.19.refs_4_, ...), custom_call_target="tpu_custom_call" | custom-call | flops 180355072 | bytes 704512 | tf_op jit(solution)/shard_map/down/pallas_call | solution.py:392
  100.3 1.6 %down.8 = bf16[4,4,16,1024]{3,2,1,0:T(8,128)(2,1)S(1)} custom-call(s32[2]{0:T(128)S(1)} %pad_add_fusion.place.refs_0_, s32[1]{0:T(128)} %bitcast.2.refs_1_, bf16[344,1024]{1,0:T(8,128)(2,1)S(1)} %copy-done, bf16[256,344]{1,0:T(8,128)(2,1)S(1)} %get-tuple-element.57.refs_3_, bf16[256,344]{1,0:T(8,128)(2,1)S(1)} %collective-permute-done.19.refs_4_, ...), custom_call_target="tpu_custom_call" | custom-call | flops 180355072 | bytes 704512 | tf_op jit(solution)/shard_map/down/pallas_call | solution.py:392
  102.0 1.6 %down.14 = bf16[4,4,16,1024]{3,2,1,0:T(8,128)(2,1)S(1)} custom-call(s32[2]{0:T(128)S(1)} %pad_add_fusion.place.refs_0_, s32[1]{0:T(128)} %bitcast.2.refs_1_, bf16[344,1024]{1,0:T(8,128)(2,1)S(1)} %copy-done, bf16[256,344]{1,0:T(8,128)(2,1)S(1)} %get-tuple-element.57.refs_3_, bf16[256,344]{1,0:T(8,128)(2,1)S(1)} %collective-permute-done.19.refs_4_, ...), custom_call_target="tpu_custom_call" | custom-call | flops 180355072 | bytes 704512 | tf_op jit(solution)/shard_map/down/pallas_call | solution.py:392
  104.2 1.6 %down.10 = bf16[4,4,16,1024]{3,2,1,0:T(8,128)(2,1)S(1)} custom-call(s32[2]{0:T(128)S(1)} %pad_add_fusion.place.refs_0_, s32[1]{0:T(128)} %bitcast.2.refs_1_, bf16[344,1024]{1,0:T(8,128)(2,1)S(1)} %copy-done, bf16[256,344]{1,0:T(8,128)(2,1)S(1)} %get-tuple-element.56.refs_3_, bf16[256,344]{1,0:T(8,128)(2,1)S(1)} %collective-permute-done.22.refs_4_, ...), custom_call_target="tpu_custom_call" | custom-call | flops 180355072 | bytes 704512 | tf_op jit(solution)/shard_map/down/pallas_call | solution.py:392
  105.9 3.2 %collective-permute-start.26 = (bf16[4,4,16,1024]{3,2,1,0:T(8,128)(2,1)S(1)}, bf16[4,4,16,1024]{3,2,1,0:T(8,128)(2,1)S(1)}, u32[]{:S(2)}, u32[]{:S(2)}) collective-permute-start(bf16[4,4,16,1024]{3,2,1,0:T(8,128)(2,1)S(1)} %down.10), channel_id=1, source_target_pairs={{0,16},{4,68},{8,24},{12,76},{16,0},{20,84},{24,8},{28,92},{32,48}... | collective-permute-start | bytes 1572872 | tf_op jit(solution)/shard_map/ppermute | solution.py:52
  109.0 1.6 %down.13 = bf16[4,4,16,1024]{3,2,1,0:T(8,128)(2,1)S(1)} custom-call(s32[2]{0:T(128)S(1)} %pad_add_fusion.place.refs_0_, s32[1]{0:T(128)} %bitcast.2.refs_1_, bf16[344,1024]{1,0:T(8,128)(2,1)S(1)} %copy-done, bf16[256,344]{1,0:T(8,128)(2,1)S(1)} %get-tuple-element.56.refs_3_, bf16[256,344]{1,0:T(8,128)(2,1)S(1)} %collective-permute-done.22.refs_4_, ...), custom_call_target="tpu_custom_call" | custom-call | flops 180355072 | bytes 704512 | tf_op jit(solution)/shard_map/down/pallas_call | solution.py:392
  110.7 0.9 collective-permute-start.30
  111.6 1.6 %down.11 = bf16[4,4,16,1024]{3,2,1,0:T(8,128)(2,1)S(1)} custom-call(s32[2]{0:T(128)S(1)} %pad_add_fusion.place.refs_0_, s32[1]{0:T(128)} %bitcast.2.refs_1_, bf16[344,1024]{1,0:T(8,128)(2,1)S(1)} %copy-done, bf16[256,344]{1,0:T(8,128)(2,1)S(1)} %get-tuple-element.56.refs_3_, bf16[256,344]{1,0:T(8,128)(2,1)S(1)} %collective-permute-done.22.refs_4_, ...), custom_call_target="tpu_custom_call" | custom-call | flops 180355072 | bytes 704512 | tf_op jit(solution)/shard_map/down/pallas_call | solution.py:392
  113.2 2.5 %collective-permute-start.28 = (bf16[4,4,16,1024]{3,2,1,0:T(8,128)(2,1)S(1)}, bf16[4,4,16,1024]{3,2,1,0:T(8,128)(2,1)S(1)}, u32[]{:S(2)}, u32[]{:S(2)}) collective-permute-start(bf16[4,4,16,1024]{3,2,1,0:T(8,128)(2,1)S(1)} %down.11), channel_id=1, source_target_pairs={{0,24},{4,100},{8,0},{12,108},{16,8},{20,116},{24,16},{28,124},{32... | collective-permute-start | bytes 1572872 | tf_op jit(solution)/shard_map/ppermute | solution.py:52
  115.7 1.6 %down.15 = bf16[4,4,16,1024]{3,2,1,0:T(8,128)(2,1)S(1)} custom-call(s32[2]{0:T(128)S(1)} %pad_add_fusion.place.refs_0_, s32[1]{0:T(128)} %bitcast.2.refs_1_, bf16[344,1024]{1,0:T(8,128)(2,1)S(1)} %copy-done, bf16[256,344]{1,0:T(8,128)(2,1)S(1)} %get-tuple-element.56.refs_3_, bf16[256,344]{1,0:T(8,128)(2,1)S(1)} %collective-permute-done.22.refs_4_, ...), custom_call_target="tpu_custom_call" | custom-call | flops 180355072 | bytes 704512 | tf_op jit(solution)/shard_map/down/pallas_call | solution.py:392
  117.3 4.9 %collective-permute-done.30 = bf16[4,4,16,1024]{3,2,1,0:T(8,128)(2,1)S(1)} collective-permute-done((bf16[4,4,16,1024]{3,2,1,0:T(8,128)(2,1)S(1)}, bf16[4,4,16,1024]{3,2,1,0:T(8,128)(2,1)S(1)}, u32[]{:S(2)}, u32[]{:S(2)}) %collective-permute-start.30) | collective-permute-done | bytes 524320 | tf_op jit(solution)/shard_map/ppermute | solution.py:52
  123.1 3.8 %collective-permute-start.32 = (bf16[4,16,1024]{2,1,0:T(8,128)(2,1)S(1)}, bf16[4,16,1024]{2,1,0:T(8,128)(2,1)S(1)}, u32[]{:S(2)}, u32[]{:S(2)}) collective-permute-start(bf16[4,16,1024]{2,1,0:T(8,128)(2,1)S(1)} %get-tuple-element.65), channel_id=1, source_target_pairs={{0,96},{4,28},{8,104},{12,4},{16,112},{20,12},{24,120},{28,20},{32... | collective-permute-start | bytes 393224 | tf_op jit(solution)/shard_map/ppermute | solution.py:52
  126.9 1.9 %collective-permute-start.33 = (bf16[4,16,1024]{2,1,0:T(8,128)(2,1)S(1)}, bf16[4,16,1024]{2,1,0:T(8,128)(2,1)S(1)}, u32[]{:S(2)}, u32[]{:S(2)}) collective-permute-start(bf16[4,16,1024]{2,1,0:T(8,128)(2,1)S(1)} %get-tuple-element.67), channel_id=1, source_target_pairs={{0,64},{4,20},{8,72},{12,28},{16,80},{20,4},{24,88},{28,12},{32,96... | collective-permute-start | bytes 393224 | tf_op jit(solution)/shard_map/ppermute | solution.py:52
  128.8 0.6 collective-permute-done.32
  129.4 5.1 %collective-permute-done.34 = bf16[4,16,1024]{2,1,0:T(8,128)(2,1)S(1)} collective-permute-done((bf16[4,16,1024]{2,1,0:T(8,128)(2,1)S(1)}, bf16[4,16,1024]{2,1,0:T(8,128)(2,1)S(1)}, u32[]{:S(2)}, u32[]{:S(2)}) %collective-permute-start.34) | collective-permute-done | bytes 131104 | tf_op jit(solution)/shard_map/ppermute | solution.py:52
  134.5 0.7 fusion.2
  (60 shorter events, 5.5 us)
Async XLA Ops:
  1.3 47.5 %copy-start.1 = (bf16[344,1024]{1,0:T(8,128)(2,1)}, bf16[344,1024]{1,0:T(8,128)(2,1)S(1)}, u32[]{:S(2)}) copy-start(bf16[344,1024]{1,0:T(8,128)(2,1)S(1)} %get-tuple-element.49.refs_8_) | copy-start | bytes 2113540
  1.4 54.8 %copy-start.2 = (bf16[344,1024]{1,0:T(8,128)(2,1)}, bf16[344,1024]{1,0:T(8,128)(2,1)S(1)}, u32[]{:S(2)}) copy-start(bf16[344,1024]{1,0:T(8,128)(2,1)S(1)} %get-tuple-element.50.refs_9_) | copy-start | bytes 2113540
  1.4 27.1 %collective-permute-start.3 = (bf16[344,1024]{1,0:T(8,128)(2,1)S(1)}, bf16[344,1024]{1,0:T(8,128)(2,1)}, u32[]{:S(2)}, u32[]{:S(2)}) collective-permute-start(bf16[344,1024]{1,0:T(8,128)(2,1)S(1)} %get-tuple-element.49.refs_8_), channel_id=1, source_target_pairs={{0,1},{1,2},{2,3},{3,0},{4,5},{5,6},{6,7},{7,4},{8,9},{9,10},{10,1... | collective-permute-start | bytes 2113544 | tf_op jit(solution)/shard_map/ppermute | solution.py:48
  3.0 25.4 %collective-permute-start.4 = (bf16[344,1024]{1,0:T(8,128)(2,1)S(1)}, bf16[344,1024]{1,0:T(8,128)(2,1)}, u32[]{:S(2)}, u32[]{:S(2)}) collective-permute-start(bf16[344,1024]{1,0:T(8,128)(2,1)S(1)} %get-tuple-element.50.refs_9_), channel_id=1, source_target_pairs={{0,3},{1,0},{2,1},{3,2},{4,7},{5,4},{6,5},{7,6},{8,11},{9,8},{10,9... | collective-permute-start | bytes 2113544 | tf_op jit(solution)/shard_map/ppermute | solution.py:48
  4.7 64.1 %copy-start.3 = (s32[32]{0:T(128)S(1)}, s32[32]{0:T(128)}, u32[]{:S(2)}) copy-start(s32[32]{0:T(128)} %param.17) | copy-start | bytes 388
  17.6 78.7 %copy-start = (bf16[344,1024]{1,0:T(8,128)(2,1)S(1)}, bf16[344,1024]{1,0:T(8,128)(2,1)}, u32[]{:S(2)}) copy-start(bf16[344,1024]{1,0:T(8,128)(2,1)} %refs_2_.15) | copy-start | bytes 2113540
  17.7 7.3 %collective-permute-start = (bf16[16,4224]{1,0:T(8,128)(2,1)S(1)}, bf16[16,4224]{1,0:T(8,128)(2,1)S(1)}, u32[]{:S(2)}, u32[]{:S(2)}) collective-permute-start(bf16[16,4224]{1,0:T(8,128)(2,1)S(1)} %get-tuple-element.36), channel_id=1, source_target_pairs={{0,1},{1,2},{2,3},{3,0},{4,5},{5,6},{6,7},{7,4},{8,9},{9,10},{10,1... | collective-permute-start | bytes 405512 | tf_op jit(solution)/shard_map/ppermute | solution.py:48
  18.1 8.9 %collective-permute-start.1 = (bf16[16,4224]{1,0:T(8,128)(2,1)S(1)}, bf16[16,4224]{1,0:T(8,128)(2,1)S(1)}, u32[]{:S(2)}, u32[]{:S(2)}) collective-permute-start(bf16[16,4224]{1,0:T(8,128)(2,1)S(1)} %get-tuple-element.37), channel_id=1, source_target_pairs={{0,2},{1,3},{2,0},{3,1},{4,6},{5,7},{6,4},{7,5},{8,10},{9,11},{10,... | collective-permute-start | bytes 405512 | tf_op jit(solution)/shard_map/ppermute | solution.py:48
  20.8 6.3 %collective-permute-start.2 = (bf16[16,4224]{1,0:T(8,128)(2,1)S(1)}, bf16[16,4224]{1,0:T(8,128)(2,1)S(1)}, u32[]{:S(2)}, u32[]{:S(2)}) collective-permute-start(bf16[16,4224]{1,0:T(8,128)(2,1)S(1)} %get-tuple-element.38), channel_id=1, source_target_pairs={{0,3},{1,0},{2,1},{3,2},{4,7},{5,4},{6,5},{7,6},{8,11},{9,8},{10,9... | collective-permute-start | bytes 405512 | tf_op jit(solution)/shard_map/ppermute | solution.py:48
  28.4 20.4 %collective-permute-start.8 = (bf16[344,1024]{1,0:T(8,128)(2,1)}, bf16[344,1024]{1,0:T(8,128)(2,1)}, u32[]{:S(2)}, u32[]{:S(2)}) collective-permute-start(bf16[344,1024]{1,0:T(8,128)(2,1)} %collective-permute-done.3.refs_10_), channel_id=1, source_target_pairs={{0,1},{1,2},{2,3},{3,0},{4,5},{5,6},{6,7},{7,4},{8,9},{9,10},{10,1... | collective-permute-start | bytes 2113544 | tf_op jit(solution)/shard_map/ppermute | solution.py:48
  29.8 19.1 %collective-permute-start.9 = (bf16[344,1024]{1,0:T(8,128)(2,1)}, bf16[344,1024]{1,0:T(8,128)(2,1)}, u32[]{:S(2)}, u32[]{:S(2)}) collective-permute-start(bf16[344,1024]{1,0:T(8,128)(2,1)} %collective-permute-done.4.refs_15_), channel_id=1, source_target_pairs={{0,3},{1,0},{2,1},{3,2},{4,7},{5,4},{6,5},{7,6},{8,11},{9,8},{10,9... | collective-permute-start | bytes 2113544 | tf_op jit(solution)/shard_map/ppermute | solution.py:48
  31.7 8.7 %collective-permute-start.7 = (bf16[16,4096]{1,0:T(8,128)(2,1)S(1)}, bf16[16,4096]{1,0:T(8,128)(2,1)S(1)}, u32[]{:S(2)}, u32[]{:S(2)}) collective-permute-start(bf16[16,4096]{1,0:T(8,128)(2,1)S(1)} %get-tuple-element.42.refs_0_), channel_id=1, source_target_pairs={{0,96},{4,28},{8,104},{12,4},{16,112},{20,12},{24,120},{28,20},{32... | collective-permute-start | bytes 393224 | tf_op jit(solution)/shard_map/ppermute | solution.py:52
  35.8 6.6 %collective-permute-start.6 = (bf16[16,4096]{1,0:T(8,128)(2,1)S(1)}, bf16[16,4096]{1,0:T(8,128)(2,1)S(1)}, u32[]{:S(2)}, u32[]{:S(2)}) collective-permute-start(bf16[16,4096]{1,0:T(8,128)(2,1)S(1)} %get-tuple-element.42.refs_0_), channel_id=1, source_target_pairs={{0,64},{4,20},{8,72},{12,28},{16,80},{20,4},{24,88},{28,12},{32,96... | collective-permute-start | bytes 393224 | tf_op jit(solution)/shard_map/ppermute | solution.py:52
  35.8 7.6 %collective-permute-start.5 = (bf16[16,4096]{1,0:T(8,128)(2,1)S(1)}, bf16[16,4096]{1,0:T(8,128)(2,1)S(1)}, u32[]{:S(2)}, u32[]{:S(2)}) collective-permute-start(bf16[16,4096]{1,0:T(8,128)(2,1)S(1)} %get-tuple-element.42.refs_0_), channel_id=1, source_target_pairs={{0,32},{4,12},{8,40},{12,20},{16,48},{20,28},{24,56},{28,4},{32,64... | collective-permute-start | bytes 393224 | tf_op jit(solution)/shard_map/ppermute | solution.py:52
  37.1 11.7 %all-to-all-start = ((bf16[4,16,1024]{2,1,0:T(8,128)(2,1)}), bf16[4,16,1024]{2,1,0:T(8,128)(2,1)S(1)}, u32[]{:S(2)}, u32[]{:S(2)}) async-start(bf16[4,16,1024]{2,1,0:T(8,128)(2,1)} %get-tuple-element.45), calls=%async_computation | async-start | bytes 262144 | tf_op jit(solution)/shard_map/all_to_all | solution.py:454
  48.8 19.5 %collective-permute-start.18 = (bf16[344,1024]{1,0:T(8,128)(2,1)S(1)}, bf16[344,1024]{1,0:T(8,128)(2,1)}, u32[]{:S(2)}, u32[]{:S(2)}) collective-permute-start(bf16[344,1024]{1,0:T(8,128)(2,1)S(1)} %get-tuple-element.49.refs_8_), channel_id=1, source_target_pairs={{0,3},{1,0},{2,1},{3,2},{4,7},{5,4},{6,5},{7,6},{8,11},{9,8},{10,9... | collective-permute-start | bytes 2113544 | tf_op jit(solution)/shard_map/ppermute | solution.py:48
  50.8 10.5 %collective-permute-start.10 = (bf16[64,4096]{1,0:T(8,128)(2,1)S(1)}, bf16[64,4096]{1,0:T(8,128)(2,1)}, u32[]{:S(2)}, u32[]{:S(2)}) collective-permute-start(bf16[64,4096]{1,0:T(8,128)(2,1)S(1)} %join.1.refs_0_), channel_id=1, source_target_pairs={{0,8},{4,36},{8,16},{12,44},{16,24},{20,52},{24,0},{28,60},{32,40}... | collective-permute-start | bytes 1572872 | tf_op jit(solution)/shard_map/ppermute | solution.py:52
  52.5 9.3 %collective-permute-start.12 = (bf16[64,4096]{1,0:T(8,128)(2,1)S(1)}, bf16[64,4096]{1,0:T(8,128)(2,1)}, u32[]{:S(2)}, u32[]{:S(2)}) collective-permute-start(bf16[64,4096]{1,0:T(8,128)(2,1)S(1)} %join.1.refs_0_), channel_id=1, source_target_pairs={{0,24},{4,100},{8,0},{12,108},{16,8},{20,116},{24,16},{28,124},{32... | collective-permute-start | bytes 1572872 | tf_op jit(solution)/shard_map/ppermute | solution.py:52
  54.0 14.2 %collective-permute-start.11 = (bf16[64,4096]{1,0:T(8,128)(2,1)S(1)}, bf16[64,4096]{1,0:T(8,128)(2,1)}, u32[]{:S(2)}, u32[]{:S(2)}) collective-permute-start(bf16[64,4096]{1,0:T(8,128)(2,1)S(1)} %join.1.refs_0_), channel_id=1, source_target_pairs={{0,16},{4,68},{8,24},{12,76},{16,0},{20,84},{24,8},{28,92},{32,48}... | collective-permute-start | bytes 1572872 | tf_op jit(solution)/shard_map/ppermute | solution.py:52
  56.1 15.8 %collective-permute-start.17 = (bf16[344,1024]{1,0:T(8,128)(2,1)S(1)}, bf16[344,1024]{1,0:T(8,128)(2,1)}, u32[]{:S(2)}, u32[]{:S(2)}) collective-permute-start(bf16[344,1024]{1,0:T(8,128)(2,1)S(1)} %get-tuple-element.50.refs_9_), channel_id=1, source_target_pairs={{0,1},{1,2},{2,3},{3,0},{4,5},{5,6},{6,7},{7,4},{8,9},{9,10},{10,1... | collective-permute-start | bytes 2113544 | tf_op jit(solution)/shard_map/ppermute | solution.py:48
  61.3 10.7 %collective-permute-start.13 = (bf16[64,4096]{1,0:T(8,128)(2,1)S(1)}, bf16[64,4096]{1,0:T(8,128)(2,1)}, u32[]{:S(2)}, u32[]{:S(2)}) collective-permute-start(bf16[64,4096]{1,0:T(8,128)(2,1)S(1)} %join.1.refs_0_), channel_id=1, source_target_pairs={{0,4},{4,0},{1,5},{5,1},{2,6},{6,2},{3,7},{7,3},{8,12},{12,8},{9,1... | collective-permute-start | bytes 1572872 | tf_op jit(solution)/shard_map/ppermute | solution.py:56
  61.8 10.2 %collective-permute-start.14 = (bf16[64,4096]{1,0:T(8,128)(2,1)}, bf16[64,4096]{1,0:T(8,128)(2,1)}, u32[]{:S(2)}, u32[]{:S(2)}) collective-permute-start(bf16[64,4096]{1,0:T(8,128)(2,1)} %collective-permute-done.10.refs_1_), channel_id=1, source_target_pairs={{0,4},{4,0},{1,5},{5,1},{2,6},{6,2},{3,7},{7,3},{8,12},{12,8},{9,1... | collective-permute-start | bytes 1572872 | tf_op jit(solution)/shard_map/ppermute | solution.py:56
  68.3 3.7 %collective-permute-start.16 = (bf16[64,4096]{1,0:T(8,128)(2,1)}, bf16[64,4096]{1,0:T(8,128)(2,1)}, u32[]{:S(2)}, u32[]{:S(2)}) collective-permute-start(bf16[64,4096]{1,0:T(8,128)(2,1)} %collective-permute-done.12.refs_3_), channel_id=1, source_target_pairs={{0,4},{4,0},{1,5},{5,1},{2,6},{6,2},{3,7},{7,3},{8,12},{12,8},{9,1... | collective-permute-start | bytes 1572872 | tf_op jit(solution)/shard_map/ppermute | solution.py:56
  68.3 3.7 %collective-permute-start.15 = (bf16[64,4096]{1,0:T(8,128)(2,1)}, bf16[64,4096]{1,0:T(8,128)(2,1)S(1)}, u32[]{:S(2)}, u32[]{:S(2)}) collective-permute-start(bf16[64,4096]{1,0:T(8,128)(2,1)} %collective-permute-done.11.refs_2_), channel_id=1, source_target_pairs={{0,4},{4,0},{1,5},{5,1},{2,6},{6,2},{3,7},{7,3},{8,12},{12,8},{9,1... | collective-permute-start | bytes 1572872 | tf_op jit(solution)/shard_map/ppermute | solution.py:56
  80.5 8.9 %collective-permute-start.19 = (bf16[256,344]{1,0:T(8,128)(2,1)S(1)}, bf16[256,344]{1,0:T(8,128)(2,1)S(1)}, u32[]{:S(2)}, u32[]{:S(2)}) collective-permute-start(bf16[256,344]{1,0:T(8,128)(2,1)S(1)} %get-tuple-element.57.refs_3_), channel_id=1, source_target_pairs={{0,1},{1,2},{2,3},{3,0},{4,5},{5,6},{6,7},{7,4},{8,9},{9,10},{10,1... | collective-permute-start | bytes 528392 | tf_op jit(solution)/shard_map/ppermute | solution.py:48
  80.6 8.9 %collective-permute-start.23 = (bf16[256,344]{1,0:T(8,128)(2,1)S(1)}, bf16[256,344]{1,0:T(8,128)(2,1)S(1)}, u32[]{:S(2)}, u32[]{:S(2)}) collective-permute-start(bf16[256,344]{1,0:T(8,128)(2,1)S(1)} %get-tuple-element.56.refs_3_), channel_id=1, source_target_pairs={{0,3},{1,0},{2,1},{3,2},{4,7},{5,4},{6,5},{7,6},{8,11},{9,8},{10,9... | collective-permute-start | bytes 528392 | tf_op jit(solution)/shard_map/ppermute | solution.py:48
  83.8 9.9 %collective-permute-start.22 = (bf16[256,344]{1,0:T(8,128)(2,1)S(1)}, bf16[256,344]{1,0:T(8,128)(2,1)S(1)}, u32[]{:S(2)}, u32[]{:S(2)}) collective-permute-start(bf16[256,344]{1,0:T(8,128)(2,1)S(1)} %get-tuple-element.56.refs_3_), channel_id=1, source_target_pairs={{0,1},{1,2},{2,3},{3,0},{4,5},{5,6},{6,7},{7,4},{8,9},{9,10},{10,1... | collective-permute-start | bytes 528392 | tf_op jit(solution)/shard_map/ppermute | solution.py:48
  83.8 9.9 %collective-permute-start.21 = (bf16[256,344]{1,0:T(8,128)(2,1)S(1)}, bf16[256,344]{1,0:T(8,128)(2,1)S(1)}, u32[]{:S(2)}, u32[]{:S(2)}) collective-permute-start(bf16[256,344]{1,0:T(8,128)(2,1)S(1)} %get-tuple-element.57.refs_3_), channel_id=1, source_target_pairs={{0,3},{1,0},{2,1},{3,2},{4,7},{5,4},{6,5},{7,6},{8,11},{9,8},{10,9... | collective-permute-start | bytes 528392 | tf_op jit(solution)/shard_map/ppermute | solution.py:48
  89.4 6.9 %collective-permute-start.20 = (bf16[256,344]{1,0:T(8,128)(2,1)S(1)}, bf16[256,344]{1,0:T(8,128)(2,1)S(1)}, u32[]{:S(2)}, u32[]{:S(2)}) collective-permute-start(bf16[256,344]{1,0:T(8,128)(2,1)S(1)} %collective-permute-done.19.refs_4_), channel_id=1, source_target_pairs={{0,1},{1,2},{2,3},{3,0},{4,5},{5,6},{6,7},{7,4},{8,9},{9,10},{10,1... | collective-permute-start | bytes 528392 | tf_op jit(solution)/shard_map/ppermute | solution.py:48
  96.3 5.7 %collective-permute-start.24 = (bf16[256,344]{1,0:T(8,128)(2,1)S(1)}, bf16[256,344]{1,0:T(8,128)(2,1)S(1)}, u32[]{:S(2)}, u32[]{:S(2)}) collective-permute-start(bf16[256,344]{1,0:T(8,128)(2,1)S(1)} %collective-permute-done.23.refs_6_), channel_id=1, source_target_pairs={{0,3},{1,0},{2,1},{3,2},{4,7},{5,4},{6,5},{7,6},{8,11},{9,8},{10,9... | collective-permute-start | bytes 528392 | tf_op jit(solution)/shard_map/ppermute | solution.py:48
  98.0 6.3 %collective-permute-start.25 = (bf16[4,4,16,1024]{3,2,1,0:T(8,128)(2,1)S(1)}, bf16[4,4,16,1024]{3,2,1,0:T(8,128)(2,1)S(1)}, u32[]{:S(2)}, u32[]{:S(2)}) collective-permute-start(bf16[4,4,16,1024]{3,2,1,0:T(8,128)(2,1)S(1)} %down.9), channel_id=1, source_target_pairs={{0,4},{4,0},{1,5},{5,1},{2,6},{6,2},{3,7},{7,3},{8,12},{12,8},{9,1... | collective-permute-start | bytes 1572872 | tf_op jit(solution)/shard_map/ppermute | solution.py:56
  99.7 9.4 %collective-permute-start.29 = (bf16[4,4,16,1024]{3,2,1,0:T(8,128)(2,1)S(1)}, bf16[4,4,16,1024]{3,2,1,0:T(8,128)(2,1)S(1)}, u32[]{:S(2)}, u32[]{:S(2)}) collective-permute-start(bf16[4,4,16,1024]{3,2,1,0:T(8,128)(2,1)S(1)} %down.12), channel_id=1, source_target_pairs={{0,4},{4,0},{1,5},{5,1},{2,6},{6,2},{3,7},{7,3},{8,12},{12,8},{9,1... | collective-permute-start | bytes 1572872 | tf_op jit(solution)/shard_map/ppermute | solution.py:56
  102.0 9.6 %collective-permute-start.27 = (bf16[4,4,16,1024]{3,2,1,0:T(8,128)(2,1)S(1)}, bf16[4,4,16,1024]{3,2,1,0:T(8,128)(2,1)S(1)}, u32[]{:S(2)}, u32[]{:S(2)}) collective-permute-start(bf16[4,4,16,1024]{3,2,1,0:T(8,128)(2,1)S(1)} %down.8), channel_id=1, source_target_pairs={{0,4},{4,0},{1,5},{5,1},{2,6},{6,2},{3,7},{7,3},{8,12},{12,8},{9,1... | collective-permute-start | bytes 1572872 | tf_op jit(solution)/shard_map/ppermute | solution.py:56
  103.6 12.1 %collective-permute-start.31 = (bf16[4,4,16,1024]{3,2,1,0:T(8,128)(2,1)S(1)}, bf16[4,4,16,1024]{3,2,1,0:T(8,128)(2,1)S(1)}, u32[]{:S(2)}, u32[]{:S(2)}) collective-permute-start(bf16[4,4,16,1024]{3,2,1,0:T(8,128)(2,1)S(1)} %down.14), channel_id=1, source_target_pairs={{0,4},{4,0},{1,5},{5,1},{2,6},{6,2},{3,7},{7,3},{8,12},{12,8},{9,1... | collective-permute-start | bytes 1572872 | tf_op jit(solution)/shard_map/ppermute | solution.py:56
  105.9 11.5 %collective-permute-start.26 = (bf16[4,4,16,1024]{3,2,1,0:T(8,128)(2,1)S(1)}, bf16[4,4,16,1024]{3,2,1,0:T(8,128)(2,1)S(1)}, u32[]{:S(2)}, u32[]{:S(2)}) collective-permute-start(bf16[4,4,16,1024]{3,2,1,0:T(8,128)(2,1)S(1)} %down.10), channel_id=1, source_target_pairs={{0,16},{4,68},{8,24},{12,76},{16,0},{20,84},{24,8},{28,92},{32,48}... | collective-permute-start | bytes 1572872 | tf_op jit(solution)/shard_map/ppermute | solution.py:52
  110.7 11.6 %collective-permute-start.30 = (bf16[4,4,16,1024]{3,2,1,0:T(8,128)(2,1)S(1)}, bf16[4,4,16,1024]{3,2,1,0:T(8,128)(2,1)S(1)}, u32[]{:S(2)}, u32[]{:S(2)}) collective-permute-start(bf16[4,4,16,1024]{3,2,1,0:T(8,128)(2,1)S(1)} %down.13), channel_id=1, source_target_pairs={{0,8},{4,36},{8,16},{12,44},{16,24},{20,52},{24,0},{28,60},{32,40}... | collective-permute-start | bytes 1572872 | tf_op jit(solution)/shard_map/ppermute | solution.py:52
  113.2 9.4 %collective-permute-start.28 = (bf16[4,4,16,1024]{3,2,1,0:T(8,128)(2,1)S(1)}, bf16[4,4,16,1024]{3,2,1,0:T(8,128)(2,1)S(1)}, u32[]{:S(2)}, u32[]{:S(2)}) collective-permute-start(bf16[4,4,16,1024]{3,2,1,0:T(8,128)(2,1)S(1)} %down.11), channel_id=1, source_target_pairs={{0,24},{4,100},{8,0},{12,108},{16,8},{20,116},{24,16},{28,124},{32... | collective-permute-start | bytes 1572872 | tf_op jit(solution)/shard_map/ppermute | solution.py:52
  123.1 6.4 %collective-permute-start.32 = (bf16[4,16,1024]{2,1,0:T(8,128)(2,1)S(1)}, bf16[4,16,1024]{2,1,0:T(8,128)(2,1)S(1)}, u32[]{:S(2)}, u32[]{:S(2)}) collective-permute-start(bf16[4,16,1024]{2,1,0:T(8,128)(2,1)S(1)} %get-tuple-element.65), channel_id=1, source_target_pairs={{0,96},{4,28},{8,104},{12,4},{16,112},{20,12},{24,120},{28,20},{32... | collective-permute-start | bytes 393224 | tf_op jit(solution)/shard_map/ppermute | solution.py:52
  126.9 7.6 %collective-permute-start.34 = (bf16[4,16,1024]{2,1,0:T(8,128)(2,1)S(1)}, bf16[4,16,1024]{2,1,0:T(8,128)(2,1)S(1)}, u32[]{:S(2)}, u32[]{:S(2)}) collective-permute-start(bf16[4,16,1024]{2,1,0:T(8,128)(2,1)S(1)} %get-tuple-element.66), channel_id=1, source_target_pairs={{0,32},{4,12},{8,40},{12,20},{16,48},{20,28},{24,56},{28,4},{32,64... | collective-permute-start | bytes 393224 | tf_op jit(solution)/shard_map/ppermute | solution.py:52
  126.9 7.6 %collective-permute-start.33 = (bf16[4,16,1024]{2,1,0:T(8,128)(2,1)S(1)}, bf16[4,16,1024]{2,1,0:T(8,128)(2,1)S(1)}, u32[]{:S(2)}, u32[]{:S(2)}) collective-permute-start(bf16[4,16,1024]{2,1,0:T(8,128)(2,1)S(1)} %get-tuple-element.67), channel_id=1, source_target_pairs={{0,64},{4,20},{8,72},{12,28},{16,80},{20,4},{24,88},{28,12},{32,96... | collective-permute-start | bytes 393224 | tf_op jit(solution)/shard_map/ppermute | solution.py:52

commit v4 on v3

--- a/solution.py
+++ b/solution.py
@@ -364,38 +364,47 @@
     )(place, source, *blocks, *map(in_hbm, sides))
 
 
-def down_kernel(base, start, place, slot, weight, *refs):
-    acts, homes, theirs, out = refs[:SIDE], refs[SIDE], refs[SIDE + 1 : -1], refs[-1]
+def down_kernel(base, picks, place, slot, weight, *refs):
+    acts, homes, refs = refs[:SIDE], refs[SIDE], refs[SIDE + 1 :]
+    theirs, outs = refs[: -len(picks)], refs[-len(picks) :]
     x = place[0]
     block = homes.shape[1]
     rows = SIDE * block
-    inputs = jnp.concatenate([a[start * block : start * block + rows] for a in acts], axis=0)
-    values = jnp.dot(inputs, weight[...], preferred_element_type=jnp.float32)
+    inputs = [a[p * rows : (p + 1) * rows] for p in picks for a in acts]
+    values = jnp.dot(
+        jnp.concatenate(inputs, axis=0), weight[...], preferred_element_type=jnp.float32
+    )
     line = lax.broadcasted_iota(jnp.int32, homes.shape[1:], 0)
     for s in range(SIDE):
         from_x = (x + SIDE - s) % SIDE
         home = homes[from_x].astype(jnp.float32)
         moves = (line == block - 1) & (from_x == SIDE - 1)
-        for d in range(SIDE):
-            value = values[s * rows + d * block : s * rows + (d + 1) * block]
-            adds = moves & (slot[0] == base + d)
-            if base + d == 0:
-                adds = adds | jnp.logical_not(moves)
-            value = value + jnp.where(adds, home, 0.0)
-            for other in theirs:
-                value = value + other[d, from_x].astype(jnp.float32)
-            out[d, from_x] = value.astype(jnp.bfloat16)
-
-
-def down(base, start, place, slot, weight, acts, homes, theirs=()):
+        for n, p in enumerate(picks):
+            for d in range(SIDE):
+                at = (n * SIDE + s) * rows + d * block
+                value = values[at : at + block]
+                here = base + p * SIDE + d
+                adds = moves & (slot[0] == here)
+                if here == 0:
+                    adds = adds | jnp.logical_not(moves)
+                value = value + jnp.where(adds, home, 0.0)
+                for other in theirs:
+                    value = value + other[d, from_x].astype(jnp.float32)
+                outs[n][d, from_x] = value.astype(jnp.bfloat16)
+
+
+def down(base, picks, place, slot, weight, acts, homes, theirs=()):
     block, width = homes.shape[1:]
+    out = jax.ShapeDtypeStruct((SIDE, SIDE, block, width), jnp.bfloat16)
     return pl.pallas_call(
-        lambda *refs: down_kernel(base, start, *refs),
-        out_shape=jax.ShapeDtypeStruct((SIDE, SIDE, block, width), jnp.bfloat16),
+        lambda *refs: down_kernel(base, picks, *refs),
+        out_shape=[out] * len(picks),
         in_specs=[SM, SM, VM] + [VM] * (SIDE + 1 + len(theirs)),
-        out_specs=VM,
-        compiler_params=params(12),
-        cost_estimate=cost(2 * SIDE * SIDE * block * weight.size, 2 * weight.size),
+        out_specs=[VM] * len(picks),
+        compiler_params=params(16),
+        cost_estimate=cost(
+            2 * len(picks) * SIDE * SIDE * block * weight.size, 2 * len(picks) * weight.size
+        ),
         name="down",
     )(place, slot, weight, *acts, homes, *theirs)
 
@@ -477,17 +486,20 @@
 
     half = slots // 2
     shifts = (2, 1, 3, 0)
+    pairs = ((2, 1), (3, 0))
     sent = [
-        down(half + s * SIDE, s * SIDE, place, slot, down_weight, theirs, homes) for s in shifts
+        list(down(half, picks, place, slot, down_weight, theirs, homes)) for picks in pairs
     ]
-    sent[1], mine[2] = lax.optimization_barrier((sent[1], mine[2]))
-    sent = [other_core(v) for v in sent]
+    sent[1][0], mine[2] = lax.optimization_barrier((sent[1][0], mine[2]))
+    received = [other_core(value) for values in sent for value in values]
     total = []
-    for s, received in zip(shifts, sent):
-        value = down(s * SIDE, s * SIDE, place, slot, down_weight, mine, homes, (received,))
-        total.append(along_chips(value, -s, False) if s else value)
+    for s, value in zip((2, 1, 3, 0), received):
+        if total:
+            value, _ = lax.optimization_barrier((value, made))
+        (made,) = down(0, (s,), place, slot, down_weight, mine, homes, (value,))
+        total.append(along_chips(made, -s, False) if s else made)
     total = add(total)
-    out = add([total[0]] + [along_chips(total[s], -s, True) for s in (1, 2, 3)])
+    out = add([along_chips(total[s], -s, True) for s in (2, 1, 3)] + [total[0]])
     return out.reshape(rows_here, width)
 
 

time: 136 us -> 134 us (0.985)
  Pallas kernels: 37 us -> 34.3 us
  waiting for transfers between devices: 45.8 us -> 47.8 us
    pallas_call x8 -> x6, Pallas kernels: 13 us -> 10.3 us  [down(): pl.pallas_call(lambda *refs: down_kernel(base, picks, *refs), out_shape=[...]
    ppermute x15, waiting for transfers between devices: 16.5 us -> 18.8 us  [along_x(): return lax.ppermute(value, 'x', x_ring(shift))]
  transfers between devices with their start and end apart: 36 -> 36, of which waited for: 18 -> 19; matrix products, arithmetic and copies ran while one was open for 1% -> 1% of each run, Pallas kernels for 20% -> 18%
where the time goes in v4:
time: 134 us; the launch traced here: 133 us
  starting transfers between devices  48.5 us (36%)
  waiting for transfers between devices  47.8 us (36%)
  Pallas kernels  34.3 us (26%)
  other arithmetic  2.2 us (2%)
    ppermute x12, waiting for transfers between devices, along_chips(): return lax.ppermute(value, REP, chip_ring(shift, first))  23.6 us
    ppermute x12, starting transfers between devices, along_chips(): return lax.ppermute(value, REP, chip_ring(shift, first))  23.3 us
    ppermute x15, waiting for transfers between devices, along_x(): return lax.ppermute(value, 'x', x_ring(shift))  18.8 us
    ppermute x15, starting transfers between devices, along_x(): return lax.ppermute(value, 'x', x_ring(shift))  18.6 us
    pallas_call x1, Pallas kernels, attend_project(): pl.pallas_call(attend_kernel, out_shape=[out] * SIDE, in_specs=[SM] + [HB...  12.9 us
    pallas_call x6, Pallas kernels, down(): pl.pallas_call(lambda *refs: down_kernel(base, picks, *refs), out_shape=[...  10.3 us
    pallas_call x1, Pallas kernels, gate_up_act(): pl.pallas_call(gate_up_kernel, out_shape=[jax.ShapeDtypeStruct((rows // 2...  8.47 us
    all_to_all x1, waiting for transfers between devices, local(): homes = lax.all_to_all(kept, 'x', 0, 0, tiled=True)  5.36 us
  transfers between devices with their start and end apart: 36, of which 19 were waited for; matrix products, arithmetic and copies ran while one was open for 1% of the time, Pallas kernels for 18%

profile of v4, /device:TPU:0, one launch (start us, length us, event | category | flops | bytes accessed | tf_op | source)
XLA Modules:
  0.0 133.4 jit_solution(15013290536715662975)
XLA Ops:
  0.0 1.3 split.1
  1.4 1.6 %collective-permute-start.3 = (bf16[344,1024]{1,0:T(8,128)(2,1)S(1)}, bf16[344,1024]{1,0:T(8,128)(2,1)}, u32[]{:S(2)}, u32[]{:S(2)}) collective-permute-start(bf16[344,1024]{1,0:T(8,128)(2,1)S(1)} %get-tuple-element.56.refs_8_), channel_id=1, source_target_pairs={{0,1},{1,2},{2,3},{3,0},{4,5},{5,6},{6,7},{7,4},{8,9},{9,10},{10,1... | collective-permute-start | bytes 2113544 | tf_op jit(solution)/shard_map/ppermute | solution.py:48
  3.0 1.7 %collective-permute-start.4 = (bf16[344,1024]{1,0:T(8,128)(2,1)S(1)}, bf16[344,1024]{1,0:T(8,128)(2,1)}, u32[]{:S(2)}, u32[]{:S(2)}) collective-permute-start(bf16[344,1024]{1,0:T(8,128)(2,1)S(1)} %get-tuple-element.57.refs_9_), channel_id=1, source_target_pairs={{0,3},{1,0},{2,1},{3,2},{4,7},{5,4},{6,5},{7,6},{8,11},{9,8},{10,9... | collective-permute-start | bytes 2113544 | tf_op jit(solution)/shard_map/ppermute | solution.py:48
  4.7 12.9 %attend_project.1 = (bf16[16,4224]{1,0:T(8,128)(2,1)S(1)}, bf16[16,4224]{1,0:T(8,128)(2,1)S(1)}, bf16[16,4224]{1,0:T(8,128)(2,1)S(1)}, bf16[16,4224]{1,0:T(8,128)(2,1)S(1)}) custom-call(s32[2]{0:T(128)S(1)} %pad_add_fusion.place.refs_0_, s32[2,64]{1,0:T(2,128)} %bitcast.22, s32[2048]{0:T(1024)} %spans.1, bf16[64,1024]{1,0:T(8,128)(2,1)} %query.1, ...), custom_call_target="tpu_custom_call" | custom-call | flops 536870912 | bytes 16777216 | tf_op jit(solution)/shard_map/attend_project/pallas_call | solution.py:188
  18.1 2.7 %collective-permute-start.1 = (bf16[16,4224]{1,0:T(8,128)(2,1)S(1)}, bf16[16,4224]{1,0:T(8,128)(2,1)S(1)}, u32[]{:S(2)}, u32[]{:S(2)}) collective-permute-start(bf16[16,4224]{1,0:T(8,128)(2,1)S(1)} %get-tuple-element.44), channel_id=1, source_target_pairs={{0,2},{1,3},{2,0},{3,1},{4,6},{5,7},{6,4},{7,5},{8,10},{9,11},{10,... | collective-permute-start | bytes 405512 | tf_op jit(solution)/shard_map/ppermute | solution.py:48
  20.8 1.4 %collective-permute-start.2 = (bf16[16,4224]{1,0:T(8,128)(2,1)S(1)}, bf16[16,4224]{1,0:T(8,128)(2,1)S(1)}, u32[]{:S(2)}, u32[]{:S(2)}) collective-permute-start(bf16[16,4224]{1,0:T(8,128)(2,1)S(1)} %get-tuple-element.45), channel_id=1, source_target_pairs={{0,3},{1,0},{2,1},{3,2},{4,7},{5,4},{6,5},{7,6},{8,11},{9,8},{10,9... | collective-permute-start | bytes 405512 | tf_op jit(solution)/shard_map/ppermute | solution.py:48
  22.3 2.7 %collective-permute-done.refs_1_ = bf16[16,4224]{1,0:T(8,128)(2,1)S(1)} collective-permute-done((bf16[16,4224]{1,0:T(8,128)(2,1)S(1)}, bf16[16,4224]{1,0:T(8,128)(2,1)S(1)}, u32[]{:S(2)}, u32[]{:S(2)}) %collective-permute-start) | collective-permute-done | bytes 135200 | tf_op jit(solution)/shard_map/ppermute | solution.py:48
  24.9 2.1 %collective-permute-done.1.refs_2_ = bf16[16,4224]{1,0:T(8,128)(2,1)S(1)} collective-permute-done((bf16[16,4224]{1,0:T(8,128)(2,1)S(1)}, bf16[16,4224]{1,0:T(8,128)(2,1)S(1)}, u32[]{:S(2)}, u32[]{:S(2)}) %collective-permute-start.1) | collective-permute-done | bytes 135200 | tf_op jit(solution)/shard_map/ppermute | solution.py:48
  27.1 1.3 normalise.1
  28.4 1.3 collective-permute-start.8
  29.8 1.9 %collective-permute-start.9 = (bf16[344,1024]{1,0:T(8,128)(2,1)}, bf16[344,1024]{1,0:T(8,128)(2,1)}, u32[]{:S(2)}, u32[]{:S(2)}) collective-permute-start(bf16[344,1024]{1,0:T(8,128)(2,1)} %collective-permute-done.4.refs_15_), channel_id=1, source_target_pairs={{0,3},{1,0},{2,1},{3,2},{4,7},{5,4},{6,5},{7,6},{8,11},{9,8},{10,9... | collective-permute-start | bytes 2113544 | tf_op jit(solution)/shard_map/ppermute | solution.py:48
  31.7 4.2 %collective-permute-start.7 = (bf16[16,4096]{1,0:T(8,128)(2,1)S(1)}, bf16[16,4096]{1,0:T(8,128)(2,1)S(1)}, u32[]{:S(2)}, u32[]{:S(2)}) collective-permute-start(bf16[16,4096]{1,0:T(8,128)(2,1)S(1)} %get-tuple-element.49.refs_0_), channel_id=1, source_target_pairs={{0,96},{4,28},{8,104},{12,4},{16,112},{20,12},{24,120},{28,20},{32... | collective-permute-start | bytes 393224 | tf_op jit(solution)/shard_map/ppermute | solution.py:52
  35.8 1.3 collective-permute-start.5
  37.1 3.3 %all-to-all-start = ((bf16[4,16,1024]{2,1,0:T(8,128)(2,1)}), bf16[4,16,1024]{2,1,0:T(8,128)(2,1)S(1)}, u32[]{:S(2)}, u32[]{:S(2)}) async-start(bf16[4,16,1024]{2,1,0:T(8,128)(2,1)} %get-tuple-element.52), calls=%async_computation | async-start | bytes 262144 | tf_op jit(solution)/shard_map/all_to_all | solution.py:463
  40.4 2.0 %collective-permute-done.6.refs_2_ = bf16[16,4096]{1,0:T(8,128)(2,1)S(1)} collective-permute-done((bf16[16,4096]{1,0:T(8,128)(2,1)S(1)}, bf16[16,4096]{1,0:T(8,128)(2,1)S(1)}, u32[]{:S(2)}, u32[]{:S(2)}) %collective-permute-start.6) | collective-permute-done | bytes 131104 | tf_op jit(solution)/shard_map/ppermute | solution.py:52
  42.4 1.0 collective-permute-done.5.refs_1_
  43.4 5.4 %all-to-all-done.refs_7_ = bf16[4,16,1024]{2,1,0:T(8,128)(2,1)S(1)} async-done(((bf16[4,16,1024]{2,1,0:T(8,128)(2,1)}), bf16[4,16,1024]{2,1,0:T(8,128)(2,1)S(1)}, u32[]{:S(2)}, u32[]{:S(2)}) %all-to-all-start) | async-done | bytes 131104 | tf_op jit(solution)/shard_map/all_to_all | solution.py:463
  48.8 2.0 %collective-permute-start.18 = (bf16[344,1024]{1,0:T(8,128)(2,1)S(1)}, bf16[344,1024]{1,0:T(8,128)(2,1)}, u32[]{:S(2)}, u32[]{:S(2)}) collective-permute-start(bf16[344,1024]{1,0:T(8,128)(2,1)S(1)} %get-tuple-element.56.refs_8_), channel_id=1, source_target_pairs={{0,3},{1,0},{2,1},{3,2},{4,7},{5,4},{6,5},{7,6},{8,11},{9,8},{10,9... | collective-permute-start | bytes 2113544 | tf_op jit(solution)/shard_map/ppermute | solution.py:48
  50.8 1.7 %collective-permute-start.10 = (bf16[64,4096]{1,0:T(8,128)(2,1)S(1)}, bf16[64,4096]{1,0:T(8,128)(2,1)}, u32[]{:S(2)}, u32[]{:S(2)}) collective-permute-start(bf16[64,4096]{1,0:T(8,128)(2,1)S(1)} %join.1.refs_0_), channel_id=1, source_target_pairs={{0,8},{4,36},{8,16},{12,44},{16,24},{20,52},{24,0},{28,60},{32,40}... | collective-permute-start | bytes 1572872 | tf_op jit(solution)/shard_map/ppermute | solution.py:52
  52.5 1.5 %collective-permute-start.12 = (bf16[64,4096]{1,0:T(8,128)(2,1)S(1)}, bf16[64,4096]{1,0:T(8,128)(2,1)}, u32[]{:S(2)}, u32[]{:S(2)}) collective-permute-start(bf16[64,4096]{1,0:T(8,128)(2,1)S(1)} %join.1.refs_0_), channel_id=1, source_target_pairs={{0,24},{4,100},{8,0},{12,108},{16,8},{20,116},{24,16},{28,124},{32... | collective-permute-start | bytes 1572872 | tf_op jit(solution)/shard_map/ppermute | solution.py:52
  54.0 2.1 %collective-permute-start.11 = (bf16[64,4096]{1,0:T(8,128)(2,1)S(1)}, bf16[64,4096]{1,0:T(8,128)(2,1)}, u32[]{:S(2)}, u32[]{:S(2)}) collective-permute-start(bf16[64,4096]{1,0:T(8,128)(2,1)S(1)} %join.1.refs_0_), channel_id=1, source_target_pairs={{0,16},{4,68},{8,24},{12,76},{16,0},{20,84},{24,8},{28,92},{32,48}... | collective-permute-start | bytes 1572872 | tf_op jit(solution)/shard_map/ppermute | solution.py:52
  56.7 4.6 %collective-permute-done.10.refs_1_ = bf16[64,4096]{1,0:T(8,128)(2,1)} collective-permute-done((bf16[64,4096]{1,0:T(8,128)(2,1)S(1)}, bf16[64,4096]{1,0:T(8,128)(2,1)}, u32[]{:S(2)}, u32[]{:S(2)}) %collective-permute-start.10) | collective-permute-done | bytes 524320 | tf_op jit(solution)/shard_map/ppermute | solution.py:52
  61.8 1.6 %collective-permute-start.14 = (bf16[64,4096]{1,0:T(8,128)(2,1)}, bf16[64,4096]{1,0:T(8,128)(2,1)}, u32[]{:S(2)}, u32[]{:S(2)}) collective-permute-start(bf16[64,4096]{1,0:T(8,128)(2,1)} %collective-permute-done.10.refs_1_), channel_id=1, source_target_pairs={{0,4},{4,0},{1,5},{5,1},{2,6},{6,2},{3,7},{7,3},{8,12},{12,8},{9,1... | collective-permute-start | bytes 1572872 | tf_op jit(solution)/shard_map/ppermute | solution.py:56
  63.4 4.9 %collective-permute-done.11.refs_2_ = bf16[64,4096]{1,0:T(8,128)(2,1)} collective-permute-done((bf16[64,4096]{1,0:T(8,128)(2,1)S(1)}, bf16[64,4096]{1,0:T(8,128)(2,1)}, u32[]{:S(2)}, u32[]{:S(2)}) %collective-permute-start.11) | collective-permute-done | bytes 524320 | tf_op jit(solution)/shard_map/ppermute | solution.py:52
  69.8 2.2 %collective-permute-done.17.refs_11_ = bf16[344,1024]{1,0:T(8,128)(2,1)} collective-permute-done((bf16[344,1024]{1,0:T(8,128)(2,1)S(1)}, bf16[344,1024]{1,0:T(8,128)(2,1)}, u32[]{:S(2)}, u32[]{:S(2)}) %collective-permute-start.17) | collective-permute-done | bytes 704544 | tf_op jit(solution)/shard_map/ppermute | solution.py:48
  72.0 8.5 %gate_up_act.1 = (bf16[256,344]{1,0:T(8,128)(2,1)S(1)}, bf16[256,344]{1,0:T(8,128)(2,1)S(1)}) custom-call(s32[2]{0:T(128)S(1)} %pad_add_fusion.place.refs_0_, s32[32]{0:T(128)S(1)} %get-tuple-element.82.source, bf16[64,4096]{1,0:T(8,128)(2,1)S(1)} %join.1.refs_0_, bf16[64,4096]{1,0:T(8,128)(2,1)} %collective-permute-done.10.refs_1_, ...), custom_call_target="tpu_custom_call" | custom-call | flops 2885681152 | bytes 14090240 | tf_op jit(solution)/shard_map/gate_up_act/pallas_call | solution.py:349
  80.6 3.2 %collective-permute-start.21 = (bf16[256,344]{1,0:T(8,128)(2,1)S(1)}, bf16[256,344]{1,0:T(8,128)(2,1)S(1)}, u32[]{:S(2)}, u32[]{:S(2)}) collective-permute-start(bf16[256,344]{1,0:T(8,128)(2,1)S(1)} %get-tuple-element.64.refs_3_), channel_id=1, source_target_pairs={{0,3},{1,0},{2,1},{3,2},{4,7},{5,4},{6,5},{7,6},{8,11},{9,8},{10,9... | collective-permute-start | bytes 528392 | tf_op jit(solution)/shard_map/ppermute | solution.py:48
  83.8 2.0 %collective-permute-start.22 = (bf16[256,344]{1,0:T(8,128)(2,1)S(1)}, bf16[256,344]{1,0:T(8,128)(2,1)S(1)}, u32[]{:S(2)}, u32[]{:S(2)}) collective-permute-start(bf16[256,344]{1,0:T(8,128)(2,1)S(1)} %get-tuple-element.63.refs_3_), channel_id=1, source_target_pairs={{0,1},{1,2},{2,3},{3,0},{4,5},{5,6},{6,7},{7,4},{8,9},{9,10},{10,1... | collective-permute-start | bytes 528392 | tf_op jit(solution)/shard_map/ppermute | solution.py:48
  85.8 3.6 %collective-permute-done.19.refs_4_ = bf16[256,344]{1,0:T(8,128)(2,1)S(1)} collective-permute-done((bf16[256,344]{1,0:T(8,128)(2,1)S(1)}, bf16[256,344]{1,0:T(8,128)(2,1)S(1)}, u32[]{:S(2)}, u32[]{:S(2)}) %collective-permute-start.19) | collective-permute-done | bytes 176160 | tf_op jit(solution)/shard_map/ppermute | solution.py:48
  89.4 2.0 %collective-permute-done.23.refs_6_ = bf16[256,344]{1,0:T(8,128)(2,1)S(1)} collective-permute-done((bf16[256,344]{1,0:T(8,128)(2,1)S(1)}, bf16[256,344]{1,0:T(8,128)(2,1)S(1)}, u32[]{:S(2)}, u32[]{:S(2)}) %collective-permute-start.23) | collective-permute-done | bytes 176160 | tf_op jit(solution)/shard_map/ppermute | solution.py:48
  91.4 2.2 %collective-permute-done.22.refs_4_ = bf16[256,344]{1,0:T(8,128)(2,1)S(1)} collective-permute-done((bf16[256,344]{1,0:T(8,128)(2,1)S(1)}, bf16[256,344]{1,0:T(8,128)(2,1)S(1)}, u32[]{:S(2)}, u32[]{:S(2)}) %collective-permute-start.22) | collective-permute-done | bytes 176160 | tf_op jit(solution)/shard_map/ppermute | solution.py:48
  93.6 2.7 %collective-permute-done.20.refs_5_ = bf16[256,344]{1,0:T(8,128)(2,1)S(1)} collective-permute-done((bf16[256,344]{1,0:T(8,128)(2,1)S(1)}, bf16[256,344]{1,0:T(8,128)(2,1)S(1)}, u32[]{:S(2)}, u32[]{:S(2)}) %collective-permute-start.20) | collective-permute-done | bytes 176160 | tf_op jit(solution)/shard_map/ppermute | solution.py:48
  96.3 1.9 %down.7 = (bf16[4,4,16,1024]{3,2,1,0:T(8,128)(2,1)S(1)}, bf16[4,4,16,1024]{3,2,1,0:T(8,128)(2,1)S(1)}) custom-call(s32[2]{0:T(128)S(1)} %pad_add_fusion.place.refs_0_, s32[1]{0:T(128)} %bitcast.2.refs_1_, bf16[344,1024]{1,0:T(8,128)(2,1)S(1)} %copy-done, bf16[256,344]{1,0:T(8,128)(2,1)S(1)} %get-tuple-element.64.refs_3_, ...), custom_call_target="tpu_custom_call" | custom-call | flops 360710144 | bytes 1409024 | tf_op jit(solution)/shard_map/down/pallas_call | solution.py:399
  98.8 1.9 %down.6 = (bf16[4,4,16,1024]{3,2,1,0:T(8,128)(2,1)S(1)}, bf16[4,4,16,1024]{3,2,1,0:T(8,128)(2,1)S(1)}) custom-call(s32[2]{0:T(128)S(1)} %pad_add_fusion.place.refs_0_, s32[1]{0:T(128)} %bitcast.2.refs_1_, bf16[344,1024]{1,0:T(8,128)(2,1)S(1)} %copy-done, bf16[256,344]{1,0:T(8,128)(2,1)S(1)} %get-tuple-element.64.refs_3_, ...), custom_call_target="tpu_custom_call" | custom-call | flops 360710144 | bytes 1409024 | tf_op jit(solution)/shard_map/down/pallas_call | solution.py:399
  100.7 1.3 collective-permute-done.24.refs_5_
  102.5 1.6 %down.8 = bf16[4,4,16,1024]{3,2,1,0:T(8,128)(2,1)S(1)} custom-call(s32[2]{0:T(128)S(1)} %pad_add_fusion.place.refs_0_, s32[1]{0:T(128)} %bitcast.2.refs_1_, bf16[344,1024]{1,0:T(8,128)(2,1)S(1)} %copy-done, bf16[256,344]{1,0:T(8,128)(2,1)S(1)} %get-tuple-element.63.refs_3_, bf16[256,344]{1,0:T(8,128)(2,1)S(1)} %collective-permute-done.22.refs_4_, ...), custom_call_target="tpu_custom_call" | custom-call | flops 180355072 | bytes 704512 | tf_op jit(solution)/shard_map/down/pallas_call | solution.py:399
  104.2 3.2 %collective-permute-start.26 = (bf16[4,4,16,1024]{3,2,1,0:T(8,128)(2,1)S(1)}, bf16[4,4,16,1024]{3,2,1,0:T(8,128)(2,1)S(1)}, u32[]{:S(2)}, u32[]{:S(2)}) collective-permute-start(bf16[4,4,16,1024]{3,2,1,0:T(8,128)(2,1)S(1)} %down.8), channel_id=1, source_target_pairs={{0,16},{4,68},{8,24},{12,76},{16,0},{20,84},{24,8},{28,92},{32,48}... | collective-permute-start | bytes 1572872 | tf_op jit(solution)/shard_map/ppermute | solution.py:52
  107.3 1.6 %down.9 = bf16[4,4,16,1024]{3,2,1,0:T(8,128)(2,1)S(1)} custom-call(s32[2]{0:T(128)S(1)} %pad_add_fusion.place.refs_0_, s32[1]{0:T(128)} %bitcast.2.refs_1_, bf16[344,1024]{1,0:T(8,128)(2,1)S(1)} %copy-done, bf16[256,344]{1,0:T(8,128)(2,1)S(1)} %get-tuple-element.63.refs_3_, bf16[256,344]{1,0:T(8,128)(2,1)S(1)} %collective-permute-done.22.refs_4_, ...), custom_call_target="tpu_custom_call" | custom-call | flops 180355072 | bytes 704512 | tf_op jit(solution)/shard_map/down/pallas_call | solution.py:399
  108.9 1.1 collective-permute-start.28
  110.0 1.6 %down.10 = bf16[4,4,16,1024]{3,2,1,0:T(8,128)(2,1)S(1)} custom-call(s32[2]{0:T(128)S(1)} %pad_add_fusion.place.refs_0_, s32[1]{0:T(128)} %bitcast.2.refs_1_, bf16[344,1024]{1,0:T(8,128)(2,1)S(1)} %copy-done, bf16[256,344]{1,0:T(8,128)(2,1)S(1)} %get-tuple-element.63.refs_3_, bf16[256,344]{1,0:T(8,128)(2,1)S(1)} %collective-permute-done.22.refs_4_, ...), custom_call_target="tpu_custom_call" | custom-call | flops 180355072 | bytes 704512 | tf_op jit(solution)/shard_map/down/pallas_call | solution.py:399
  111.7 1.1 collective-permute-start.30
  112.8 1.6 %down.11 = bf16[4,4,16,1024]{3,2,1,0:T(8,128)(2,1)S(1)} custom-call(s32[2]{0:T(128)S(1)} %pad_add_fusion.place.refs_0_, s32[1]{0:T(128)} %bitcast.2.refs_1_, bf16[344,1024]{1,0:T(8,128)(2,1)S(1)} %copy-done, bf16[256,344]{1,0:T(8,128)(2,1)S(1)} %get-tuple-element.63.refs_3_, bf16[256,344]{1,0:T(8,128)(2,1)S(1)} %collective-permute-done.22.refs_4_, ...), custom_call_target="tpu_custom_call" | custom-call | flops 180355072 | bytes 704512 | tf_op jit(solution)/shard_map/down/pallas_call | solution.py:399
  114.9 6.1 %collective-permute-done.28 = bf16[4,4,16,1024]{3,2,1,0:T(8,128)(2,1)S(1)} collective-permute-done((bf16[4,4,16,1024]{3,2,1,0:T(8,128)(2,1)S(1)}, bf16[4,4,16,1024]{3,2,1,0:T(8,128)(2,1)S(1)}, u32[]{:S(2)}, u32[]{:S(2)}) %collective-permute-start.28) | collective-permute-done | bytes 524320 | tf_op jit(solution)/shard_map/ppermute | solution.py:52
  121.0 1.1 collective-permute-done.30
  122.5 4.0 %collective-permute-start.32 = (bf16[4,16,1024]{2,1,0:T(8,128)(2,1)S(1)}, bf16[4,16,1024]{2,1,0:T(8,128)(2,1)S(1)}, u32[]{:S(2)}, u32[]{:S(2)}) collective-permute-start(bf16[4,16,1024]{2,1,0:T(8,128)(2,1)S(1)} %get-tuple-element.79), channel_id=1, source_target_pairs={{0,64},{4,20},{8,72},{12,28},{16,80},{20,4},{24,88},{28,12},{32,96... | collective-permute-start | bytes 393224 | tf_op jit(solution)/shard_map/ppermute | solution.py:52
  126.5 1.0 collective-permute-start.34
  127.5 2.2 %collective-permute-start.33 = (bf16[4,16,1024]{2,1,0:T(8,128)(2,1)S(1)}, bf16[4,16,1024]{2,1,0:T(8,128)(2,1)S(1)}, u32[]{:S(2)}, u32[]{:S(2)}) collective-permute-start(bf16[4,16,1024]{2,1,0:T(8,128)(2,1)S(1)} %get-tuple-element.81), channel_id=1, source_target_pairs={{0,96},{4,28},{8,104},{12,4},{16,112},{20,12},{24,120},{28,20},{32... | collective-permute-start | bytes 393224 | tf_op jit(solution)/shard_map/ppermute | solution.py:52
  129.7 2.9 %collective-permute-done.34 = bf16[4,16,1024]{2,1,0:T(8,128)(2,1)S(1)} collective-permute-done((bf16[4,16,1024]{2,1,0:T(8,128)(2,1)S(1)}, bf16[4,16,1024]{2,1,0:T(8,128)(2,1)S(1)}, u32[]{:S(2)}, u32[]{:S(2)}) %collective-permute-start.34) | collective-permute-done | bytes 131104 | tf_op jit(solution)/shard_map/ppermute | solution.py:52
  (58 shorter events, 6.1 us)
Async XLA Ops:
  1.3 47.5 %copy-start.1 = (bf16[344,1024]{1,0:T(8,128)(2,1)}, bf16[344,1024]{1,0:T(8,128)(2,1)S(1)}, u32[]{:S(2)}) copy-start(bf16[344,1024]{1,0:T(8,128)(2,1)S(1)} %get-tuple-element.56.refs_8_) | copy-start | bytes 2113540
  1.4 54.8 %copy-start.2 = (bf16[344,1024]{1,0:T(8,128)(2,1)}, bf16[344,1024]{1,0:T(8,128)(2,1)S(1)}, u32[]{:S(2)}) copy-start(bf16[344,1024]{1,0:T(8,128)(2,1)S(1)} %get-tuple-element.57.refs_9_) | copy-start | bytes 2113540
  1.4 27.1 %collective-permute-start.3 = (bf16[344,1024]{1,0:T(8,128)(2,1)S(1)}, bf16[344,1024]{1,0:T(8,128)(2,1)}, u32[]{:S(2)}, u32[]{:S(2)}) collective-permute-start(bf16[344,1024]{1,0:T(8,128)(2,1)S(1)} %get-tuple-element.56.refs_8_), channel_id=1, source_target_pairs={{0,1},{1,2},{2,3},{3,0},{4,5},{5,6},{6,7},{7,4},{8,9},{9,10},{10,1... | collective-permute-start | bytes 2113544 | tf_op jit(solution)/shard_map/ppermute | solution.py:48
  3.0 25.4 %collective-permute-start.4 = (bf16[344,1024]{1,0:T(8,128)(2,1)S(1)}, bf16[344,1024]{1,0:T(8,128)(2,1)}, u32[]{:S(2)}, u32[]{:S(2)}) collective-permute-start(bf16[344,1024]{1,0:T(8,128)(2,1)S(1)} %get-tuple-element.57.refs_9_), channel_id=1, source_target_pairs={{0,3},{1,0},{2,1},{3,2},{4,7},{5,4},{6,5},{7,6},{8,11},{9,8},{10,9... | collective-permute-start | bytes 2113544 | tf_op jit(solution)/shard_map/ppermute | solution.py:48
  4.7 64.1 %copy-start.3 = (s32[32]{0:T(128)S(1)}, s32[32]{0:T(128)}, u32[]{:S(2)}) copy-start(s32[32]{0:T(128)} %param.17) | copy-start | bytes 388
  17.6 78.7 %copy-start = (bf16[344,1024]{1,0:T(8,128)(2,1)S(1)}, bf16[344,1024]{1,0:T(8,128)(2,1)}, u32[]{:S(2)}) copy-start(bf16[344,1024]{1,0:T(8,128)(2,1)} %refs_2_.11) | copy-start | bytes 2113540
  17.7 7.3 %collective-permute-start = (bf16[16,4224]{1,0:T(8,128)(2,1)S(1)}, bf16[16,4224]{1,0:T(8,128)(2,1)S(1)}, u32[]{:S(2)}, u32[]{:S(2)}) collective-permute-start(bf16[16,4224]{1,0:T(8,128)(2,1)S(1)} %get-tuple-element.43), channel_id=1, source_target_pairs={{0,1},{1,2},{2,3},{3,0},{4,5},{5,6},{6,7},{7,4},{8,9},{9,10},{10,1... | collective-permute-start | bytes 405512 | tf_op jit(solution)/shard_map/ppermute | solution.py:48
  18.1 8.9 %collective-permute-start.1 = (bf16[16,4224]{1,0:T(8,128)(2,1)S(1)}, bf16[16,4224]{1,0:T(8,128)(2,1)S(1)}, u32[]{:S(2)}, u32[]{:S(2)}) collective-permute-start(bf16[16,4224]{1,0:T(8,128)(2,1)S(1)} %get-tuple-element.44), channel_id=1, source_target_pairs={{0,2},{1,3},{2,0},{3,1},{4,6},{5,7},{6,4},{7,5},{8,10},{9,11},{10,... | collective-permute-start | bytes 405512 | tf_op jit(solution)/shard_map/ppermute | solution.py:48
  20.8 6.3 %collective-permute-start.2 = (bf16[16,4224]{1,0:T(8,128)(2,1)S(1)}, bf16[16,4224]{1,0:T(8,128)(2,1)S(1)}, u32[]{:S(2)}, u32[]{:S(2)}) collective-permute-start(bf16[16,4224]{1,0:T(8,128)(2,1)S(1)} %get-tuple-element.45), channel_id=1, source_target_pairs={{0,3},{1,0},{2,1},{3,2},{4,7},{5,4},{6,5},{7,6},{8,11},{9,8},{10,9... | collective-permute-start | bytes 405512 | tf_op jit(solution)/shard_map/ppermute | solution.py:48
  28.4 20.4 %collective-permute-start.8 = (bf16[344,1024]{1,0:T(8,128)(2,1)}, bf16[344,1024]{1,0:T(8,128)(2,1)}, u32[]{:S(2)}, u32[]{:S(2)}) collective-permute-start(bf16[344,1024]{1,0:T(8,128)(2,1)} %collective-permute-done.3.refs_10_), channel_id=1, source_target_pairs={{0,1},{1,2},{2,3},{3,0},{4,5},{5,6},{6,7},{7,4},{8,9},{9,10},{10,1... | collective-permute-start | bytes 2113544 | tf_op jit(solution)/shard_map/ppermute | solution.py:48
  29.8 19.1 %collective-permute-start.9 = (bf16[344,1024]{1,0:T(8,128)(2,1)}, bf16[344,1024]{1,0:T(8,128)(2,1)}, u32[]{:S(2)}, u32[]{:S(2)}) collective-permute-start(bf16[344,1024]{1,0:T(8,128)(2,1)} %collective-permute-done.4.refs_15_), channel_id=1, source_target_pairs={{0,3},{1,0},{2,1},{3,2},{4,7},{5,4},{6,5},{7,6},{8,11},{9,8},{10,9... | collective-permute-start | bytes 2113544 | tf_op jit(solution)/shard_map/ppermute | solution.py:48
  31.7 8.7 %collective-permute-start.7 = (bf16[16,4096]{1,0:T(8,128)(2,1)S(1)}, bf16[16,4096]{1,0:T(8,128)(2,1)S(1)}, u32[]{:S(2)}, u32[]{:S(2)}) collective-permute-start(bf16[16,4096]{1,0:T(8,128)(2,1)S(1)} %get-tuple-element.49.refs_0_), channel_id=1, source_target_pairs={{0,96},{4,28},{8,104},{12,4},{16,112},{20,12},{24,120},{28,20},{32... | collective-permute-start | bytes 393224 | tf_op jit(solution)/shard_map/ppermute | solution.py:52
  35.8 6.6 %collective-permute-start.6 = (bf16[16,4096]{1,0:T(8,128)(2,1)S(1)}, bf16[16,4096]{1,0:T(8,128)(2,1)S(1)}, u32[]{:S(2)}, u32[]{:S(2)}) collective-permute-start(bf16[16,4096]{1,0:T(8,128)(2,1)S(1)} %get-tuple-element.49.refs_0_), channel_id=1, source_target_pairs={{0,64},{4,20},{8,72},{12,28},{16,80},{20,4},{24,88},{28,12},{32,96... | collective-permute-start | bytes 393224 | tf_op jit(solution)/shard_map/ppermute | solution.py:52
  35.8 7.6 %collective-permute-start.5 = (bf16[16,4096]{1,0:T(8,128)(2,1)S(1)}, bf16[16,4096]{1,0:T(8,128)(2,1)S(1)}, u32[]{:S(2)}, u32[]{:S(2)}) collective-permute-start(bf16[16,4096]{1,0:T(8,128)(2,1)S(1)} %get-tuple-element.49.refs_0_), channel_id=1, source_target_pairs={{0,32},{4,12},{8,40},{12,20},{16,48},{20,28},{24,56},{28,4},{32,64... | collective-permute-start | bytes 393224 | tf_op jit(solution)/shard_map/ppermute | solution.py:52
  37.1 11.7 %all-to-all-start = ((bf16[4,16,1024]{2,1,0:T(8,128)(2,1)}), bf16[4,16,1024]{2,1,0:T(8,128)(2,1)S(1)}, u32[]{:S(2)}, u32[]{:S(2)}) async-start(bf16[4,16,1024]{2,1,0:T(8,128)(2,1)} %get-tuple-element.52), calls=%async_computation | async-start | bytes 262144 | tf_op jit(solution)/shard_map/all_to_all | solution.py:463
  48.8 19.5 %collective-permute-start.18 = (bf16[344,1024]{1,0:T(8,128)(2,1)S(1)}, bf16[344,1024]{1,0:T(8,128)(2,1)}, u32[]{:S(2)}, u32[]{:S(2)}) collective-permute-start(bf16[344,1024]{1,0:T(8,128)(2,1)S(1)} %get-tuple-element.56.refs_8_), channel_id=1, source_target_pairs={{0,3},{1,0},{2,1},{3,2},{4,7},{5,4},{6,5},{7,6},{8,11},{9,8},{10,9... | collective-permute-start | bytes 2113544 | tf_op jit(solution)/shard_map/ppermute | solution.py:48
  50.8 10.5 %collective-permute-start.10 = (bf16[64,4096]{1,0:T(8,128)(2,1)S(1)}, bf16[64,4096]{1,0:T(8,128)(2,1)}, u32[]{:S(2)}, u32[]{:S(2)}) collective-permute-start(bf16[64,4096]{1,0:T(8,128)(2,1)S(1)} %join.1.refs_0_), channel_id=1, source_target_pairs={{0,8},{4,36},{8,16},{12,44},{16,24},{20,52},{24,0},{28,60},{32,40}... | collective-permute-start | bytes 1572872 | tf_op jit(solution)/shard_map/ppermute | solution.py:52
  52.5 9.3 %collective-permute-start.12 = (bf16[64,4096]{1,0:T(8,128)(2,1)S(1)}, bf16[64,4096]{1,0:T(8,128)(2,1)}, u32[]{:S(2)}, u32[]{:S(2)}) collective-permute-start(bf16[64,4096]{1,0:T(8,128)(2,1)S(1)} %join.1.refs_0_), channel_id=1, source_target_pairs={{0,24},{4,100},{8,0},{12,108},{16,8},{20,116},{24,16},{28,124},{32... | collective-permute-start | bytes 1572872 | tf_op jit(solution)/shard_map/ppermute | solution.py:52
  54.0 14.2 %collective-permute-start.11 = (bf16[64,4096]{1,0:T(8,128)(2,1)S(1)}, bf16[64,4096]{1,0:T(8,128)(2,1)}, u32[]{:S(2)}, u32[]{:S(2)}) collective-permute-start(bf16[64,4096]{1,0:T(8,128)(2,1)S(1)} %join.1.refs_0_), channel_id=1, source_target_pairs={{0,16},{4,68},{8,24},{12,76},{16,0},{20,84},{24,8},{28,92},{32,48}... | collective-permute-start | bytes 1572872 | tf_op jit(solution)/shard_map/ppermute | solution.py:52
  56.1 15.8 %collective-permute-start.17 = (bf16[344,1024]{1,0:T(8,128)(2,1)S(1)}, bf16[344,1024]{1,0:T(8,128)(2,1)}, u32[]{:S(2)}, u32[]{:S(2)}) collective-permute-start(bf16[344,1024]{1,0:T(8,128)(2,1)S(1)} %get-tuple-element.57.refs_9_), channel_id=1, source_target_pairs={{0,1},{1,2},{2,3},{3,0},{4,5},{5,6},{6,7},{7,4},{8,9},{9,10},{10,1... | collective-permute-start | bytes 2113544 | tf_op jit(solution)/shard_map/ppermute | solution.py:48
  61.3 10.7 %collective-permute-start.13 = (bf16[64,4096]{1,0:T(8,128)(2,1)S(1)}, bf16[64,4096]{1,0:T(8,128)(2,1)}, u32[]{:S(2)}, u32[]{:S(2)}) collective-permute-start(bf16[64,4096]{1,0:T(8,128)(2,1)S(1)} %join.1.refs_0_), channel_id=1, source_target_pairs={{0,4},{4,0},{1,5},{5,1},{2,6},{6,2},{3,7},{7,3},{8,12},{12,8},{9,1... | collective-permute-start | bytes 1572872 | tf_op jit(solution)/shard_map/ppermute | solution.py:56
  61.8 10.2 %collective-permute-start.14 = (bf16[64,4096]{1,0:T(8,128)(2,1)}, bf16[64,4096]{1,0:T(8,128)(2,1)}, u32[]{:S(2)}, u32[]{:S(2)}) collective-permute-start(bf16[64,4096]{1,0:T(8,128)(2,1)} %collective-permute-done.10.refs_1_), channel_id=1, source_target_pairs={{0,4},{4,0},{1,5},{5,1},{2,6},{6,2},{3,7},{7,3},{8,12},{12,8},{9,1... | collective-permute-start | bytes 1572872 | tf_op jit(solution)/shard_map/ppermute | solution.py:56
  68.3 3.7 %collective-permute-start.16 = (bf16[64,4096]{1,0:T(8,128)(2,1)}, bf16[64,4096]{1,0:T(8,128)(2,1)}, u32[]{:S(2)}, u32[]{:S(2)}) collective-permute-start(bf16[64,4096]{1,0:T(8,128)(2,1)} %collective-permute-done.12.refs_3_), channel_id=1, source_target_pairs={{0,4},{4,0},{1,5},{5,1},{2,6},{6,2},{3,7},{7,3},{8,12},{12,8},{9,1... | collective-permute-start | bytes 1572872 | tf_op jit(solution)/shard_map/ppermute | solution.py:56
  68.3 3.7 %collective-permute-start.15 = (bf16[64,4096]{1,0:T(8,128)(2,1)}, bf16[64,4096]{1,0:T(8,128)(2,1)S(1)}, u32[]{:S(2)}, u32[]{:S(2)}) collective-permute-start(bf16[64,4096]{1,0:T(8,128)(2,1)} %collective-permute-done.11.refs_2_), channel_id=1, source_target_pairs={{0,4},{4,0},{1,5},{5,1},{2,6},{6,2},{3,7},{7,3},{8,12},{12,8},{9,1... | collective-permute-start | bytes 1572872 | tf_op jit(solution)/shard_map/ppermute | solution.py:56
  80.5 8.9 %collective-permute-start.19 = (bf16[256,344]{1,0:T(8,128)(2,1)S(1)}, bf16[256,344]{1,0:T(8,128)(2,1)S(1)}, u32[]{:S(2)}, u32[]{:S(2)}) collective-permute-start(bf16[256,344]{1,0:T(8,128)(2,1)S(1)} %get-tuple-element.64.refs_3_), channel_id=1, source_target_pairs={{0,1},{1,2},{2,3},{3,0},{4,5},{5,6},{6,7},{7,4},{8,9},{9,10},{10,1... | collective-permute-start | bytes 528392 | tf_op jit(solution)/shard_map/ppermute | solution.py:48
  80.6 8.8 %collective-permute-start.21 = (bf16[256,344]{1,0:T(8,128)(2,1)S(1)}, bf16[256,344]{1,0:T(8,128)(2,1)S(1)}, u32[]{:S(2)}, u32[]{:S(2)}) collective-permute-start(bf16[256,344]{1,0:T(8,128)(2,1)S(1)} %get-tuple-element.64.refs_3_), channel_id=1, source_target_pairs={{0,3},{1,0},{2,1},{3,2},{4,7},{5,4},{6,5},{7,6},{8,11},{9,8},{10,9... | collective-permute-start | bytes 528392 | tf_op jit(solution)/shard_map/ppermute | solution.py:48
  83.8 7.6 %collective-permute-start.23 = (bf16[256,344]{1,0:T(8,128)(2,1)S(1)}, bf16[256,344]{1,0:T(8,128)(2,1)S(1)}, u32[]{:S(2)}, u32[]{:S(2)}) collective-permute-start(bf16[256,344]{1,0:T(8,128)(2,1)S(1)} %get-tuple-element.63.refs_3_), channel_id=1, source_target_pairs={{0,3},{1,0},{2,1},{3,2},{4,7},{5,4},{6,5},{7,6},{8,11},{9,8},{10,9... | collective-permute-start | bytes 528392 | tf_op jit(solution)/shard_map/ppermute | solution.py:48
  83.8 9.8 %collective-permute-start.22 = (bf16[256,344]{1,0:T(8,128)(2,1)S(1)}, bf16[256,344]{1,0:T(8,128)(2,1)S(1)}, u32[]{:S(2)}, u32[]{:S(2)}) collective-permute-start(bf16[256,344]{1,0:T(8,128)(2,1)S(1)} %get-tuple-element.63.refs_3_), channel_id=1, source_target_pairs={{0,1},{1,2},{2,3},{3,0},{4,5},{5,6},{6,7},{7,4},{8,9},{9,10},{10,1... | collective-permute-start | bytes 528392 | tf_op jit(solution)/shard_map/ppermute | solution.py:48
  89.4 6.9 %collective-permute-start.20 = (bf16[256,344]{1,0:T(8,128)(2,1)S(1)}, bf16[256,344]{1,0:T(8,128)(2,1)S(1)}, u32[]{:S(2)}, u32[]{:S(2)}) collective-permute-start(bf16[256,344]{1,0:T(8,128)(2,1)S(1)} %collective-permute-done.19.refs_4_), channel_id=1, source_target_pairs={{0,1},{1,2},{2,3},{3,0},{4,5},{5,6},{6,7},{7,4},{8,9},{9,10},{10,1... | collective-permute-start | bytes 528392 | tf_op jit(solution)/shard_map/ppermute | solution.py:48
  96.3 5.7 %collective-permute-start.24 = (bf16[256,344]{1,0:T(8,128)(2,1)S(1)}, bf16[256,344]{1,0:T(8,128)(2,1)S(1)}, u32[]{:S(2)}, u32[]{:S(2)}) collective-permute-start(bf16[256,344]{1,0:T(8,128)(2,1)S(1)} %collective-permute-done.23.refs_6_), channel_id=1, source_target_pairs={{0,3},{1,0},{2,1},{3,2},{4,7},{5,4},{6,5},{7,6},{8,11},{9,8},{10,9... | collective-permute-start | bytes 528392 | tf_op jit(solution)/shard_map/ppermute | solution.py:48
  98.2 4.3 %collective-permute-start.25 = (bf16[4,4,16,1024]{3,2,1,0:T(8,128)(2,1)S(1)}, bf16[4,4,16,1024]{3,2,1,0:T(8,128)(2,1)S(1)}, u32[]{:S(2)}, u32[]{:S(2)}) collective-permute-start(bf16[4,4,16,1024]{3,2,1,0:T(8,128)(2,1)S(1)} %get-tuple-element.72), channel_id=1, source_target_pairs={{0,4},{4,0},{1,5},{5,1},{2,6},{6,2},{3,7},{7,3},{8,12},{12,8},{9,1... | collective-permute-start | bytes 1572872 | tf_op jit(solution)/shard_map/ppermute | solution.py:56
  98.3 9.0 %collective-permute-start.27 = (bf16[4,4,16,1024]{3,2,1,0:T(8,128)(2,1)S(1)}, bf16[4,4,16,1024]{3,2,1,0:T(8,128)(2,1)S(1)}, u32[]{:S(2)}, u32[]{:S(2)}) collective-permute-start(bf16[4,4,16,1024]{3,2,1,0:T(8,128)(2,1)S(1)} %get-tuple-element.73), channel_id=1, source_target_pairs={{0,4},{4,0},{1,5},{5,1},{2,6},{6,2},{3,7},{7,3},{8,12},{12,8},{9,1... | collective-permute-start | bytes 1572872 | tf_op jit(solution)/shard_map/ppermute | solution.py:56
  102.0 8.0 %collective-permute-start.29 = (bf16[4,4,16,1024]{3,2,1,0:T(8,128)(2,1)S(1)}, bf16[4,4,16,1024]{3,2,1,0:T(8,128)(2,1)S(1)}, u32[]{:S(2)}, u32[]{:S(2)}) collective-permute-start(bf16[4,4,16,1024]{3,2,1,0:T(8,128)(2,1)S(1)} %get-tuple-element.75), channel_id=1, source_target_pairs={{0,4},{4,0},{1,5},{5,1},{2,6},{6,2},{3,7},{7,3},{8,12},{12,8},{9,1... | collective-permute-start | bytes 1572872 | tf_op jit(solution)/shard_map/ppermute | solution.py:56
  102.0 10.7 %collective-permute-start.31 = (bf16[4,4,16,1024]{3,2,1,0:T(8,128)(2,1)S(1)}, bf16[4,4,16,1024]{3,2,1,0:T(8,128)(2,1)S(1)}, u32[]{:S(2)}, u32[]{:S(2)}) collective-permute-start(bf16[4,4,16,1024]{3,2,1,0:T(8,128)(2,1)S(1)} %get-tuple-element.77), channel_id=1, source_target_pairs={{0,4},{4,0},{1,5},{5,1},{2,6},{6,2},{3,7},{7,3},{8,12},{12,8},{9,1... | collective-permute-start | bytes 1572872 | tf_op jit(solution)/shard_map/ppermute | solution.py:56
  104.2 10.8 %collective-permute-start.26 = (bf16[4,4,16,1024]{3,2,1,0:T(8,128)(2,1)S(1)}, bf16[4,4,16,1024]{3,2,1,0:T(8,128)(2,1)S(1)}, u32[]{:S(2)}, u32[]{:S(2)}) collective-permute-start(bf16[4,4,16,1024]{3,2,1,0:T(8,128)(2,1)S(1)} %down.8), channel_id=1, source_target_pairs={{0,16},{4,68},{8,24},{12,76},{16,0},{20,84},{24,8},{28,92},{32,48}... | collective-permute-start | bytes 1572872 | tf_op jit(solution)/shard_map/ppermute | solution.py:52
  108.9 12.1 %collective-permute-start.28 = (bf16[4,4,16,1024]{3,2,1,0:T(8,128)(2,1)S(1)}, bf16[4,4,16,1024]{3,2,1,0:T(8,128)(2,1)S(1)}, u32[]{:S(2)}, u32[]{:S(2)}) collective-permute-start(bf16[4,4,16,1024]{3,2,1,0:T(8,128)(2,1)S(1)} %down.9), channel_id=1, source_target_pairs={{0,24},{4,100},{8,0},{12,108},{16,8},{20,116},{24,16},{28,124},{32... | collective-permute-start | bytes 1572872 | tf_op jit(solution)/shard_map/ppermute | solution.py:52
  111.7 10.5 %collective-permute-start.30 = (bf16[4,4,16,1024]{3,2,1,0:T(8,128)(2,1)S(1)}, bf16[4,4,16,1024]{3,2,1,0:T(8,128)(2,1)S(1)}, u32[]{:S(2)}, u32[]{:S(2)}) collective-permute-start(bf16[4,4,16,1024]{3,2,1,0:T(8,128)(2,1)S(1)} %down.10), channel_id=1, source_target_pairs={{0,8},{4,36},{8,16},{12,44},{16,24},{20,52},{24,0},{28,60},{32,40}... | collective-permute-start | bytes 1572872 | tf_op jit(solution)/shard_map/ppermute | solution.py:52
  122.5 7.2 %collective-permute-start.32 = (bf16[4,16,1024]{2,1,0:T(8,128)(2,1)S(1)}, bf16[4,16,1024]{2,1,0:T(8,128)(2,1)S(1)}, u32[]{:S(2)}, u32[]{:S(2)}) collective-permute-start(bf16[4,16,1024]{2,1,0:T(8,128)(2,1)S(1)} %get-tuple-element.79), channel_id=1, source_target_pairs={{0,64},{4,20},{8,72},{12,28},{16,80},{20,4},{24,88},{28,12},{32,96... | collective-permute-start | bytes 393224 | tf_op jit(solution)/shard_map/ppermute | solution.py:52
  126.5 6.2 %collective-permute-start.34 = (bf16[4,16,1024]{2,1,0:T(8,128)(2,1)S(1)}, bf16[4,16,1024]{2,1,0:T(8,128)(2,1)S(1)}, u32[]{:S(2)}, u32[]{:S(2)}) collective-permute-start(bf16[4,16,1024]{2,1,0:T(8,128)(2,1)S(1)} %get-tuple-element.80), channel_id=1, source_target_pairs={{0,32},{4,12},{8,40},{12,20},{16,48},{20,28},{24,56},{28,4},{32,64... | collective-permute-start | bytes 393224 | tf_op jit(solution)/shard_map/ppermute | solution.py:52
  127.5 5.2 %collective-permute-start.33 = (bf16[4,16,1024]{2,1,0:T(8,128)(2,1)S(1)}, bf16[4,16,1024]{2,1,0:T(8,128)(2,1)S(1)}, u32[]{:S(2)}, u32[]{:S(2)}) collective-permute-start(bf16[4,16,1024]{2,1,0:T(8,128)(2,1)S(1)} %get-tuple-element.81), channel_id=1, source_target_pairs={{0,96},{4,28},{8,104},{12,4},{16,112},{20,12},{24,120},{28,20},{32... | collective-permute-start | bytes 393224 | tf_op jit(solution)/shard_map/ppermute | solution.py:52

commit v5 on v4

--- a/solution.py
+++ b/solution.py
@@ -388,8 +388,8 @@
                 if here == 0:
                     adds = adds | jnp.logical_not(moves)
                 value = value + jnp.where(adds, home, 0.0)
-                for other in theirs:
-                    value = value + other[d, from_x].astype(jnp.float32)
+                if theirs:
+                    value = value + theirs[n][d, from_x].astype(jnp.float32)
                 outs[n][d, from_x] = value.astype(jnp.bfloat16)
 
 
@@ -493,11 +493,11 @@
     sent[1][0], mine[2] = lax.optimization_barrier((sent[1][0], mine[2]))
     received = [other_core(value) for values in sent for value in values]
     total = []
-    for s, value in zip((2, 1, 3, 0), received):
+    for picks, values in (((2,), received[:1]), ((1, 3), received[1:3]), ((0,), received[3:])):
         if total:
-            value, _ = lax.optimization_barrier((value, made))
-        (made,) = down(0, (s,), place, slot, down_weight, mine, homes, (value,))
-        total.append(along_chips(made, -s, False) if s else made)
+            *values, _ = lax.optimization_barrier((*values, made[0]))
+        made = down(0, picks, place, slot, down_weight, mine, homes, tuple(values))
+        total += [along_chips(v, -s, False) if s else v for s, v in zip(picks, made)]
     total = add(total)
     out = add([along_chips(total[s], -s, True) for s in (2, 1, 3)] + [total[0]])
     return out.reshape(rows_here, width)

time: 134 us -> 132 us (0.985)
    pallas_call x6 -> x5, Pallas kernels: 10.3 us -> 8.95 us  [down(): pl.pallas_call(lambda *refs: down_kernel(base, picks, *refs), out_shape=[...]
where the time goes in v5:
time: 132 us
  starting transfers between devices  49.3 us (37%)
  waiting for transfers between devices  46.9 us (36%)
  Pallas kernels  33 us (25%)
  other arithmetic  2.19 us (2%)
    ppermute x12, starting transfers between devices, along_chips(): return lax.ppermute(value, REP, chip_ring(shift, first))  24.1 us
    ppermute x12, waiting for transfers between devices, along_chips(): return lax.ppermute(value, REP, chip_ring(shift, first))  22.7 us
    ppermute x15, waiting for transfers between devices, along_x(): return lax.ppermute(value, 'x', x_ring(shift))  18.8 us
    ppermute x15, starting transfers between devices, along_x(): return lax.ppermute(value, 'x', x_ring(shift))  18.6 us
    pallas_call x1, Pallas kernels, attend_project(): pl.pallas_call(attend_kernel, out_shape=[out] * SIDE, in_specs=[SM] + [HB...  12.9 us
    pallas_call x5, Pallas kernels, down(): pl.pallas_call(lambda *refs: down_kernel(base, picks, *refs), out_shape=[...  8.95 us
    pallas_call x1, Pallas kernels, gate_up_act(): pl.pallas_call(gate_up_kernel, out_shape=[jax.ShapeDtypeStruct((rows // 2...  8.47 us
    all_to_all x1, waiting for transfers between devices, local(): homes = lax.all_to_all(kept, 'x', 0, 0, tiled=True)  5.36 us
  transfers between devices with their start and end apart: 36, of which 19 were waited for; matrix products, arithmetic and copies ran while one was open for 1% of the time, Pallas kernels for 18%

profile of v5, /device:TPU:0, one launch (start us, length us, event | category | flops | bytes accessed | tf_op | source)
XLA Modules:
  0.0 132.0 jit_solution(14879069166745332344)
XLA Ops:
  0.0 1.3 %split.1 = (bf16[344,1024]{1,0:T(8,128)(2,1)S(1)}, bf16[344,1024]{1,0:T(8,128)(2,1)S(1)}) custom-call(bf16[2,344,1024]{2,1,0:T(8,128)(2,1)} %bitcast.20), custom_call_target="tpu_custom_call" | custom-call | tf_op jit(solution)/shard_map/split/pallas_call | solution.py:298
  1.4 1.6 %collective-permute-start.3 = (bf16[344,1024]{1,0:T(8,128)(2,1)S(1)}, bf16[344,1024]{1,0:T(8,128)(2,1)}, u32[]{:S(2)}, u32[]{:S(2)}) collective-permute-start(bf16[344,1024]{1,0:T(8,128)(2,1)S(1)} %get-tuple-element.58.refs_8_), channel_id=1, source_target_pairs={{0,1},{1,2},{2,3},{3,0},{4,5},{5,6},{6,7},{7,4},{8,9},{9,10},{10,1... | collective-permute-start | bytes 2113544 | tf_op jit(solution)/shard_map/ppermute | solution.py:48
  3.0 1.7 %collective-permute-start.4 = (bf16[344,1024]{1,0:T(8,128)(2,1)S(1)}, bf16[344,1024]{1,0:T(8,128)(2,1)}, u32[]{:S(2)}, u32[]{:S(2)}) collective-permute-start(bf16[344,1024]{1,0:T(8,128)(2,1)S(1)} %get-tuple-element.59.refs_9_), channel_id=1, source_target_pairs={{0,3},{1,0},{2,1},{3,2},{4,7},{5,4},{6,5},{7,6},{8,11},{9,8},{10,9... | collective-permute-start | bytes 2113544 | tf_op jit(solution)/shard_map/ppermute | solution.py:48
  4.7 12.9 %attend_project.1 = (bf16[16,4224]{1,0:T(8,128)(2,1)S(1)}, bf16[16,4224]{1,0:T(8,128)(2,1)S(1)}, bf16[16,4224]{1,0:T(8,128)(2,1)S(1)}, bf16[16,4224]{1,0:T(8,128)(2,1)S(1)}) custom-call(s32[2]{0:T(128)S(1)} %pad_add_fusion.place.refs_0_, s32[2,64]{1,0:T(2,128)} %bitcast.22, s32[2048]{0:T(1024)} %spans.1, bf16[64,1024]{1,0:T(8,128)(2,1)} %query.1, ...), custom_call_target="tpu_custom_call" | custom-call | flops 536870912 | bytes 16777216 | tf_op jit(solution)/shard_map/attend_project/pallas_call | solution.py:188
  18.1 2.7 %collective-permute-start.1 = (bf16[16,4224]{1,0:T(8,128)(2,1)S(1)}, bf16[16,4224]{1,0:T(8,128)(2,1)S(1)}, u32[]{:S(2)}, u32[]{:S(2)}) collective-permute-start(bf16[16,4224]{1,0:T(8,128)(2,1)S(1)} %get-tuple-element.46), channel_id=1, source_target_pairs={{0,2},{1,3},{2,0},{3,1},{4,6},{5,7},{6,4},{7,5},{8,10},{9,11},{10,... | collective-permute-start | bytes 405512 | tf_op jit(solution)/shard_map/ppermute | solution.py:48
  20.8 1.4 %collective-permute-start.2 = (bf16[16,4224]{1,0:T(8,128)(2,1)S(1)}, bf16[16,4224]{1,0:T(8,128)(2,1)S(1)}, u32[]{:S(2)}, u32[]{:S(2)}) collective-permute-start(bf16[16,4224]{1,0:T(8,128)(2,1)S(1)} %get-tuple-element.47), channel_id=1, source_target_pairs={{0,3},{1,0},{2,1},{3,2},{4,7},{5,4},{6,5},{7,6},{8,11},{9,8},{10,9... | collective-permute-start | bytes 405512 | tf_op jit(solution)/shard_map/ppermute | solution.py:48
  22.3 2.7 %collective-permute-done.refs_1_ = bf16[16,4224]{1,0:T(8,128)(2,1)S(1)} collective-permute-done((bf16[16,4224]{1,0:T(8,128)(2,1)S(1)}, bf16[16,4224]{1,0:T(8,128)(2,1)S(1)}, u32[]{:S(2)}, u32[]{:S(2)}) %collective-permute-start) | collective-permute-done | bytes 135200 | tf_op jit(solution)/shard_map/ppermute | solution.py:48
  24.9 2.1 %collective-permute-done.1.refs_2_ = bf16[16,4224]{1,0:T(8,128)(2,1)S(1)} collective-permute-done((bf16[16,4224]{1,0:T(8,128)(2,1)S(1)}, bf16[16,4224]{1,0:T(8,128)(2,1)S(1)}, u32[]{:S(2)}, u32[]{:S(2)}) %collective-permute-start.1) | collective-permute-done | bytes 135200 | tf_op jit(solution)/shard_map/ppermute | solution.py:48
  27.1 1.3 normalise.1
  28.4 1.3 %collective-permute-start.8 = (bf16[344,1024]{1,0:T(8,128)(2,1)}, bf16[344,1024]{1,0:T(8,128)(2,1)}, u32[]{:S(2)}, u32[]{:S(2)}) collective-permute-start(bf16[344,1024]{1,0:T(8,128)(2,1)} %collective-permute-done.3.refs_10_), channel_id=1, source_target_pairs={{0,1},{1,2},{2,3},{3,0},{4,5},{5,6},{6,7},{7,4},{8,9},{9,10},{10,1... | collective-permute-start | bytes 2113544 | tf_op jit(solution)/shard_map/ppermute | solution.py:48
  29.8 1.9 %collective-permute-start.9 = (bf16[344,1024]{1,0:T(8,128)(2,1)}, bf16[344,1024]{1,0:T(8,128)(2,1)}, u32[]{:S(2)}, u32[]{:S(2)}) collective-permute-start(bf16[344,1024]{1,0:T(8,128)(2,1)} %collective-permute-done.4.refs_15_), channel_id=1, source_target_pairs={{0,3},{1,0},{2,1},{3,2},{4,7},{5,4},{6,5},{7,6},{8,11},{9,8},{10,9... | collective-permute-start | bytes 2113544 | tf_op jit(solution)/shard_map/ppermute | solution.py:48
  31.7 4.2 %collective-permute-start.7 = (bf16[16,4096]{1,0:T(8,128)(2,1)S(1)}, bf16[16,4096]{1,0:T(8,128)(2,1)S(1)}, u32[]{:S(2)}, u32[]{:S(2)}) collective-permute-start(bf16[16,4096]{1,0:T(8,128)(2,1)S(1)} %get-tuple-element.51.refs_0_), channel_id=1, source_target_pairs={{0,96},{4,28},{8,104},{12,4},{16,112},{20,12},{24,120},{28,20},{32... | collective-permute-start | bytes 393224 | tf_op jit(solution)/shard_map/ppermute | solution.py:52
  35.8 1.3 collective-permute-start.5
  37.1 3.3 %all-to-all-start = ((bf16[4,16,1024]{2,1,0:T(8,128)(2,1)}), bf16[4,16,1024]{2,1,0:T(8,128)(2,1)S(1)}, u32[]{:S(2)}, u32[]{:S(2)}) async-start(bf16[4,16,1024]{2,1,0:T(8,128)(2,1)} %get-tuple-element.54), calls=%async_computation | async-start | bytes 262144 | tf_op jit(solution)/shard_map/all_to_all | solution.py:463
  40.4 2.0 %collective-permute-done.6.refs_2_ = bf16[16,4096]{1,0:T(8,128)(2,1)S(1)} collective-permute-done((bf16[16,4096]{1,0:T(8,128)(2,1)S(1)}, bf16[16,4096]{1,0:T(8,128)(2,1)S(1)}, u32[]{:S(2)}, u32[]{:S(2)}) %collective-permute-start.6) | collective-permute-done | bytes 131104 | tf_op jit(solution)/shard_map/ppermute | solution.py:52
  42.4 1.0 collective-permute-done.5.refs_1_
  43.4 5.4 %all-to-all-done.refs_7_ = bf16[4,16,1024]{2,1,0:T(8,128)(2,1)S(1)} async-done(((bf16[4,16,1024]{2,1,0:T(8,128)(2,1)}), bf16[4,16,1024]{2,1,0:T(8,128)(2,1)S(1)}, u32[]{:S(2)}, u32[]{:S(2)}) %all-to-all-start) | async-done | bytes 131104 | tf_op jit(solution)/shard_map/all_to_all | solution.py:463
  48.8 2.0 %collective-permute-start.18 = (bf16[344,1024]{1,0:T(8,128)(2,1)S(1)}, bf16[344,1024]{1,0:T(8,128)(2,1)}, u32[]{:S(2)}, u32[]{:S(2)}) collective-permute-start(bf16[344,1024]{1,0:T(8,128)(2,1)S(1)} %get-tuple-element.58.refs_8_), channel_id=1, source_target_pairs={{0,3},{1,0},{2,1},{3,2},{4,7},{5,4},{6,5},{7,6},{8,11},{9,8},{10,9... | collective-permute-start | bytes 2113544 | tf_op jit(solution)/shard_map/ppermute | solution.py:48
  50.8 1.7 %collective-permute-start.10 = (bf16[64,4096]{1,0:T(8,128)(2,1)S(1)}, bf16[64,4096]{1,0:T(8,128)(2,1)}, u32[]{:S(2)}, u32[]{:S(2)}) collective-permute-start(bf16[64,4096]{1,0:T(8,128)(2,1)S(1)} %join.1.refs_0_), channel_id=1, source_target_pairs={{0,8},{4,36},{8,16},{12,44},{16,24},{20,52},{24,0},{28,60},{32,40}... | collective-permute-start | bytes 1572872 | tf_op jit(solution)/shard_map/ppermute | solution.py:52
  52.5 1.5 %collective-permute-start.12 = (bf16[64,4096]{1,0:T(8,128)(2,1)S(1)}, bf16[64,4096]{1,0:T(8,128)(2,1)}, u32[]{:S(2)}, u32[]{:S(2)}) collective-permute-start(bf16[64,4096]{1,0:T(8,128)(2,1)S(1)} %join.1.refs_0_), channel_id=1, source_target_pairs={{0,24},{4,100},{8,0},{12,108},{16,8},{20,116},{24,16},{28,124},{32... | collective-permute-start | bytes 1572872 | tf_op jit(solution)/shard_map/ppermute | solution.py:52
  54.0 2.1 %collective-permute-start.11 = (bf16[64,4096]{1,0:T(8,128)(2,1)S(1)}, bf16[64,4096]{1,0:T(8,128)(2,1)}, u32[]{:S(2)}, u32[]{:S(2)}) collective-permute-start(bf16[64,4096]{1,0:T(8,128)(2,1)S(1)} %join.1.refs_0_), channel_id=1, source_target_pairs={{0,16},{4,68},{8,24},{12,76},{16,0},{20,84},{24,8},{28,92},{32,48}... | collective-permute-start | bytes 1572872 | tf_op jit(solution)/shard_map/ppermute | solution.py:52
  56.7 4.6 %collective-permute-done.10.refs_1_ = bf16[64,4096]{1,0:T(8,128)(2,1)} collective-permute-done((bf16[64,4096]{1,0:T(8,128)(2,1)S(1)}, bf16[64,4096]{1,0:T(8,128)(2,1)}, u32[]{:S(2)}, u32[]{:S(2)}) %collective-permute-start.10) | collective-permute-done | bytes 524320 | tf_op jit(solution)/shard_map/ppermute | solution.py:52
  61.8 1.6 %collective-permute-start.14 = (bf16[64,4096]{1,0:T(8,128)(2,1)}, bf16[64,4096]{1,0:T(8,128)(2,1)}, u32[]{:S(2)}, u32[]{:S(2)}) collective-permute-start(bf16[64,4096]{1,0:T(8,128)(2,1)} %collective-permute-done.10.refs_1_), channel_id=1, source_target_pairs={{0,4},{4,0},{1,5},{5,1},{2,6},{6,2},{3,7},{7,3},{8,12},{12,8},{9,1... | collective-permute-start | bytes 1572872 | tf_op jit(solution)/shard_map/ppermute | solution.py:56
  63.4 4.9 %collective-permute-done.11.refs_2_ = bf16[64,4096]{1,0:T(8,128)(2,1)} collective-permute-done((bf16[64,4096]{1,0:T(8,128)(2,1)S(1)}, bf16[64,4096]{1,0:T(8,128)(2,1)}, u32[]{:S(2)}, u32[]{:S(2)}) %collective-permute-start.11) | collective-permute-done | bytes 524320 | tf_op jit(solution)/shard_map/ppermute | solution.py:52
  69.8 2.2 %collective-permute-done.17.refs_11_ = bf16[344,1024]{1,0:T(8,128)(2,1)} collective-permute-done((bf16[344,1024]{1,0:T(8,128)(2,1)S(1)}, bf16[344,1024]{1,0:T(8,128)(2,1)}, u32[]{:S(2)}, u32[]{:S(2)}) %collective-permute-start.17) | collective-permute-done | bytes 704544 | tf_op jit(solution)/shard_map/ppermute | solution.py:48
  72.0 8.5 %gate_up_act.1 = (bf16[256,344]{1,0:T(8,128)(2,1)S(1)}, bf16[256,344]{1,0:T(8,128)(2,1)S(1)}) custom-call(s32[2]{0:T(128)S(1)} %pad_add_fusion.place.refs_0_, s32[32]{0:T(128)S(1)} %get-tuple-element.86.source, bf16[64,4096]{1,0:T(8,128)(2,1)S(1)} %join.1.refs_0_, bf16[64,4096]{1,0:T(8,128)(2,1)} %collective-permute-done.10.refs_1_, ...), custom_call_target="tpu_custom_call" | custom-call | flops 2885681152 | bytes 14090240 | tf_op jit(solution)/shard_map/gate_up_act/pallas_call | solution.py:349
  80.6 3.2 %collective-permute-start.21 = (bf16[256,344]{1,0:T(8,128)(2,1)S(1)}, bf16[256,344]{1,0:T(8,128)(2,1)S(1)}, u32[]{:S(2)}, u32[]{:S(2)}) collective-permute-start(bf16[256,344]{1,0:T(8,128)(2,1)S(1)} %get-tuple-element.66.refs_3_), channel_id=1, source_target_pairs={{0,3},{1,0},{2,1},{3,2},{4,7},{5,4},{6,5},{7,6},{8,11},{9,8},{10,9... | collective-permute-start | bytes 528392 | tf_op jit(solution)/shard_map/ppermute | solution.py:48
  83.8 2.0 %collective-permute-start.22 = (bf16[256,344]{1,0:T(8,128)(2,1)S(1)}, bf16[256,344]{1,0:T(8,128)(2,1)S(1)}, u32[]{:S(2)}, u32[]{:S(2)}) collective-permute-start(bf16[256,344]{1,0:T(8,128)(2,1)S(1)} %get-tuple-element.65.refs_3_), channel_id=1, source_target_pairs={{0,1},{1,2},{2,3},{3,0},{4,5},{5,6},{6,7},{7,4},{8,9},{9,10},{10,1... | collective-permute-start | bytes 528392 | tf_op jit(solution)/shard_map/ppermute | solution.py:48
  85.8 3.6 %collective-permute-done.19.refs_4_ = bf16[256,344]{1,0:T(8,128)(2,1)S(1)} collective-permute-done((bf16[256,344]{1,0:T(8,128)(2,1)S(1)}, bf16[256,344]{1,0:T(8,128)(2,1)S(1)}, u32[]{:S(2)}, u32[]{:S(2)}) %collective-permute-start.19) | collective-permute-done | bytes 176160 | tf_op jit(solution)/shard_map/ppermute | solution.py:48
  89.4 2.0 %collective-permute-done.23.refs_6_ = bf16[256,344]{1,0:T(8,128)(2,1)S(1)} collective-permute-done((bf16[256,344]{1,0:T(8,128)(2,1)S(1)}, bf16[256,344]{1,0:T(8,128)(2,1)S(1)}, u32[]{:S(2)}, u32[]{:S(2)}) %collective-permute-start.23) | collective-permute-done | bytes 176160 | tf_op jit(solution)/shard_map/ppermute | solution.py:48
  91.4 2.2 %collective-permute-done.22.refs_4_ = bf16[256,344]{1,0:T(8,128)(2,1)S(1)} collective-permute-done((bf16[256,344]{1,0:T(8,128)(2,1)S(1)}, bf16[256,344]{1,0:T(8,128)(2,1)S(1)}, u32[]{:S(2)}, u32[]{:S(2)}) %collective-permute-start.22) | collective-permute-done | bytes 176160 | tf_op jit(solution)/shard_map/ppermute | solution.py:48
  93.6 2.7 %collective-permute-done.20.refs_5_ = bf16[256,344]{1,0:T(8,128)(2,1)S(1)} collective-permute-done((bf16[256,344]{1,0:T(8,128)(2,1)S(1)}, bf16[256,344]{1,0:T(8,128)(2,1)S(1)}, u32[]{:S(2)}, u32[]{:S(2)}) %collective-permute-start.20) | collective-permute-done | bytes 176160 | tf_op jit(solution)/shard_map/ppermute | solution.py:48
  96.3 1.9 %down.6 = (bf16[4,4,16,1024]{3,2,1,0:T(8,128)(2,1)S(1)}, bf16[4,4,16,1024]{3,2,1,0:T(8,128)(2,1)S(1)}) custom-call(s32[2]{0:T(128)S(1)} %pad_add_fusion.place.refs_0_, s32[1]{0:T(128)} %bitcast.2.refs_1_, bf16[344,1024]{1,0:T(8,128)(2,1)S(1)} %copy-done, bf16[256,344]{1,0:T(8,128)(2,1)S(1)} %get-tuple-element.66.refs_3_, ...), custom_call_target="tpu_custom_call" | custom-call | flops 360710144 | bytes 1409024 | tf_op jit(solution)/shard_map/down/pallas_call | solution.py:399
  98.8 1.9 %down.5 = (bf16[4,4,16,1024]{3,2,1,0:T(8,128)(2,1)S(1)}, bf16[4,4,16,1024]{3,2,1,0:T(8,128)(2,1)S(1)}) custom-call(s32[2]{0:T(128)S(1)} %pad_add_fusion.place.refs_0_, s32[1]{0:T(128)} %bitcast.2.refs_1_, bf16[344,1024]{1,0:T(8,128)(2,1)S(1)} %copy-done, bf16[256,344]{1,0:T(8,128)(2,1)S(1)} %get-tuple-element.66.refs_3_, ...), custom_call_target="tpu_custom_call" | custom-call | flops 360710144 | bytes 1409024 | tf_op jit(solution)/shard_map/down/pallas_call | solution.py:399
  100.7 1.3 collective-permute-done.24.refs_5_
  102.5 1.6 %down.7 = bf16[4,4,16,1024]{3,2,1,0:T(8,128)(2,1)S(1)} custom-call(s32[2]{0:T(128)S(1)} %pad_add_fusion.place.refs_0_, s32[1]{0:T(128)} %bitcast.2.refs_1_, bf16[344,1024]{1,0:T(8,128)(2,1)S(1)} %copy-done, bf16[256,344]{1,0:T(8,128)(2,1)S(1)} %get-tuple-element.65.refs_3_, bf16[256,344]{1,0:T(8,128)(2,1)S(1)} %collective-permute-done.22.refs_4_, ...), custom_call_target="tpu_custom_call" | custom-call | flops 180355072 | bytes 704512 | tf_op jit(solution)/shard_map/down/pallas_call | solution.py:399
  104.2 3.2 %collective-permute-start.26 = (bf16[4,4,16,1024]{3,2,1,0:T(8,128)(2,1)S(1)}, bf16[4,4,16,1024]{3,2,1,0:T(8,128)(2,1)S(1)}, u32[]{:S(2)}, u32[]{:S(2)}) collective-permute-start(bf16[4,4,16,1024]{3,2,1,0:T(8,128)(2,1)S(1)} %down.7), channel_id=1, source_target_pairs={{0,16},{4,68},{8,24},{12,76},{16,0},{20,84},{24,8},{28,92},{32,48}... | collective-permute-start | bytes 1572872 | tf_op jit(solution)/shard_map/ppermute | solution.py:52
  107.3 1.9 %down.8 = (bf16[4,4,16,1024]{3,2,1,0:T(8,128)(2,1)S(1)}, bf16[4,4,16,1024]{3,2,1,0:T(8,128)(2,1)S(1)}) custom-call(s32[2]{0:T(128)S(1)} %pad_add_fusion.place.refs_0_, s32[1]{0:T(128)} %bitcast.2.refs_1_, bf16[344,1024]{1,0:T(8,128)(2,1)S(1)} %copy-done, bf16[256,344]{1,0:T(8,128)(2,1)S(1)} %get-tuple-element.65.refs_3_, ...), custom_call_target="tpu_custom_call" | custom-call | flops 360710144 | bytes 1409024 | tf_op jit(solution)/shard_map/down/pallas_call | solution.py:399
  109.2 1.0 collective-permute-start.30
  110.2 2.4 %collective-permute-start.29 = (bf16[4,4,16,1024]{3,2,1,0:T(8,128)(2,1)S(1)}, bf16[4,4,16,1024]{3,2,1,0:T(8,128)(2,1)S(1)}, u32[]{:S(2)}, u32[]{:S(2)}) collective-permute-start(bf16[4,4,16,1024]{3,2,1,0:T(8,128)(2,1)S(1)} %get-tuple-element.79), channel_id=1, source_target_pairs={{0,24},{4,100},{8,0},{12,108},{16,8},{20,116},{24,16},{28,124},{32... | collective-permute-start | bytes 1572872 | tf_op jit(solution)/shard_map/ppermute | solution.py:52
  112.5 1.6 %down.9 = bf16[4,4,16,1024]{3,2,1,0:T(8,128)(2,1)S(1)} custom-call(s32[2]{0:T(128)S(1)} %pad_add_fusion.place.refs_0_, s32[1]{0:T(128)} %bitcast.2.refs_1_, bf16[344,1024]{1,0:T(8,128)(2,1)S(1)} %copy-done, bf16[256,344]{1,0:T(8,128)(2,1)S(1)} %get-tuple-element.65.refs_3_, bf16[256,344]{1,0:T(8,128)(2,1)S(1)} %collective-permute-done.22.refs_4_, ...), custom_call_target="tpu_custom_call" | custom-call | flops 180355072 | bytes 704512 | tf_op jit(solution)/shard_map/down/pallas_call | solution.py:399
  114.2 0.8 collective-permute-done.26
  115.0 5.5 %collective-permute-done.30 = bf16[4,4,16,1024]{3,2,1,0:T(8,128)(2,1)S(1)} collective-permute-done((bf16[4,4,16,1024]{3,2,1,0:T(8,128)(2,1)S(1)}, bf16[4,4,16,1024]{3,2,1,0:T(8,128)(2,1)S(1)}, u32[]{:S(2)}, u32[]{:S(2)}) %collective-permute-start.30) | collective-permute-done | bytes 524320 | tf_op jit(solution)/shard_map/ppermute | solution.py:52
  121.4 3.7 %collective-permute-start.32 = (bf16[4,16,1024]{2,1,0:T(8,128)(2,1)S(1)}, bf16[4,16,1024]{2,1,0:T(8,128)(2,1)S(1)}, u32[]{:S(2)}, u32[]{:S(2)}) collective-permute-start(bf16[4,16,1024]{2,1,0:T(8,128)(2,1)S(1)} %get-tuple-element.83), channel_id=1, source_target_pairs={{0,64},{4,20},{8,72},{12,28},{16,80},{20,4},{24,88},{28,12},{32,96... | collective-permute-start | bytes 393224 | tf_op jit(solution)/shard_map/ppermute | solution.py:52
  125.1 1.0 collective-permute-start.34
  126.1 2.2 %collective-permute-start.33 = (bf16[4,16,1024]{2,1,0:T(8,128)(2,1)S(1)}, bf16[4,16,1024]{2,1,0:T(8,128)(2,1)S(1)}, u32[]{:S(2)}, u32[]{:S(2)}) collective-permute-start(bf16[4,16,1024]{2,1,0:T(8,128)(2,1)S(1)} %get-tuple-element.85), channel_id=1, source_target_pairs={{0,96},{4,28},{8,104},{12,4},{16,112},{20,12},{24,120},{28,20},{32... | collective-permute-start | bytes 393224 | tf_op jit(solution)/shard_map/ppermute | solution.py:52
  128.3 2.9 %collective-permute-done.34 = bf16[4,16,1024]{2,1,0:T(8,128)(2,1)S(1)} collective-permute-done((bf16[4,16,1024]{2,1,0:T(8,128)(2,1)S(1)}, bf16[4,16,1024]{2,1,0:T(8,128)(2,1)S(1)}, u32[]{:S(2)}, u32[]{:S(2)}) %collective-permute-start.34) | collective-permute-done | bytes 131104 | tf_op jit(solution)/shard_map/ppermute | solution.py:52
  131.2 0.7 fusion
  (57 shorter events, 5.3 us)
Async XLA Ops:
  1.3 47.5 %copy-start.1 = (bf16[344,1024]{1,0:T(8,128)(2,1)}, bf16[344,1024]{1,0:T(8,128)(2,1)S(1)}, u32[]{:S(2)}) copy-start(bf16[344,1024]{1,0:T(8,128)(2,1)S(1)} %get-tuple-element.58.refs_8_) | copy-start | bytes 2113540
  1.4 54.8 %copy-start.2 = (bf16[344,1024]{1,0:T(8,128)(2,1)}, bf16[344,1024]{1,0:T(8,128)(2,1)S(1)}, u32[]{:S(2)}) copy-start(bf16[344,1024]{1,0:T(8,128)(2,1)S(1)} %get-tuple-element.59.refs_9_) | copy-start | bytes 2113540
  1.4 27.1 %collective-permute-start.3 = (bf16[344,1024]{1,0:T(8,128)(2,1)S(1)}, bf16[344,1024]{1,0:T(8,128)(2,1)}, u32[]{:S(2)}, u32[]{:S(2)}) collective-permute-start(bf16[344,1024]{1,0:T(8,128)(2,1)S(1)} %get-tuple-element.58.refs_8_), channel_id=1, source_target_pairs={{0,1},{1,2},{2,3},{3,0},{4,5},{5,6},{6,7},{7,4},{8,9},{9,10},{10,1... | collective-permute-start | bytes 2113544 | tf_op jit(solution)/shard_map/ppermute | solution.py:48
  3.0 25.4 %collective-permute-start.4 = (bf16[344,1024]{1,0:T(8,128)(2,1)S(1)}, bf16[344,1024]{1,0:T(8,128)(2,1)}, u32[]{:S(2)}, u32[]{:S(2)}) collective-permute-start(bf16[344,1024]{1,0:T(8,128)(2,1)S(1)} %get-tuple-element.59.refs_9_), channel_id=1, source_target_pairs={{0,3},{1,0},{2,1},{3,2},{4,7},{5,4},{6,5},{7,6},{8,11},{9,8},{10,9... | collective-permute-start | bytes 2113544 | tf_op jit(solution)/shard_map/ppermute | solution.py:48
  4.7 64.1 %copy-start.3 = (s32[32]{0:T(128)S(1)}, s32[32]{0:T(128)}, u32[]{:S(2)}) copy-start(s32[32]{0:T(128)} %param.17) | copy-start | bytes 388
  17.6 78.7 %copy-start = (bf16[344,1024]{1,0:T(8,128)(2,1)S(1)}, bf16[344,1024]{1,0:T(8,128)(2,1)}, u32[]{:S(2)}) copy-start(bf16[344,1024]{1,0:T(8,128)(2,1)} %refs_2_.9) | copy-start | bytes 2113540
  17.7 7.3 %collective-permute-start = (bf16[16,4224]{1,0:T(8,128)(2,1)S(1)}, bf16[16,4224]{1,0:T(8,128)(2,1)S(1)}, u32[]{:S(2)}, u32[]{:S(2)}) collective-permute-start(bf16[16,4224]{1,0:T(8,128)(2,1)S(1)} %get-tuple-element.45), channel_id=1, source_target_pairs={{0,1},{1,2},{2,3},{3,0},{4,5},{5,6},{6,7},{7,4},{8,9},{9,10},{10,1... | collective-permute-start | bytes 405512 | tf_op jit(solution)/shard_map/ppermute | solution.py:48
  18.1 8.9 %collective-permute-start.1 = (bf16[16,4224]{1,0:T(8,128)(2,1)S(1)}, bf16[16,4224]{1,0:T(8,128)(2,1)S(1)}, u32[]{:S(2)}, u32[]{:S(2)}) collective-permute-start(bf16[16,4224]{1,0:T(8,128)(2,1)S(1)} %get-tuple-element.46), channel_id=1, source_target_pairs={{0,2},{1,3},{2,0},{3,1},{4,6},{5,7},{6,4},{7,5},{8,10},{9,11},{10,... | collective-permute-start | bytes 405512 | tf_op jit(solution)/shard_map/ppermute | solution.py:48
  20.8 6.3 %collective-permute-start.2 = (bf16[16,4224]{1,0:T(8,128)(2,1)S(1)}, bf16[16,4224]{1,0:T(8,128)(2,1)S(1)}, u32[]{:S(2)}, u32[]{:S(2)}) collective-permute-start(bf16[16,4224]{1,0:T(8,128)(2,1)S(1)} %get-tuple-element.47), channel_id=1, source_target_pairs={{0,3},{1,0},{2,1},{3,2},{4,7},{5,4},{6,5},{7,6},{8,11},{9,8},{10,9... | collective-permute-start | bytes 405512 | tf_op jit(solution)/shard_map/ppermute | solution.py:48
  28.4 20.4 %collective-permute-start.8 = (bf16[344,1024]{1,0:T(8,128)(2,1)}, bf16[344,1024]{1,0:T(8,128)(2,1)}, u32[]{:S(2)}, u32[]{:S(2)}) collective-permute-start(bf16[344,1024]{1,0:T(8,128)(2,1)} %collective-permute-done.3.refs_10_), channel_id=1, source_target_pairs={{0,1},{1,2},{2,3},{3,0},{4,5},{5,6},{6,7},{7,4},{8,9},{9,10},{10,1... | collective-permute-start | bytes 2113544 | tf_op jit(solution)/shard_map/ppermute | solution.py:48
  29.8 19.1 %collective-permute-start.9 = (bf16[344,1024]{1,0:T(8,128)(2,1)}, bf16[344,1024]{1,0:T(8,128)(2,1)}, u32[]{:S(2)}, u32[]{:S(2)}) collective-permute-start(bf16[344,1024]{1,0:T(8,128)(2,1)} %collective-permute-done.4.refs_15_), channel_id=1, source_target_pairs={{0,3},{1,0},{2,1},{3,2},{4,7},{5,4},{6,5},{7,6},{8,11},{9,8},{10,9... | collective-permute-start | bytes 2113544 | tf_op jit(solution)/shard_map/ppermute | solution.py:48
  31.7 8.7 %collective-permute-start.7 = (bf16[16,4096]{1,0:T(8,128)(2,1)S(1)}, bf16[16,4096]{1,0:T(8,128)(2,1)S(1)}, u32[]{:S(2)}, u32[]{:S(2)}) collective-permute-start(bf16[16,4096]{1,0:T(8,128)(2,1)S(1)} %get-tuple-element.51.refs_0_), channel_id=1, source_target_pairs={{0,96},{4,28},{8,104},{12,4},{16,112},{20,12},{24,120},{28,20},{32... | collective-permute-start | bytes 393224 | tf_op jit(solution)/shard_map/ppermute | solution.py:52
  35.8 6.6 %collective-permute-start.6 = (bf16[16,4096]{1,0:T(8,128)(2,1)S(1)}, bf16[16,4096]{1,0:T(8,128)(2,1)S(1)}, u32[]{:S(2)}, u32[]{:S(2)}) collective-permute-start(bf16[16,4096]{1,0:T(8,128)(2,1)S(1)} %get-tuple-element.51.refs_0_), channel_id=1, source_target_pairs={{0,64},{4,20},{8,72},{12,28},{16,80},{20,4},{24,88},{28,12},{32,96... | collective-permute-start | bytes 393224 | tf_op jit(solution)/shard_map/ppermute | solution.py:52
  35.8 7.6 %collective-permute-start.5 = (bf16[16,4096]{1,0:T(8,128)(2,1)S(1)}, bf16[16,4096]{1,0:T(8,128)(2,1)S(1)}, u32[]{:S(2)}, u32[]{:S(2)}) collective-permute-start(bf16[16,4096]{1,0:T(8,128)(2,1)S(1)} %get-tuple-element.51.refs_0_), channel_id=1, source_target_pairs={{0,32},{4,12},{8,40},{12,20},{16,48},{20,28},{24,56},{28,4},{32,64... | collective-permute-start | bytes 393224 | tf_op jit(solution)/shard_map/ppermute | solution.py:52
  37.1 11.7 %all-to-all-start = ((bf16[4,16,1024]{2,1,0:T(8,128)(2,1)}), bf16[4,16,1024]{2,1,0:T(8,128)(2,1)S(1)}, u32[]{:S(2)}, u32[]{:S(2)}) async-start(bf16[4,16,1024]{2,1,0:T(8,128)(2,1)} %get-tuple-element.54), calls=%async_computation | async-start | bytes 262144 | tf_op jit(solution)/shard_map/all_to_all | solution.py:463
  48.8 19.5 %collective-permute-start.18 = (bf16[344,1024]{1,0:T(8,128)(2,1)S(1)}, bf16[344,1024]{1,0:T(8,128)(2,1)}, u32[]{:S(2)}, u32[]{:S(2)}) collective-permute-start(bf16[344,1024]{1,0:T(8,128)(2,1)S(1)} %get-tuple-element.58.refs_8_), channel_id=1, source_target_pairs={{0,3},{1,0},{2,1},{3,2},{4,7},{5,4},{6,5},{7,6},{8,11},{9,8},{10,9... | collective-permute-start | bytes 2113544 | tf_op jit(solution)/shard_map/ppermute | solution.py:48
  50.8 10.5 %collective-permute-start.10 = (bf16[64,4096]{1,0:T(8,128)(2,1)S(1)}, bf16[64,4096]{1,0:T(8,128)(2,1)}, u32[]{:S(2)}, u32[]{:S(2)}) collective-permute-start(bf16[64,4096]{1,0:T(8,128)(2,1)S(1)} %join.1.refs_0_), channel_id=1, source_target_pairs={{0,8},{4,36},{8,16},{12,44},{16,24},{20,52},{24,0},{28,60},{32,40}... | collective-permute-start | bytes 1572872 | tf_op jit(solution)/shard_map/ppermute | solution.py:52
  52.5 9.3 %collective-permute-start.12 = (bf16[64,4096]{1,0:T(8,128)(2,1)S(1)}, bf16[64,4096]{1,0:T(8,128)(2,1)}, u32[]{:S(2)}, u32[]{:S(2)}) collective-permute-start(bf16[64,4096]{1,0:T(8,128)(2,1)S(1)} %join.1.refs_0_), channel_id=1, source_target_pairs={{0,24},{4,100},{8,0},{12,108},{16,8},{20,116},{24,16},{28,124},{32... | collective-permute-start | bytes 1572872 | tf_op jit(solution)/shard_map/ppermute | solution.py:52
  54.0 14.2 %collective-permute-start.11 = (bf16[64,4096]{1,0:T(8,128)(2,1)S(1)}, bf16[64,4096]{1,0:T(8,128)(2,1)}, u32[]{:S(2)}, u32[]{:S(2)}) collective-permute-start(bf16[64,4096]{1,0:T(8,128)(2,1)S(1)} %join.1.refs_0_), channel_id=1, source_target_pairs={{0,16},{4,68},{8,24},{12,76},{16,0},{20,84},{24,8},{28,92},{32,48}... | collective-permute-start | bytes 1572872 | tf_op jit(solution)/shard_map/ppermute | solution.py:52
  56.1 15.8 %collective-permute-start.17 = (bf16[344,1024]{1,0:T(8,128)(2,1)S(1)}, bf16[344,1024]{1,0:T(8,128)(2,1)}, u32[]{:S(2)}, u32[]{:S(2)}) collective-permute-start(bf16[344,1024]{1,0:T(8,128)(2,1)S(1)} %get-tuple-element.59.refs_9_), channel_id=1, source_target_pairs={{0,1},{1,2},{2,3},{3,0},{4,5},{5,6},{6,7},{7,4},{8,9},{9,10},{10,1... | collective-permute-start | bytes 2113544 | tf_op jit(solution)/shard_map/ppermute | solution.py:48
  61.3 10.7 %collective-permute-start.13 = (bf16[64,4096]{1,0:T(8,128)(2,1)S(1)}, bf16[64,4096]{1,0:T(8,128)(2,1)}, u32[]{:S(2)}, u32[]{:S(2)}) collective-permute-start(bf16[64,4096]{1,0:T(8,128)(2,1)S(1)} %join.1.refs_0_), channel_id=1, source_target_pairs={{0,4},{4,0},{1,5},{5,1},{2,6},{6,2},{3,7},{7,3},{8,12},{12,8},{9,1... | collective-permute-start | bytes 1572872 | tf_op jit(solution)/shard_map/ppermute | solution.py:56
  61.8 10.2 %collective-permute-start.14 = (bf16[64,4096]{1,0:T(8,128)(2,1)}, bf16[64,4096]{1,0:T(8,128)(2,1)}, u32[]{:S(2)}, u32[]{:S(2)}) collective-permute-start(bf16[64,4096]{1,0:T(8,128)(2,1)} %collective-permute-done.10.refs_1_), channel_id=1, source_target_pairs={{0,4},{4,0},{1,5},{5,1},{2,6},{6,2},{3,7},{7,3},{8,12},{12,8},{9,1... | collective-permute-start | bytes 1572872 | tf_op jit(solution)/shard_map/ppermute | solution.py:56
  68.3 3.7 %collective-permute-start.16 = (bf16[64,4096]{1,0:T(8,128)(2,1)}, bf16[64,4096]{1,0:T(8,128)(2,1)}, u32[]{:S(2)}, u32[]{:S(2)}) collective-permute-start(bf16[64,4096]{1,0:T(8,128)(2,1)} %collective-permute-done.12.refs_3_), channel_id=1, source_target_pairs={{0,4},{4,0},{1,5},{5,1},{2,6},{6,2},{3,7},{7,3},{8,12},{12,8},{9,1... | collective-permute-start | bytes 1572872 | tf_op jit(solution)/shard_map/ppermute | solution.py:56
  68.3 3.7 %collective-permute-start.15 = (bf16[64,4096]{1,0:T(8,128)(2,1)}, bf16[64,4096]{1,0:T(8,128)(2,1)S(1)}, u32[]{:S(2)}, u32[]{:S(2)}) collective-permute-start(bf16[64,4096]{1,0:T(8,128)(2,1)} %collective-permute-done.11.refs_2_), channel_id=1, source_target_pairs={{0,4},{4,0},{1,5},{5,1},{2,6},{6,2},{3,7},{7,3},{8,12},{12,8},{9,1... | collective-permute-start | bytes 1572872 | tf_op jit(solution)/shard_map/ppermute | solution.py:56
  80.5 8.9 %collective-permute-start.19 = (bf16[256,344]{1,0:T(8,128)(2,1)S(1)}, bf16[256,344]{1,0:T(8,128)(2,1)S(1)}, u32[]{:S(2)}, u32[]{:S(2)}) collective-permute-start(bf16[256,344]{1,0:T(8,128)(2,1)S(1)} %get-tuple-element.66.refs_3_), channel_id=1, source_target_pairs={{0,1},{1,2},{2,3},{3,0},{4,5},{5,6},{6,7},{7,4},{8,9},{9,10},{10,1... | collective-permute-start | bytes 528392 | tf_op jit(solution)/shard_map/ppermute | solution.py:48
  80.6 8.8 %collective-permute-start.21 = (bf16[256,344]{1,0:T(8,128)(2,1)S(1)}, bf16[256,344]{1,0:T(8,128)(2,1)S(1)}, u32[]{:S(2)}, u32[]{:S(2)}) collective-permute-start(bf16[256,344]{1,0:T(8,128)(2,1)S(1)} %get-tuple-element.66.refs_3_), channel_id=1, source_target_pairs={{0,3},{1,0},{2,1},{3,2},{4,7},{5,4},{6,5},{7,6},{8,11},{9,8},{10,9... | collective-permute-start | bytes 528392 | tf_op jit(solution)/shard_map/ppermute | solution.py:48
  83.8 7.6 %collective-permute-start.23 = (bf16[256,344]{1,0:T(8,128)(2,1)S(1)}, bf16[256,344]{1,0:T(8,128)(2,1)S(1)}, u32[]{:S(2)}, u32[]{:S(2)}) collective-permute-start(bf16[256,344]{1,0:T(8,128)(2,1)S(1)} %get-tuple-element.65.refs_3_), channel_id=1, source_target_pairs={{0,3},{1,0},{2,1},{3,2},{4,7},{5,4},{6,5},{7,6},{8,11},{9,8},{10,9... | collective-permute-start | bytes 528392 | tf_op jit(solution)/shard_map/ppermute | solution.py:48
  83.8 9.8 %collective-permute-start.22 = (bf16[256,344]{1,0:T(8,128)(2,1)S(1)}, bf16[256,344]{1,0:T(8,128)(2,1)S(1)}, u32[]{:S(2)}, u32[]{:S(2)}) collective-permute-start(bf16[256,344]{1,0:T(8,128)(2,1)S(1)} %get-tuple-element.65.refs_3_), channel_id=1, source_target_pairs={{0,1},{1,2},{2,3},{3,0},{4,5},{5,6},{6,7},{7,4},{8,9},{9,10},{10,1... | collective-permute-start | bytes 528392 | tf_op jit(solution)/shard_map/ppermute | solution.py:48
  89.4 6.9 %collective-permute-start.20 = (bf16[256,344]{1,0:T(8,128)(2,1)S(1)}, bf16[256,344]{1,0:T(8,128)(2,1)S(1)}, u32[]{:S(2)}, u32[]{:S(2)}) collective-permute-start(bf16[256,344]{1,0:T(8,128)(2,1)S(1)} %collective-permute-done.19.refs_4_), channel_id=1, source_target_pairs={{0,1},{1,2},{2,3},{3,0},{4,5},{5,6},{6,7},{7,4},{8,9},{9,10},{10,1... | collective-permute-start | bytes 528392 | tf_op jit(solution)/shard_map/ppermute | solution.py:48
  96.3 5.7 %collective-permute-start.24 = (bf16[256,344]{1,0:T(8,128)(2,1)S(1)}, bf16[256,344]{1,0:T(8,128)(2,1)S(1)}, u32[]{:S(2)}, u32[]{:S(2)}) collective-permute-start(bf16[256,344]{1,0:T(8,128)(2,1)S(1)} %collective-permute-done.23.refs_6_), channel_id=1, source_target_pairs={{0,3},{1,0},{2,1},{3,2},{4,7},{5,4},{6,5},{7,6},{8,11},{9,8},{10,9... | collective-permute-start | bytes 528392 | tf_op jit(solution)/shard_map/ppermute | solution.py:48
  98.2 4.3 %collective-permute-start.25 = (bf16[4,4,16,1024]{3,2,1,0:T(8,128)(2,1)S(1)}, bf16[4,4,16,1024]{3,2,1,0:T(8,128)(2,1)S(1)}, u32[]{:S(2)}, u32[]{:S(2)}) collective-permute-start(bf16[4,4,16,1024]{3,2,1,0:T(8,128)(2,1)S(1)} %get-tuple-element.74), channel_id=1, source_target_pairs={{0,4},{4,0},{1,5},{5,1},{2,6},{6,2},{3,7},{7,3},{8,12},{12,8},{9,1... | collective-permute-start | bytes 1572872 | tf_op jit(solution)/shard_map/ppermute | solution.py:56
  98.3 9.0 %collective-permute-start.27 = (bf16[4,4,16,1024]{3,2,1,0:T(8,128)(2,1)S(1)}, bf16[4,4,16,1024]{3,2,1,0:T(8,128)(2,1)S(1)}, u32[]{:S(2)}, u32[]{:S(2)}) collective-permute-start(bf16[4,4,16,1024]{3,2,1,0:T(8,128)(2,1)S(1)} %get-tuple-element.75), channel_id=1, source_target_pairs={{0,4},{4,0},{1,5},{5,1},{2,6},{6,2},{3,7},{7,3},{8,12},{12,8},{9,1... | collective-permute-start | bytes 1572872 | tf_op jit(solution)/shard_map/ppermute | solution.py:56
  102.0 5.3 %collective-permute-start.28 = (bf16[4,4,16,1024]{3,2,1,0:T(8,128)(2,1)S(1)}, bf16[4,4,16,1024]{3,2,1,0:T(8,128)(2,1)S(1)}, u32[]{:S(2)}, u32[]{:S(2)}) collective-permute-start(bf16[4,4,16,1024]{3,2,1,0:T(8,128)(2,1)S(1)} %get-tuple-element.76), channel_id=1, source_target_pairs={{0,4},{4,0},{1,5},{5,1},{2,6},{6,2},{3,7},{7,3},{8,12},{12,8},{9,1... | collective-permute-start | bytes 1572872 | tf_op jit(solution)/shard_map/ppermute | solution.py:56
  102.0 10.5 %collective-permute-start.31 = (bf16[4,4,16,1024]{3,2,1,0:T(8,128)(2,1)S(1)}, bf16[4,4,16,1024]{3,2,1,0:T(8,128)(2,1)S(1)}, u32[]{:S(2)}, u32[]{:S(2)}) collective-permute-start(bf16[4,4,16,1024]{3,2,1,0:T(8,128)(2,1)S(1)} %get-tuple-element.81), channel_id=1, source_target_pairs={{0,4},{4,0},{1,5},{5,1},{2,6},{6,2},{3,7},{7,3},{8,12},{12,8},{9,1... | collective-permute-start | bytes 1572872 | tf_op jit(solution)/shard_map/ppermute | solution.py:56
  104.2 10.9 %collective-permute-start.26 = (bf16[4,4,16,1024]{3,2,1,0:T(8,128)(2,1)S(1)}, bf16[4,4,16,1024]{3,2,1,0:T(8,128)(2,1)S(1)}, u32[]{:S(2)}, u32[]{:S(2)}) collective-permute-start(bf16[4,4,16,1024]{3,2,1,0:T(8,128)(2,1)S(1)} %down.7), channel_id=1, source_target_pairs={{0,16},{4,68},{8,24},{12,76},{16,0},{20,84},{24,8},{28,92},{32,48}... | collective-permute-start | bytes 1572872 | tf_op jit(solution)/shard_map/ppermute | solution.py:52
  109.2 11.3 %collective-permute-start.30 = (bf16[4,4,16,1024]{3,2,1,0:T(8,128)(2,1)S(1)}, bf16[4,4,16,1024]{3,2,1,0:T(8,128)(2,1)S(1)}, u32[]{:S(2)}, u32[]{:S(2)}) collective-permute-start(bf16[4,4,16,1024]{3,2,1,0:T(8,128)(2,1)S(1)} %get-tuple-element.80), channel_id=1, source_target_pairs={{0,8},{4,36},{8,16},{12,44},{16,24},{20,52},{24,0},{28,60},{32,40}... | collective-permute-start | bytes 1572872 | tf_op jit(solution)/shard_map/ppermute | solution.py:52
  110.2 10.8 %collective-permute-start.29 = (bf16[4,4,16,1024]{3,2,1,0:T(8,128)(2,1)S(1)}, bf16[4,4,16,1024]{3,2,1,0:T(8,128)(2,1)S(1)}, u32[]{:S(2)}, u32[]{:S(2)}) collective-permute-start(bf16[4,4,16,1024]{3,2,1,0:T(8,128)(2,1)S(1)} %get-tuple-element.79), channel_id=1, source_target_pairs={{0,24},{4,100},{8,0},{12,108},{16,8},{20,116},{24,16},{28,124},{32... | collective-permute-start | bytes 1572872 | tf_op jit(solution)/shard_map/ppermute | solution.py:52
  121.4 6.9 %collective-permute-start.32 = (bf16[4,16,1024]{2,1,0:T(8,128)(2,1)S(1)}, bf16[4,16,1024]{2,1,0:T(8,128)(2,1)S(1)}, u32[]{:S(2)}, u32[]{:S(2)}) collective-permute-start(bf16[4,16,1024]{2,1,0:T(8,128)(2,1)S(1)} %get-tuple-element.83), channel_id=1, source_target_pairs={{0,64},{4,20},{8,72},{12,28},{16,80},{20,4},{24,88},{28,12},{32,96... | collective-permute-start | bytes 393224 | tf_op jit(solution)/shard_map/ppermute | solution.py:52
  125.1 6.2 %collective-permute-start.34 = (bf16[4,16,1024]{2,1,0:T(8,128)(2,1)S(1)}, bf16[4,16,1024]{2,1,0:T(8,128)(2,1)S(1)}, u32[]{:S(2)}, u32[]{:S(2)}) collective-permute-start(bf16[4,16,1024]{2,1,0:T(8,128)(2,1)S(1)} %get-tuple-element.84), channel_id=1, source_target_pairs={{0,32},{4,12},{8,40},{12,20},{16,48},{20,28},{24,56},{28,4},{32,64... | collective-permute-start | bytes 393224 | tf_op jit(solution)/shard_map/ppermute | solution.py:52
  126.1 5.2 %collective-permute-start.33 = (bf16[4,16,1024]{2,1,0:T(8,128)(2,1)S(1)}, bf16[4,16,1024]{2,1,0:T(8,128)(2,1)S(1)}, u32[]{:S(2)}, u32[]{:S(2)}) collective-permute-start(bf16[4,16,1024]{2,1,0:T(8,128)(2,1)S(1)} %get-tuple-element.85), channel_id=1, source_target_pairs={{0,96},{4,28},{8,104},{12,4},{16,112},{20,12},{24,120},{28,20},{32... | collective-permute-start | bytes 393224 | tf_op jit(solution)/shard_map/ppermute | solution.py:52
